TPU v7x, 32 devices: a whole 2x2x4 slice. The times are simulated.
32 devices in a mesh: grp: 2 (over y), trade: 4 (over z), date: 2 (over x), path: 2 (over core).
Axes of the slice: x: 2, y: 2, z: 4, core: 2. Of those that a mesh axis runs over, the one named last changes fastest.
Arguments:
- driver_increments: float32 [16, 256, 128], P(('grp', 'date'), 'path'), parts along dimension 0, may hold values from -4 to 4
- persistence_ratio: float32 [16, 128], P(('grp', 'date')), parts along dimension 0, may hold values from 0 to 1, as said below
- deal_sensitivity: bfloat16 [128, 65536], P(None, ('grp', 'trade')), parts along dimension 1, may hold values from -0.5 to 0.5
- signed_notional: float32 [65536], P(('grp', 'trade')), parts along dimension 0, may hold values from -0.4 to 0.4
- batch_obligor: int32 [512], P(('grp', 'trade')), parts along dimension 0, may hold values from 0 to 127, as said below
- collateral_ceiling: float32 [256], P(('grp', 'trade')), parts along dimension 0, may hold values from -1 to 1
- default_discount_mass: float32 [16, 128], P(('grp', 'date'), 'trade'), parts along dimension 0, may hold values from 0.1 to 1
Outputs:
- exposure_profile: float32 [16, 128], P(('grp', 'date'), 'trade'), parts along dimension 0
- shock_gradient: float32 [16, 256, 128], P(('grp', 'date'), 'path'), parts along dimension 0
There are 2 independent parts, one for each index of `grp`. A program takes and returns all parts, laid end to end along the dimension named above; each array names one. Nothing has to cross between parts.
Inputs may be any that keep to these rules, and one draw needn't show every extreme that they name: `persistence_ratio`: strictly between 0 and 1. `batch_obligor`: counterparty c belongs to trade shard c // 32. Of the 64 trade blocks of one trade shard, at most 32 have counterparties on any one trade shard, and in every trade shard some counterparty shard receives exactly 32 of them.
All inputs are finite; a program needn't handle non-finite values.
Results may differ from a plain program's by a relative error of at most 0.0019.
Values sent between devices are 32-bit elements; how exact they have to be, the bound alone decides.
No kernel may reach another device: no remote copies, remote signals or barrier semaphores. Data moves between devices by JAX's collectives and lax.ppermute only.
A program may use at most 64 MiB of HBM per device.

v0:
```python
import jax
import jax.numpy as jnp
from jax import lax
from jax.sharding import PartitionSpec as P

block_width = 128
cluster_extent = 512
highest = lax.Precision.HIGHEST


def entering(value, axis, combine, identity, reverse):
    length, index = (lax.axis_size(axis), lax.axis_index(axis))
    everything = jax.tree.map(lambda part: lax.all_gather(part, axis), value)
    start = jax.tree.map(
        lambda part, zero: jnp.broadcast_to(jnp.asarray(zero, part.dtype), part.shape),
        value,
        identity,
    )

    def hop(k, before):
        at = length - 1 - k if reverse else k
        reached = at > index if reverse else at < index
        new = combine(before, jax.tree.map(lambda part: part[at], everything))
        return jax.tree.map(lambda a, b: jnp.where(reached, a, b), new, before)

    return lax.fori_loop(0, length, hop, start)


def compose(earlier, later):
    return (later[0] * earlier[0], later[0] * earlier[1] + later[1])


def reverse_chain(direct, persistence_ratio):
    date_count = direct.shape[0]
    factor_gain = jnp.ones((direct.shape[2],), jnp.float32)
    message = jnp.zeros(direct.shape[1:], jnp.float32)
    for date_step in reversed(range(date_count)):
        message = persistence_ratio[date_step][None, :] * (direct[date_step] + message)
        factor_gain = persistence_ratio[date_step] * factor_gain
    identity = (jnp.ones_like(factor_gain), jnp.zeros_like(message))
    _, arriving = entering((factor_gain, message), "date", compose, identity, True)
    adjoints = []
    message = arriving
    for date_step in reversed(range(date_count)):
        adjoint = direct[date_step] + message
        adjoints.append(adjoint)
        message = persistence_ratio[date_step][None, :] * adjoint
    return jnp.stack(adjoints[::-1])


def shards(
    driver_increments,
    persistence_ratio,
    deal_sensitivity,
    signed_notional,
    batch_obligor,
    collateral_ceiling,
    default_discount_mass,
):
    date_count, path_count, factor_count = driver_increments.shape
    factor_gain = jnp.ones((factor_count,), jnp.float32)
    carried = jnp.zeros((path_count, factor_count), jnp.float32)
    for date_step in range(date_count):
        carried = persistence_ratio[date_step][None, :] * carried + driver_increments[date_step]
        factor_gain = persistence_ratio[date_step] * factor_gain
    identity = (jnp.ones_like(factor_gain), jnp.zeros_like(carried))
    _, arriving = entering((factor_gain, carried), "date", compose, identity, False)
    states = []
    carried = arriving
    for date_step in range(date_count):
        carried = persistence_ratio[date_step][None, :] * carried + driver_increments[date_step]
        states.append(carried)
    row_count = date_count * path_count
    state_bf = jnp.stack(states).reshape(row_count, factor_count).astype(jnp.bfloat16)
    deal_ordinal = deal_sensitivity.shape[1]
    block_count = deal_ordinal // block_width
    cluster_ordinal = deal_ordinal // cluster_extent
    per_group = cluster_extent // block_width

    def value_group(group_index, block_sums):
        opening_offset = group_index * cluster_extent
        sensitivity_portion = lax.dynamic_slice_in_dim(
            deal_sensitivity, opening_offset, cluster_extent, 1
        )
        size_part = lax.dynamic_slice_in_dim(signed_notional, opening_offset, cluster_extent, 0)
        linear = jnp.dot(state_bf, sensitivity_portion, preferred_element_type=jnp.float32)
        trade_value = jax.nn.softplus(linear) * size_part[None, :]
        summed = trade_value.reshape(row_count, per_group, block_width).sum(axis=2)
        return lax.dynamic_update_slice_in_dim(block_sums, summed.T, group_index * per_group, 0)

    block_sums = lax.fori_loop(
        0, cluster_ordinal, value_group, jnp.zeros((block_count, row_count), jnp.float32)
    )
    cpty_dev = collateral_ceiling.shape[0]
    shard_count = lax.axis_size("trade")
    ownership = (
        batch_obligor[:, None] == jnp.arange(cpty_dev * shard_count, dtype=jnp.int32)[None, :]
    ).astype(jnp.float32)
    partial_value = lax.dot_general(
        ownership, block_sums, (((0,), (0,)), ((), ())), precision=highest
    )
    netted = lax.psum_scatter(partial_value, "trade", scatter_dimension=0, tiled=True)
    shifted = netted - collateral_ceiling[:, None]
    exposure = jax.nn.softplus(shifted).reshape(cpty_dev, date_count, path_count)
    path_total = lax.psum(jnp.sum(exposure, axis=2).T, "path")
    exposure_profile = path_total / (path_count * lax.axis_size("path"))
    net_adjoint = (
        default_discount_mass.T[:, :, None]
        * jax.nn.sigmoid(shifted).reshape(cpty_dev, date_count, path_count)
    ).reshape(cpty_dev, row_count)
    gathered = lax.all_gather(net_adjoint, "trade", axis=0, tiled=True)
    block_adjoint = jnp.dot(ownership, gathered, precision=highest)

    def pull_group(group_index, running):
        opening_offset = group_index * cluster_extent
        sensitivity_portion = lax.dynamic_slice_in_dim(
            deal_sensitivity, opening_offset, cluster_extent, 1
        )
        size_part = lax.dynamic_slice_in_dim(signed_notional, opening_offset, cluster_extent, 0)
        linear = jnp.dot(state_bf, sensitivity_portion, preferred_element_type=jnp.float32)
        slope_term = jax.nn.sigmoid(linear) * size_part[None, :]
        upstream = lax.dynamic_slice_in_dim(block_adjoint, group_index * per_group, per_group, 0)
        value_adjoint = (
            (upstream.T[:, :, None] * slope_term.reshape(row_count, per_group, block_width))
            .reshape(row_count, cluster_extent)
            .astype(jnp.bfloat16)
        )
        product = lax.dot_general(
            value_adjoint,
            sensitivity_portion,
            (((1,), (1,)), ((), ())),
            preferred_element_type=jnp.float32,
        )
        return running + product

    direct = lax.fori_loop(
        0, cluster_ordinal, pull_group, jnp.zeros((row_count, factor_count), jnp.float32)
    )
    direct = direct.reshape(date_count, path_count, factor_count)
    summed = lax.psum(direct, "trade")
    shock_gradient = reverse_chain(summed, persistence_ratio)
    return (exposure_profile, shock_gradient)


def solution(mesh):
    return jax.shard_map(
        shards,
        mesh=mesh,
        in_specs=(
            P(("grp", "date"), "path", None),
            P(("grp", "date"), None),
            P(None, ("grp", "trade")),
            P(("grp", "trade")),
            P(("grp", "trade")),
            P(("grp", "trade")),
            P(("grp", "date"), "trade"),
        ),
        out_specs=(P(("grp", "date"), "trade"), P(("grp", "date"), "path", None)),
        check_vma=False,
    )
```

profile of v0, /device:TPU:0, one launch (start us, length us, event | category | flops | bytes accessed | tf_op | source)
XLA Modules:
  0.0 200.2 jit_solution(7079904627721618631)
XLA Ops:
  8.8 5.1 %all-gather = f32[2,1,128]{2,1,0:T(1,128)S(1)} all-gather(f32[1,1,128]{2,1,0:T(1,128)S(1)} %get-tuple-element.550), channel_id=1, replica_groups=mesh['grp'=2,'trade'=4,'date'=2,'path'=2] {'date'}, dimensions={0}, use_global_device_ids=true | all-gather | bytes 1536 | tf_op jit(solution)/shard_map/all_gather | solution.py:13
  14.8 4.9 %all_gather.20 = f32[2,128,128]{2,1,0:T(8,128)S(1)} all-gather(f32[1,128,128]{2,1,0:T(8,128)S(1)} %multiply_add_fusion), channel_id=1, replica_groups=mesh['grp'=2,'trade'=4,'date'=2,'path'=2] {'date'}, dimensions={0}, use_global_device_ids=true | all-gather | bytes 196608 | tf_op jit(solution)/shard_map/all_gather | solution.py:13
  20.9 41.0 %while.57 = (s32[]{:T(128)}, f32[64,512]{1,0:T(8,128)S(1)}, bf16[128,8192]{1,0:T(8,128)(2,1)}, bf16[512,128]{1,0:T(8,128)(2,1)S(1)}, f32[8192]{0:T(1024)}, /*ind...) while((s32[]{:T(128)}, f32[64,512]{1,0:T(8,128)S(1)}, ...), condition=%wide.region_4.5_spmd, body=%wide.region_2.4_spmd.sunk | while | flops 69203976 | bytes 293085 | solution.py:91
  21.7 1.8 bitcast_reduce_fusion.2
  24.2 1.8 bitcast_reduce_fusion.2
  26.8 1.8 bitcast_reduce_fusion.2
  29.4 1.8 bitcast_reduce_fusion.2
  31.9 1.8 bitcast_reduce_fusion.2
  34.5 1.8 bitcast_reduce_fusion.2
  37.0 1.8 bitcast_reduce_fusion.2
  39.6 1.7 bitcast_reduce_fusion.2
  42.2 1.8 bitcast_reduce_fusion.2
  44.7 1.8 bitcast_reduce_fusion.2
  47.3 1.8 bitcast_reduce_fusion.2
  49.8 1.7 bitcast_reduce_fusion.2
  52.4 1.8 bitcast_reduce_fusion.2
  55.0 1.8 bitcast_reduce_fusion.2
  57.5 1.8 bitcast_reduce_fusion.2
  60.1 1.8 bitcast_reduce_fusion.2
  63.1 21.4 %reduce-scatter.2.cloned.1.call-done = f32[32,512]{1,0:T(8,128)} async-done(((f32[128,512]{1,0:T(8,128)}), f32[32,512]{1,0:T(8,128)}) %reduce-scatter.2.cloned.1.call-update) | async-done | bytes 65552 | tf_op jit(solution)/shard_map/reduce_scatter | solution.py:102
  85.6 13.8 %all_gather.21 = f32[128,512]{1,0:T(8,128)S(1)} all-gather(f32[32,512]{1,0:T(8,128)S(1)} %get-tuple-element.544), channel_id=1, replica_groups=mesh['grp'=2,'trade'=4,'date'=2,'path'=2] {'trade'}, dimensions={0}, use_global_device_ids=true | all-gather | bytes 327680 | tf_op jit(solution)/shard_map/all_gather | solution.py:111
  99.7 50.3 %while.59 = (s32[]{:T(128)}, f32[512,128]{1,0:T(8,128)S(1)}, f32[64,512]{1,0:T(8,128)S(1)}, bf16[128,8192]{1,0:T(8,128)(2,1)}, bf16[512,128]{1,0:T(8,128)(2,1)S(...) while((s32[]{:T(128)}, f32[512,128]{1,0:T(8,128)S(1)}, ...), condition=%wide.region_9.10_spmd.clone, body=%wide.region_8.9_spmd.clone.sunk | while | flops 135921680 | bytes 3063530 | solution.py:136
  101.3 1.6 fusion.50
  104.4 1.6 fusion.50
  110.7 1.6 fusion.50
  113.8 1.6 fusion.50
  132.7 1.6 fusion.50
  145.3 1.6 fusion.50
  150.8 4.2 %all-gather.1 = f32[2,1,128]{2,1,0:T(1,128)S(1)} all-gather(f32[1,1,128]{2,1,0:T(1,128)S(1)} %get-tuple-element.546), channel_id=1, replica_groups=mesh['grp'=2,'trade'=4,'date'=2,'path'=2] {'date'}, dimensions={0}, use_global_device_ids=true | all-gather | bytes 1536 | tf_op jit(solution)/shard_map/all_gather | solution.py:13
  155.1 3.4 %psum.14 = f32[4,32]{0,1:T(8,128)S(1)} all-reduce(f32[4,32]{0,1:T(8,128)S(1)} %bitcast.153), channel_id=1, replica_groups=mesh['grp'=2,'trade'=4,'date'=2,'path'=2] {'path'}, use_global_device_ids=true, to_apply=%region_7.8 | all-reduce | flops 128 | bytes 1024 | tf_op jit(solution)/shard_map/psum | solution.py:105
  159.1 25.7 %all-reduce.2.cloned.1.call-done = f32[4,128,128]{2,1,0:T(8,128)} async-done(((f32[4,128,128]{2,1,0:T(8,128)}), f32[4,128,128]{2,1,0:T(8,128)}) %all-reduce.2.cloned.1.call-update) | async-done | bytes 262160 | tf_op jit(solution)/shard_map/psum | solution.py:140
  185.8 4.9 %all_gather.23 = f32[2,128,128]{2,1,0:T(8,128)S(1)} all-gather(f32[1,128,128]{2,1,0:T(8,128)S(1)} %add_multiply_fusion), channel_id=1, replica_groups=mesh['grp'=2,'trade'=4,'date'=2,'path'=2] {'date'}, dimensions={0}, use_global_device_ids=true | all-gather | bytes 196608 | tf_op jit(solution)/shard_map/all_gather | solution.py:13
  (153 shorter events, 63.8 us)
Async XLA Ops:
  7.2 13.6 %copy-start = (f32[4,128,128]{2,1,0:T(8,128)S(1)}, f32[4,128,128]{2,1,0:T(8,128)}, u32[]{:S(2)}) copy-start(f32[4,128,128]{2,1,0:T(8,128)} %param.15) | copy-start | bytes 786436
  7.2 77.3 %reduce-scatter.2.cloned.1.call-start = ((), (), s32[]{:S(2)}) async-start(), calls=%async_computation.1 | async-start | bytes 327680 | tf_op jit(solution)/shard_map/reduce_scatter | solution.py:102
  20.8 41.0 %copy-start.2 = (s32[64]{0:T(128)S(1)}, s32[64]{0:T(128)}, u32[]{:S(2)}) copy-start(s32[64]{0:T(128)} %param.19) | copy-start | bytes 772
  20.9 42.2 %copy-start.3 = (f32[4,32]{1,0:T(4,128)S(1)}, f32[4,32]{1,0:T(4,128)}, u32[]{:S(2)}) copy-start(f32[4,32]{1,0:T(4,128)} %param.21) | copy-start | bytes 1540
  20.9 63.7 %copy-start.4 = (f32[32]{0:T(128)S(1)}, f32[32]{0:T(128)}, u32[]{:S(2)}) copy-start(f32[32]{0:T(128)} %param.20) | copy-start | bytes 388
  63.0 121.9 %all-reduce.2.cloned.1.call-start = ((), (), s32[]{:S(2)}) async-start(), calls=%async_computation.2 | async-start | bytes 524288 | tf_op jit(solution)/shard_map/psum | solution.py:140
  150.0 0.7 copy-start.1
Sparse Core Ops, SparseCore 0:
  63.1 21.3 reduce-scatter.1
  150.9 33.9 all-reduce.1
where the time goes:
time: 202 us; the launch traced here: 200 us
  matrix products  54.4 us (27%)
  waiting for transfers between devices  47.1 us (23%)
  local copies, waits for them, and re-layouts  38.5 us (19%)
  blocking collectives  36.4 us (18%)
  between operations  14.2 us (7%)
  other arithmetic  8.08 us (4%)
    dot_general x16, matrix products, value_group(): jnp.dot(state_bf, sensitivity_portion, preferred_element_type=jnp.float32)  28 us
    psum x1, waiting for transfers between devices, shards(): summed = lax.psum(direct, 'trade')  25.7 us
    dot_general x16, matrix products, pull_group(): lax.dot_general(value_adjoint, sensitivity_portion, (((1,), (1,)), ((), (...  25.1 us
    reduce_scatter x1, waiting for transfers between devices, shards(): lax.psum_scatter(partial_value, 'trade', scatter_dimension=0, tiled=True)  21.4 us
    all_gather x4, blocking collectives, entering(): everything = jax.tree.map(lambda part: lax.all_gather(part, axis), value)  19.2 us
    all_gather x1, blocking collectives, shards(): gathered = lax.all_gather(net_adjoint, 'trade', axis=0, tiled=True)  13.8 us
    dynamic_slice x16, local copies, waits for them, and re-layouts, pull_group(): lax.dynamic_slice_in_dim(signed_notional, opening_offset, cluster_extent, 0)  12.2 us
    dynamic_slice x16, local copies, waits for them, and re-layouts, value_group(): lax.dynamic_slice_in_dim(signed_notional, opening_offset, cluster_extent, 0)  12.2 us
  transfers between devices with their start and end apart: 2, of which 2 were waited for; matrix products, arithmetic and copies ran while one was open for 0% of the time, Pallas kernels for 0%

commit v1 on v0

v1 whole, which is shorter than its diff:
```python
import functools

import jax
import jax.numpy as jnp
from jax import lax
from jax.experimental import pallas as pl
from jax.experimental.pallas import tpu as pltpu
from jax.sharding import PartitionSpec as P

block_width = 128
highest = lax.Precision.HIGHEST
f32 = jnp.float32
bf16 = jnp.bfloat16


def swap(value, axes, sizes, flips):
    count = 1
    for size in sizes:
        count *= size
    pairs = []
    for flat in range(count):
        rest, target, scale = flat, 0, 1
        for size, flip in zip(reversed(sizes), reversed(flips)):
            target += ((rest % size) ^ flip) * scale
            rest //= size
            scale *= size
        pairs.append((flat, target))
    return lax.ppermute(value, axes, pairs)


def entering(value, axis, combine, identity, reverse):
    length, index = (lax.axis_size(axis), lax.axis_index(axis))
    everything = jax.tree.map(lambda part: lax.all_gather(part, axis), value)
    before = jax.tree.map(
        lambda part, zero: jnp.broadcast_to(jnp.asarray(zero, part.dtype), part.shape),
        value,
        identity,
    )
    for k in range(length):
        at = length - 1 - k if reverse else k
        reached = at > index if reverse else at < index
        new = combine(before, jax.tree.map(lambda part: part[at], everything))
        before = jax.tree.map(lambda a, b: jnp.where(reached, a, b), new, before)
    return before


def compose(earlier, later):
    return (later[0] * earlier[0], later[0] * earlier[1] + later[1])


def softplus(v):
    return jnp.maximum(v, jnp.log(1.0 + jnp.exp(jnp.minimum(v, 80.0))))


def value_kernel(blocks, x_ref, rho_ref, arriving_ref, first_ref, d_ref, n_ref, sums_ref, state_ref):
    dates, paths, _ = x_ref.shape

    @pl.when(pl.program_id(0) == 0)
    def _():
        carried = arriving_ref[...] * first_ref[0:1, :]
        for t in range(dates):
            carried = rho_ref[t : t + 1, :] * carried + x_ref[t]
            state_ref[:, t * paths : (t + 1) * paths] = carried.T.astype(bf16)

    size_t = n_ref[...].T
    linear = jnp.dot(d_ref[...].T, state_ref[...], preferred_element_type=f32)
    for b in range(blocks):
        value = softplus(linear[b * block_width : (b + 1) * block_width]) * size_t[:, b : b + 1]
        sums_ref[b : b + 1, :] = jnp.sum(value, axis=0, keepdims=True)


def value_pass(x, rho, arriving, keep, d, n):
    dates, paths, factors = x.shape
    rows, trades = dates * paths, d.shape[1]
    step = min(2048, trades)
    blocks = step // block_width
    whole = lambda *shape: pl.BlockSpec(shape, lambda i: (0,) * len(shape))
    return pl.pallas_call(
        functools.partial(value_kernel, blocks),
        grid=(trades // step,),
        in_specs=[
            whole(dates, paths, factors),
            whole(dates, factors),
            whole(paths, factors),
            whole(8, factors),
            pl.BlockSpec((factors, step), lambda i: (0, i)),
            pl.BlockSpec((blocks, block_width), lambda i: (i, 0)),
        ],
        out_specs=[pl.BlockSpec((blocks, rows), lambda i: (i, 0)), whole(factors, rows)],
        out_shape=[
            jax.ShapeDtypeStruct((trades // block_width, rows), f32),
            jax.ShapeDtypeStruct((factors, rows), bf16),
        ],
        compiler_params=pltpu.CompilerParams(vmem_limit_bytes=50 << 20),
        cost_estimate=pl.CostEstimate(
            flops=2 * rows * trades * factors, bytes_accessed=2 * trades * factors, transcendentals=2 * rows * trades
        ),
        name="value_pass",
    )(x, rho, arriving, keep, d, n)


def split_dot(selector, value):
    selector = selector.astype(bf16)
    high = value.astype(bf16)
    rest = value - high.astype(f32)
    middle = rest.astype(bf16)
    low = (rest - middle.astype(f32)).astype(bf16)
    dot = functools.partial(jnp.dot, selector, preferred_element_type=f32)
    return dot(low) + dot(middle) + dot(high)


def net_stage(shards, cpty_dev, dates, me, sums, small, upstream_ref, exposure_ref):
    blocks, rows = sums[0].shape
    paths = rows // dates
    cpties = shards * cpty_dev
    shift = cpty_dev.bit_length() - 1
    netted = None
    own = None
    columns = []
    for k in range(shards):
        tall = small[k][...].T
        columns.append(tall)

        def label(owner):
            owner = owner.astype(jnp.int32)
            return (((owner >> shift) ^ me) << shift) + (owner & (cpty_dev - 1))

        row = label(small[k][dates + 1 : dates + 2, :blocks])
        pick = lax.broadcasted_iota(jnp.int32, (cpties, blocks), 0) == row
        part = split_dot(jnp.where(pick, 1.0, 0.0), sums[k][...])
        netted = part if netted is None else netted + part
        if k == 0:
            column = label(tall[:blocks, dates + 1 : dates + 2])
            own = jnp.where(lax.broadcasted_iota(jnp.int32, (blocks, cpties), 1) == column, 1.0, 0.0)
    adjoint = []
    for k in range(shards):
        shifted = netted[k * cpty_dev : (k + 1) * cpty_dev] - columns[k][:cpty_dev, dates : dates + 1]
        slope = 0.5 * jnp.tanh(0.5 * shifted) + 0.5
        adjoint.append(
            jnp.concatenate(
                [
                    slope[:, t * paths : (t + 1) * paths] * columns[k][:cpty_dev, t : t + 1]
                    for t in range(dates)
                ],
                axis=1,
            )
        )
        if k == 0:
            exposed = softplus(shifted)
            lane = lax.broadcasted_iota(jnp.int32, (cpty_dev, 128), 1)
            table = jnp.zeros((cpty_dev, 128), f32)
            for t in range(dates):
                total = jnp.sum(exposed[:, t * paths : (t + 1) * paths], axis=1, keepdims=True)
                table = jnp.where(lane == t, total, table)
            exposure_ref[...] = table.T[:dates]
    upstream_ref[...] = split_dot(own, jnp.concatenate(adjoint, axis=0))


def pull_step(blocks, upstream, half_ref, d_ref, n_ref, total_ref):
    size_t = 0.5 * n_ref[...].T
    linear = jnp.dot(d_ref[...].T, half_ref[...], preferred_element_type=f32)
    parts = []
    for b in range(blocks):
        slope = jnp.tanh(linear[b * block_width : (b + 1) * block_width])
        size = size_t[:, b : b + 1]
        parts.append(((slope * size + size) * upstream[b : b + 1, :]).astype(bf16))
    total_ref[...] += jnp.dot(d_ref[...], jnp.concatenate(parts, axis=0), preferred_element_type=f32)


def pull_net_kernel(shards, cpty_dev, dates, blocks, me_ref, state_ref, rho_ref, d_ref, n_ref, *refs):
    sums, refs = refs[:shards], refs[shards:]
    small, refs = refs[:shards], refs[shards:]
    exposure_ref, refs = refs[0], refs[1:]
    chain, refs = refs[:shards], refs[shards:]
    message, refs = refs[:shards], refs[shards:]
    upstream_ref, half_ref, total_ref, chained_ref, message_ref = refs
    rows = state_ref.shape[1]
    paths = rows // dates
    i = pl.program_id(0)
    me = me_ref[0]

    @pl.when(i == 0)
    def _():
        half_ref[...] = state_ref[...] * 0.5
        total_ref[...] = jnp.zeros_like(total_ref)
        net_stage(shards, cpty_dev, dates, me, sums, small, upstream_ref, exposure_ref)

    upstream = upstream_ref[pl.ds(pl.multiple_of(i * blocks, blocks), blocks), :]
    pull_step(blocks, upstream, half_ref, d_ref, n_ref, total_ref)

    @pl.when(i == pl.num_programs(0) - 1)
    def _():
        carried = jnp.zeros((paths, rho_ref.shape[1]), f32)
        for t in reversed(range(dates)):
            adjoint = total_ref[:, t * paths : (t + 1) * paths].T + carried
            chained_ref[t] = adjoint
            carried = rho_ref[t : t + 1, :] * adjoint
        message_ref[...] = carried
        piece = paths // shards
        for k in range(shards):
            at = pl.ds(pl.multiple_of((me ^ k) * piece, piece), piece)
            chain[k][...] = chained_ref[:, at, :]
            message[k][...] = message_ref[at, :]


def pull_net_pass(shards, dates, cpty_dev, me, state, rho, d, n, sums, small):
    factors, rows = state.shape
    trades = d.shape[1]
    paths = rows // dates
    piece = paths // shards
    step = min(2048, trades)
    blocks = step // block_width
    whole = lambda *shape: pl.BlockSpec(shape, lambda i, s: (0,) * len(shape))
    out = pl.pallas_call(
        functools.partial(pull_net_kernel, shards, cpty_dev, dates, blocks),
        grid_spec=pltpu.PrefetchScalarGridSpec(
            num_scalar_prefetch=1,
            grid=(trades // step,),
            in_specs=[
                whole(factors, rows),
                whole(dates, factors),
                pl.BlockSpec((factors, step), lambda i, s: (0, i)),
                pl.BlockSpec((blocks, block_width), lambda i, s: (i, 0)),
            ]
            + [whole(*part.shape) for part in sums]
            + [whole(*part.shape) for part in small],
            out_specs=[whole(dates, cpty_dev)]
            + [whole(dates, piece, factors)] * shards
            + [whole(piece, factors)] * shards,
            scratch_shapes=[
                pltpu.VMEM(sums[0].shape, f32),
                pltpu.VMEM((factors, rows), bf16),
                pltpu.VMEM((factors, rows), f32),
                pltpu.VMEM((dates, paths, factors), f32),
                pltpu.VMEM((paths, factors), f32),
            ],
        ),
        out_shape=[jax.ShapeDtypeStruct((dates, cpty_dev), f32)]
        + [jax.ShapeDtypeStruct((dates, piece, factors), f32)] * shards
        + [jax.ShapeDtypeStruct((piece, factors), f32)] * shards,
        compiler_params=pltpu.CompilerParams(vmem_limit_bytes=50 << 20),
        cost_estimate=pl.CostEstimate(
            flops=4 * rows * trades * factors, bytes_accessed=2 * trades * factors, transcendentals=rows * trades
        ),
        name="pull_net_pass",
    )(me, state, rho, d, n, *sums, *small)
    return out[0], out[1 : 1 + shards], out[1 + shards :]


def pull_kernel(blocks, state_ref, d_ref, n_ref, upstream_ref, direct_ref, half_ref, total_ref):
    dates, paths, _ = direct_ref.shape

    @pl.when(pl.program_id(0) == 0)
    def _():
        half_ref[...] = state_ref[...] * 0.5
        total_ref[...] = jnp.zeros_like(total_ref)

    pull_step(blocks, upstream_ref[...], half_ref, d_ref, n_ref, total_ref)

    @pl.when(pl.program_id(0) == pl.num_programs(0) - 1)
    def _():
        for t in range(dates):
            direct_ref[t] = total_ref[:, t * paths : (t + 1) * paths].T


def pull_pass(dates, state, d, n, upstream):
    factors, rows = state.shape
    trades = d.shape[1]
    paths = rows // dates
    step = min(2048, trades)
    blocks = step // block_width
    whole = lambda *shape: pl.BlockSpec(shape, lambda i: (0,) * len(shape))
    return pl.pallas_call(
        functools.partial(pull_kernel, blocks),
        grid=(trades // step,),
        in_specs=[
            whole(factors, rows),
            pl.BlockSpec((factors, step), lambda i: (0, i)),
            pl.BlockSpec((blocks, block_width), lambda i: (i, 0)),
            pl.BlockSpec((blocks, rows), lambda i: (i, 0)),
        ],
        out_specs=whole(dates, paths, factors),
        out_shape=jax.ShapeDtypeStruct((dates, paths, factors), f32),
        scratch_shapes=[pltpu.VMEM((factors, rows), bf16), pltpu.VMEM((factors, rows), f32)],
        compiler_params=pltpu.CompilerParams(vmem_limit_bytes=50 << 20),
        name="pull_pass",
    )(state, d, n, upstream)


def place_kernel(shards, me_ref, *refs):
    pieces, out_ref = refs[:shards], refs[shards]
    size = pieces[0].shape[1]
    for k in range(shards):
        at = pl.ds(pl.multiple_of((me_ref[0] ^ k) * size, size), size)
        out_ref[:, at, :] = pieces[k][...]


def place(me, pieces):
    shards = len(pieces)
    dates, size, factors = pieces[0].shape
    whole = lambda *shape: pl.BlockSpec(shape, lambda i, s: (0,) * len(shape))
    return pl.pallas_call(
        functools.partial(place_kernel, shards),
        grid_spec=pltpu.PrefetchScalarGridSpec(
            num_scalar_prefetch=1,
            grid=(1,),
            in_specs=[whole(dates, size, factors)] * shards,
            out_specs=whole(dates, shards * size, factors),
        ),
        out_shape=jax.ShapeDtypeStruct((dates, shards * size, factors), f32),
        name="place",
    )(me, *pieces)


def local_chain(x, rho):
    carried = x[0]
    gain = rho[0]
    for t in range(1, x.shape[0]):
        carried = rho[t][None, :] * carried + x[t]
        gain = rho[t] * gain
    return gain, carried


def near(x, rho, d, size, obligor, ceiling, mass):
    dates, paths, factors = x.shape
    shards = lax.axis_size("trade")
    cpty_dev = ceiling.shape[0]
    n = size.reshape(-1, block_width)
    blocks = n.shape[0]
    me = lax.axis_index("trade").astype(jnp.int32)[None]
    later = lax.axis_index("date") > 0
    _, carried = local_chain(x, rho)
    arriving = swap(carried, ("date",), (2,), (1,))
    keep = jnp.broadcast_to(jnp.where(later, 1.0, 0.0).astype(f32), (8, factors))

    wide = lambda part: jnp.pad(part, ((0, 0), (0, 128 - part.shape[1])))
    facts = jnp.concatenate([wide(mass), wide(ceiling[None, :]), wide(obligor.astype(f32)[None, :])], axis=0)
    facts = jnp.pad(facts, ((0, 8 - facts.shape[0]), (0, 0)))
    small = [facts] + [swap(facts, ("trade",), (shards,), (k,)) for k in range(1, shards)]

    sums, state = value_pass(x, rho, arriving, keep, d, n)
    sums = [sums] + [swap(sums, ("trade",), (shards,), (k,)) for k in range(1, shards)]
    exposure, chain, message = pull_net_pass(shards, dates, cpty_dev, me, state, rho, d, n, sums, small)
    total_paths = paths * lax.axis_size("path")
    exposure_profile = (exposure + swap(exposure, ("path",), (2,), (1,))) / total_paths

    chain = [chain[0]] + [swap(chain[k], ("trade",), (shards,), (k,)) for k in range(1, shards)]
    message = [swap(message[k], ("trade", "date"), (shards, 2), (k, 1)) for k in range(shards)]
    total = functools.reduce(jnp.add, chain)
    reached = jnp.where(later, 0.0, functools.reduce(jnp.add, message))
    rows = []
    for t in reversed(range(dates)):
        rows.append(total[t] + reached)
        reached = rho[t][None, :] * reached
    own = jnp.stack(rows[::-1])
    pieces = [own] + [swap(own, ("trade",), (shards,), (k,)) for k in range(1, shards)]
    return exposure_profile, place(me, pieces)


def far(x, rho, d, size, obligor, ceiling, mass):
    dates, paths, factors = x.shape
    rows = dates * paths
    cpty_dev = ceiling.shape[0]
    n = size.reshape(-1, block_width)
    value = local_chain(x, rho)
    identity = (jnp.ones_like(value[0]), jnp.zeros_like(value[1]))
    _, arriving = entering(value, "date", compose, identity, False)
    sums, state = value_pass(x, rho, arriving, jnp.ones((8, factors), f32), d, n)
    cpties = cpty_dev * lax.axis_size("trade")
    ownership = (obligor[:, None] == jnp.arange(cpties, dtype=jnp.int32)[None, :]).astype(f32)
    partial = lax.dot_general(ownership, sums, (((0,), (0,)), ((), ())), precision=highest)
    netted = lax.psum_scatter(partial, "trade", scatter_dimension=0, tiled=True)
    shifted = (netted - ceiling[:, None]).reshape(cpty_dev, dates, paths)
    exposure = jnp.sum(jax.nn.softplus(shifted), axis=2).T
    exposure_profile = lax.psum(exposure, "path") / (paths * lax.axis_size("path"))
    adjoint = (mass.T[:, :, None] * jax.nn.sigmoid(shifted)).reshape(cpty_dev, rows)
    gathered = lax.all_gather(adjoint, "trade", axis=0, tiled=True)
    upstream = jnp.dot(ownership, gathered, precision=highest)
    direct = lax.psum(pull_pass(dates, state, d, n, upstream), "trade")

    gain = jnp.ones((factors,), f32)
    message = jnp.zeros((paths, factors), f32)
    for t in reversed(range(dates)):
        message = rho[t][None, :] * (direct[t] + message)
        gain = rho[t] * gain
    _, message = entering((gain, message), "date", compose, identity, True)
    adjoints = []
    for t in reversed(range(dates)):
        adjoint = direct[t] + message
        adjoints.append(adjoint)
        message = rho[t][None, :] * adjoint
    return exposure_profile, jnp.stack(adjoints[::-1])


def solution(mesh):
    close = mesh.shape["date"] == 2 and mesh.shape["trade"] == 4 and mesh.shape["path"] == 2
    return jax.shard_map(
        near if close else far,
        mesh=mesh,
        in_specs=(
            P(("grp", "date"), "path", None),
            P(("grp", "date"), None),
            P(None, ("grp", "trade")),
            P(("grp", "trade")),
            P(("grp", "trade")),
            P(("grp", "trade")),
            P(("grp", "date"), "trade"),
        ),
        out_specs=(P(("grp", "date"), "trade"), P(("grp", "date"), "path", None)),
        check_vma=False,
    )
```

time: 202 us -> 69.2 us (0.34)
  matrix products: 54.4 us -> 0 us
  blocking collectives: 36.4 us -> 0 us
  local copies, waits for them, and re-layouts: 38.5 us -> 6.04 us
  waiting for transfers between devices: 47.1 us -> 15.6 us
  starting transfers between devices: 0.08 us -> 30 us
  Pallas kernels: 0 us -> 14.7 us
  between operations: 14.2 us -> 0.79 us
  other arithmetic: 8.08 us -> 1.6 us
    dot_general x34 -> x0, matrix products: 54.4 us -> none  [the longest x16 28 us: value_group(): jnp.dot(state_bf, sensitivity_portion, preferred_element_type=jnp.float32)]
    all_gather x5 -> x0, blocking collectives: 33 us -> none  [the longest x4 19.2 us: entering(): everything = jax.tree.map(lambda part: lax.all_gather(part, axis), value)]
    ppermute x0 -> x18, starting transfers between devices: none -> 30 us  [swap(): return lax.ppermute(value, axes, pairs)]
    psum x1 -> x0, waiting for transfers between devices: 25.7 us -> none  [shards(): summed = lax.psum(direct, 'trade')]
    dynamic_slice x32 -> x0, local copies, waits for them, and re-layouts: 24.5 us -> none  [the longest x16 12.2 us: pull_group(): lax.dynamic_slice_in_dim(signed_notional, opening_offset, cluster_extent, 0)]
    reduce_scatter x1 -> x0, waiting for transfers between devices: 21.4 us -> none  [shards(): lax.psum_scatter(partial_value, 'trade', scatter_dimension=0, tiled=True)]
    ppermute x0 -> x18, waiting for transfers between devices: none -> 15.6 us  [swap(): return lax.ppermute(value, axes, pairs)]
    pallas_call x0 -> x3, Pallas kernels: none -> 14.7 us  [the longest x1 6.61 us: value_pass(): pl.pallas_call(functools.partial(value_kernel, blocks), grid=(trades // s...]
  transfers between devices with their start and end apart: 2 -> 18, of which waited for: 2 -> 8; matrix products, arithmetic and copies ran while one was open for 0% -> 1% of each run, Pallas kernels for 0% -> 0%
where the time goes in v1:
time: 69.2 us; the launch traced here: 68.8 us
  starting transfers between devices  30 us (43%)
  waiting for transfers between devices  15.6 us (23%)
  Pallas kernels  14.7 us (21%)
  local copies, waits for them, and re-layouts  6.04 us (9%)
  other arithmetic  1.6 us (2%)
  between operations  0.79 us (1%)
    ppermute x18, starting transfers between devices, swap(): return lax.ppermute(value, axes, pairs)  30 us
    ppermute x18, waiting for transfers between devices, swap(): return lax.ppermute(value, axes, pairs)  15.6 us
    pallas_call x1, Pallas kernels, value_pass(): pl.pallas_call(functools.partial(value_kernel, blocks), grid=(trades // s...  6.61 us
    pallas_call x1, Pallas kernels, pull_net_pass(): pl.pallas_call(functools.partial(pull_net_kernel, shards, cpty_dev, dates...  6.47 us
    unnamed x28, local copies, waits for them, and re-layouts  5.23 us
    pallas_call x1, Pallas kernels, place(): pl.pallas_call(functools.partial(place_kernel, shards), grid_spec=pltpu.P...  1.65 us
  transfers between devices with their start and end apart: 18, of which 8 were waited for; matrix products, arithmetic and copies ran while one was open for 1% of the time, Pallas kernels for 0%

profile of v1, /device:TPU:0, one launch (start us, length us, event | category | flops | bytes accessed | tf_op | source)
XLA Modules:
  0.0 68.8 jit_solution(17803940487739917476)
XLA Ops:
  0.6 0.8 %slice_bitcast_fusion.6 = (f32[128]{0:T(128)S(1)}, f32[128]{0:T(128)S(1)}, f32[128]{0:T(128)S(1)}) fusion(f32[4,128]{1,0:T(4,128)} %rho_ref.3), kind=kLoop, calls=%fused_computation.32 | loop fusion | bytes 3072 | tf_op jit(solution)/shard_map/mul | solution.py:319
  1.4 1.0 %bitcast_add_fusion = f32[128,128]{1,0:T(8,128)S(1)} fusion(f32[4,128,128]{2,1,0:T(8,128)} %x_ref.1, f32[128]{0:T(128)S(1)} %get-tuple-element.30, f32[128]{0:T(128)S(1)} %get-tuple-element.31, f32[128]{0:T(128)S(1)} %get-tuple-element.29), kind=kLoop, calls=%fused_computation.1 | loop fusion | flops 98304 | bytes 329216 | tf_op jit(solution)/shard_map/add | solution.py:319
  2.4 3.0 %collective-permute-start = (f32[128,128]{1,0:T(8,128)S(1)}, f32[128,128]{1,0:T(8,128)S(1)}, u32[]{:S(2)}, u32[]{:S(2)}) collective-permute-start(f32[128,128]{1,0:T(8,128)S(1)} %bitcast_add_fusion), channel_id=1, source_target_pairs={{0,2},{2,0},{1,3},{3,1},{4,6},{6,4},{5,7},{7,5},{8,10},{10,8},{9,1... | collective-permute-start | bytes 196616 | tf_op jit(solution)/shard_map/ppermute | solution.py:28
  5.4 2.2 %collective-permute-done.arriving_ref = f32[128,128]{1,0:T(8,128)S(1)} collective-permute-done((f32[128,128]{1,0:T(8,128)S(1)}, f32[128,128]{1,0:T(8,128)S(1)}, u32[]{:S(2)}, u32[]{:S(2)}) %collective-permute-start) | collective-permute-done | bytes 65568 | tf_op jit(solution)/shard_map/ppermute | solution.py:28
  7.6 0.9 %copy-done = f32[4,128,128]{2,1,0:T(8,128)S(1)} copy-done((f32[4,128,128]{2,1,0:T(8,128)S(1)}, f32[4,128,128]{2,1,0:T(8,128)}, u32[]{:S(2)}) %copy-start) | copy-done | bytes 262168
  8.6 0.7 copy-done.1
  9.3 1.6 %copy-done.3 = bf16[128,8192]{1,0:T(8,128)(2,1)S(1)} copy-done((bf16[128,8192]{1,0:T(8,128)(2,1)S(1)}, bf16[128,8192]{1,0:T(8,128)(2,1)}, u32[]{:S(2)}) %copy-start.3) | copy-done | bytes 2097176
  10.9 0.8 %copy-done.5 = f32[8192]{0:T(1024)S(1)} copy-done((f32[8192]{0:T(1024)S(1)}, f32[8192]{0:T(1024)}, u32[]{:S(2)}) %copy-start.5) | copy-done | bytes 32792
  11.7 6.6 %value_pass.1 = (f32[64,512]{1,0:T(8,128)S(1)}, bf16[128,512]{1,0:T(8,128)(2,1)S(1)}) custom-call(f32[4,128,128]{2,1,0:T(8,128)S(1)} %copy-done, f32[4,128]{1,0:T(4,128)S(1)} %copy-done.1, f32[128,128]{1,0:T(8,128)S(1)} %collective-permute-done.arriving_ref, f32[8,128]{1,0:T(8,128)S(1)} %broadcast_in_dim.17.first_ref, bf16[128,8192]{1,0:T(8,128)(2,1)S(1)} %copy-done.3, ...), custom_call_target="tpu_custom_call" | custom-call | flops 1073741824 | bytes 2097152 | tf_op jit(solution)/shard_map/value_pass/pallas_call | solution.py:78
  18.3 4.2 %collective-permute-start.3 = (f32[64,512]{1,0:T(8,128)S(1)}, f32[64,512]{1,0:T(8,128)S(1)}, u32[]{:S(2)}, u32[]{:S(2)}) collective-permute-start(f32[64,512]{1,0:T(8,128)S(1)} %get-tuple-element.14.refs_0_), channel_id=1, source_target_pairs={{0,12},{4,8},{8,4},{12,0},{1,13},{5,9},{9,5},{13,1},{2,14},{6,10},... | collective-permute-start | bytes 393224 | tf_op jit(solution)/shard_map/ppermute | solution.py:28
  22.5 0.6 collective-permute-start.1
  23.1 3.8 %collective-permute-start.6 = (f32[8,128]{1,0:T(8,128)S(1)}, f32[8,128]{1,0:T(8,128)S(1)}, u32[]{:S(2)}, u32[]{:S(2)}) collective-permute-start(f32[8,128]{1,0:T(8,128)S(1)} %pad.19.refs_4_), channel_id=1, source_target_pairs={{0,12},{4,8},{8,4},{12,0},{1,13},{5,9},{9,5},{13,1},{2,14},{6,10},... | collective-permute-start | bytes 12296 | tf_op jit(solution)/shard_map/ppermute | solution.py:28
  27.0 3.7 %collective-permute-done.6.refs_7_ = f32[8,128]{1,0:T(8,128)S(1)} collective-permute-done((f32[8,128]{1,0:T(8,128)S(1)}, f32[8,128]{1,0:T(8,128)S(1)}, u32[]{:S(2)}, u32[]{:S(2)}) %collective-permute-start.6) | collective-permute-done | bytes 4128 | tf_op jit(solution)/shard_map/ppermute | solution.py:28
  30.7 2.6 %collective-permute-start.4 = (f32[8,128]{1,0:T(8,128)S(1)}, f32[8,128]{1,0:T(8,128)S(1)}, u32[]{:S(2)}, u32[]{:S(2)}) collective-permute-start(f32[8,128]{1,0:T(8,128)S(1)} %pad.19.refs_4_), channel_id=1, source_target_pairs={{0,4},{4,0},{8,12},{12,8},{1,5},{5,1},{9,13},{13,9},{2,6},{6,2},{1... | collective-permute-start | bytes 12296 | tf_op jit(solution)/shard_map/ppermute | solution.py:28
  33.3 1.6 %collective-permute-done.4.refs_5_ = f32[8,128]{1,0:T(8,128)S(1)} collective-permute-done((f32[8,128]{1,0:T(8,128)S(1)}, f32[8,128]{1,0:T(8,128)S(1)}, u32[]{:S(2)}, u32[]{:S(2)}) %collective-permute-start.4) | collective-permute-done | bytes 4128 | tf_op jit(solution)/shard_map/ppermute | solution.py:28
  34.9 6.5 %pull_net_pass.1 = (f32[4,32]{1,0:T(4,128)S(1)}, f32[4,32,128]{2,1,0:T(8,128)S(1)}, f32[4,32,128]{2,1,0:T(8,128)S(1)}, f32[4,32,128]{2,1,0:T(8,128)S(1)}, f32[4,...) custom-call(s32[1]{0:T(128)} %bitcast.me_ref, ...), custom_call_target="tpu_custom_call" | custom-call | flops 2147483648 | bytes 2097152 | tf_op jit(solution)/shard_map/pull_net_pass/pallas_call | solution.py:214
  41.4 2.1 %collective-permute-start.8 = (f32[4,32,128]{2,1,0:T(8,128)S(1)}, f32[4,32,128]{2,1,0:T(8,128)S(1)}, u32[]{:S(2)}, u32[]{:S(2)}) collective-permute-start(f32[4,32,128]{2,1,0:T(8,128)S(1)} %get-tuple-element.17), channel_id=1, source_target_pairs={{0,4},{4,0},{8,12},{12,8},{1,5},{5,1},{9,13},{13,9},{2,6},{6,2},{1... | collective-permute-start | bytes 196616 | tf_op jit(solution)/shard_map/ppermute | solution.py:28
  43.4 1.6 %collective-permute-start.9 = (f32[4,32,128]{2,1,0:T(8,128)S(1)}, f32[4,32,128]{2,1,0:T(8,128)S(1)}, u32[]{:S(2)}, u32[]{:S(2)}) collective-permute-start(f32[4,32,128]{2,1,0:T(8,128)S(1)} %get-tuple-element.18), channel_id=1, source_target_pairs={{0,8},{4,12},{8,0},{12,4},{1,9},{5,13},{9,1},{13,5},{2,10},{6,14},... | collective-permute-start | bytes 196616 | tf_op jit(solution)/shard_map/ppermute | solution.py:28
  45.0 0.9 %collective-permute-start.10 = (f32[4,32,128]{2,1,0:T(8,128)S(1)}, f32[4,32,128]{2,1,0:T(8,128)S(1)}, u32[]{:S(2)}, u32[]{:S(2)}) collective-permute-start(f32[4,32,128]{2,1,0:T(8,128)S(1)} %get-tuple-element.19), channel_id=1, source_target_pairs={{0,12},{4,8},{8,4},{12,0},{1,13},{5,9},{9,5},{13,1},{2,14},{6,10},... | collective-permute-start | bytes 196616 | tf_op jit(solution)/shard_map/ppermute | solution.py:28
  45.9 1.5 %collective-permute-start.11 = (f32[32,128]{1,0:T(8,128)S(1)}, f32[32,128]{1,0:T(8,128)S(1)}, u32[]{:S(2)}, u32[]{:S(2)}) collective-permute-start(f32[32,128]{1,0:T(8,128)S(1)} %get-tuple-element.20), channel_id=1, source_target_pairs={{0,2},{2,0},{4,6},{6,4},{8,10},{10,8},{12,14},{14,12},{1,3},{3,1},... | collective-permute-start | bytes 49160 | tf_op jit(solution)/shard_map/ppermute | solution.py:28
  47.4 1.2 %collective-permute-start.12 = (f32[32,128]{1,0:T(8,128)S(1)}, f32[32,128]{1,0:T(8,128)S(1)}, u32[]{:S(2)}, u32[]{:S(2)}) collective-permute-start(f32[32,128]{1,0:T(8,128)S(1)} %get-tuple-element.21), channel_id=1, source_target_pairs={{0,6},{2,4},{4,2},{6,0},{8,14},{10,12},{12,10},{14,8},{1,7},{3,5},... | collective-permute-start | bytes 49160 | tf_op jit(solution)/shard_map/ppermute | solution.py:28
  48.7 0.7 collective-permute-done.9
  49.3 2.5 %collective-permute-start.13 = (f32[32,128]{1,0:T(8,128)S(1)}, f32[32,128]{1,0:T(8,128)S(1)}, u32[]{:S(2)}, u32[]{:S(2)}) collective-permute-start(f32[32,128]{1,0:T(8,128)S(1)} %get-tuple-element.22), channel_id=1, source_target_pairs={{0,10},{2,8},{4,14},{6,12},{8,2},{10,0},{12,6},{14,4},{1,11},{3,9}... | collective-permute-start | bytes 49160 | tf_op jit(solution)/shard_map/ppermute | solution.py:28
  51.8 1.6 %collective-permute-start.14 = (f32[32,128]{1,0:T(8,128)S(1)}, f32[32,128]{1,0:T(8,128)S(1)}, u32[]{:S(2)}, u32[]{:S(2)}) collective-permute-start(f32[32,128]{1,0:T(8,128)S(1)} %get-tuple-element.23), channel_id=1, source_target_pairs={{0,14},{2,12},{4,10},{6,8},{8,6},{10,4},{12,2},{14,0},{1,15},{3,13... | collective-permute-start | bytes 49160 | tf_op jit(solution)/shard_map/ppermute | solution.py:28
  53.4 1.4 %collective-permute-done.13 = f32[32,128]{1,0:T(8,128)S(1)} collective-permute-done((f32[32,128]{1,0:T(8,128)S(1)}, f32[32,128]{1,0:T(8,128)S(1)}, u32[]{:S(2)}, u32[]{:S(2)}) %collective-permute-start.13) | collective-permute-done | bytes 16416 | tf_op jit(solution)/shard_map/ppermute | solution.py:28
  54.8 3.5 %collective-permute-done.14 = f32[32,128]{1,0:T(8,128)S(1)} collective-permute-done((f32[32,128]{1,0:T(8,128)S(1)}, f32[32,128]{1,0:T(8,128)S(1)}, u32[]{:S(2)}, u32[]{:S(2)}) %collective-permute-start.14) | collective-permute-done | bytes 16416 | tf_op jit(solution)/shard_map/ppermute | solution.py:28
  58.4 1.1 %collective-permute-start.17 = (f32[4,32,128]{2,1,0:T(8,128)S(1)}, f32[4,32,128]{2,1,0:T(8,128)S(1)}, u32[]{:S(2)}, u32[]{:S(2)}) collective-permute-start(f32[4,32,128]{2,1,0:T(8,128)S(1)} %pad_maximum_fusion.refs_0_), channel_id=1, source_target_pairs={{0,12},{4,8},{8,4},{12,0},{1,13},{5,9},{9,5},{13,1},{2,14},{6,10},... | collective-permute-start | bytes 196616 | tf_op jit(solution)/shard_map/ppermute | solution.py:28
  59.5 1.0 %collective-permute-start.16 = (f32[4,32,128]{2,1,0:T(8,128)S(1)}, f32[4,32,128]{2,1,0:T(8,128)S(1)}, u32[]{:S(2)}, u32[]{:S(2)}) collective-permute-start(f32[4,32,128]{2,1,0:T(8,128)S(1)} %pad_maximum_fusion.refs_0_), channel_id=1, source_target_pairs={{0,8},{4,12},{8,0},{12,4},{1,9},{5,13},{9,1},{13,5},{2,10},{6,14},... | collective-permute-start | bytes 196616 | tf_op jit(solution)/shard_map/ppermute | solution.py:28
  60.5 2.3 %collective-permute-start.15 = (f32[4,32,128]{2,1,0:T(8,128)S(1)}, f32[4,32,128]{2,1,0:T(8,128)S(1)}, u32[]{:S(2)}, u32[]{:S(2)}) collective-permute-start(f32[4,32,128]{2,1,0:T(8,128)S(1)} %pad_maximum_fusion.refs_0_), channel_id=1, source_target_pairs={{0,4},{4,0},{8,12},{12,8},{1,5},{5,1},{9,13},{13,9},{2,6},{6,2},{1... | collective-permute-start | bytes 196616 | tf_op jit(solution)/shard_map/ppermute | solution.py:28
  63.4 1.2 %collective-permute-done.17.refs_3_ = f32[4,32,128]{2,1,0:T(8,128)S(1)} collective-permute-done((f32[4,32,128]{2,1,0:T(8,128)S(1)}, f32[4,32,128]{2,1,0:T(8,128)S(1)}, u32[]{:S(2)}, u32[]{:S(2)}) %collective-permute-start.17) | collective-permute-done | bytes 65568 | tf_op jit(solution)/shard_map/ppermute | solution.py:28
  64.6 1.3 %collective-permute-done.16.refs_2_ = f32[4,32,128]{2,1,0:T(8,128)S(1)} collective-permute-done((f32[4,32,128]{2,1,0:T(8,128)S(1)}, f32[4,32,128]{2,1,0:T(8,128)S(1)}, u32[]{:S(2)}, u32[]{:S(2)}) %collective-permute-start.16) | collective-permute-done | bytes 65568 | tf_op jit(solution)/shard_map/ppermute | solution.py:28
  67.2 1.7 %place.1 = f32[4,128,128]{2,1,0:T(8,128)} custom-call(s32[1]{0:T(128)} %bitcast.me_ref, f32[4,32,128]{2,1,0:T(8,128)} %copy-done.7, f32[4,32,128]{2,1,0:T(8,128)} %copy-done.10, f32[4,32,128]{2,1,0:T(8,128)} %copy-done.9, f32[4,32,128]{2,1,0:T(8,128)} %copy-done.8), custom_call_target="tpu_custom_call" | custom-call | tf_op jit(solution)/shard_map/place/pallas_call | solution.py:302
  (46 shorter events, 1.9 us)
Async XLA Ops:
  2.4 5.2 %collective-permute-start = (f32[128,128]{1,0:T(8,128)S(1)}, f32[128,128]{1,0:T(8,128)S(1)}, u32[]{:S(2)}, u32[]{:S(2)}) collective-permute-start(f32[128,128]{1,0:T(8,128)S(1)} %bitcast_add_fusion), channel_id=1, source_target_pairs={{0,2},{2,0},{1,3},{3,1},{4,6},{6,4},{5,7},{7,5},{8,10},{10,8},{9,1... | collective-permute-start | bytes 196616 | tf_op jit(solution)/shard_map/ppermute | solution.py:28
  7.6 1.0 %copy-start = (f32[4,128,128]{2,1,0:T(8,128)S(1)}, f32[4,128,128]{2,1,0:T(8,128)}, u32[]{:S(2)}) copy-start(f32[4,128,128]{2,1,0:T(8,128)} %x_ref.1) | copy-start | bytes 786436
  8.6 0.7 copy-start.1
  9.3 1.6 %copy-start.3 = (bf16[128,8192]{1,0:T(8,128)(2,1)S(1)}, bf16[128,8192]{1,0:T(8,128)(2,1)}, u32[]{:S(2)}) copy-start(bf16[128,8192]{1,0:T(8,128)(2,1)} %d_ref.3) | copy-start | bytes 6291460
  10.9 0.8 %copy-start.5 = (f32[8192]{0:T(1024)S(1)}, f32[8192]{0:T(1024)}, u32[]{:S(2)}) copy-start(f32[8192]{0:T(1024)} %param.10) | copy-start | bytes 98308
  11.6 11.5 %copy-start.13 = (s32[64]{0:T(128)S(1)}, s32[64]{0:T(128)}, u32[]{:S(2)}) copy-start(s32[64]{0:T(128)} %param.11) | copy-start | bytes 772
  11.6 11.5 %copy-start.11 = (f32[4,32]{1,0:T(4,128)S(1)}, f32[4,32]{1,0:T(4,128)}, u32[]{:S(2)}) copy-start(f32[4,32]{1,0:T(4,128)} %param.13) | copy-start | bytes 1540
  11.6 11.5 %copy-start.12 = (f32[32]{0:T(128)S(1)}, f32[32]{0:T(128)}, u32[]{:S(2)}) copy-start(f32[32]{0:T(128)} %param.12) | copy-start | bytes 388
  11.6 23.2 %copy-start.2 = (f32[4,128]{1,0:T(4,128)S(1)}, f32[4,128]{1,0:T(4,128)}, u32[]{:S(2)}) copy-start(f32[4,128]{1,0:T(4,128)} %rho_ref.3) | copy-start | bytes 6148
  11.6 23.2 %copy-start.4 = (bf16[128,8192]{1,0:T(8,128)(2,1)S(1)}, bf16[128,8192]{1,0:T(8,128)(2,1)}, u32[]{:S(2)}) copy-start(bf16[128,8192]{1,0:T(8,128)(2,1)} %d_ref.3) | copy-start | bytes 6291460
  11.6 23.2 %copy-start.6 = (f32[8192]{0:T(1024)S(1)}, f32[8192]{0:T(1024)}, u32[]{:S(2)}) copy-start(f32[8192]{0:T(1024)} %param.10) | copy-start | bytes 98308
  18.3 16.6 %collective-permute-start.3 = (f32[64,512]{1,0:T(8,128)S(1)}, f32[64,512]{1,0:T(8,128)S(1)}, u32[]{:S(2)}, u32[]{:S(2)}) collective-permute-start(f32[64,512]{1,0:T(8,128)S(1)} %get-tuple-element.14.refs_0_), channel_id=1, source_target_pairs={{0,12},{4,8},{8,4},{12,0},{1,13},{5,9},{9,5},{13,1},{2,14},{6,10},... | collective-permute-start | bytes 393224 | tf_op jit(solution)/shard_map/ppermute | solution.py:28
  22.5 12.4 %collective-permute-start.2 = (f32[64,512]{1,0:T(8,128)S(1)}, f32[64,512]{1,0:T(8,128)S(1)}, u32[]{:S(2)}, u32[]{:S(2)}) collective-permute-start(f32[64,512]{1,0:T(8,128)S(1)} %get-tuple-element.14.refs_0_), channel_id=1, source_target_pairs={{0,8},{4,12},{8,0},{12,4},{1,9},{5,13},{9,1},{13,5},{2,10},{6,14},... | collective-permute-start | bytes 393224 | tf_op jit(solution)/shard_map/ppermute | solution.py:28
  22.5 12.4 %collective-permute-start.1 = (f32[64,512]{1,0:T(8,128)S(1)}, f32[64,512]{1,0:T(8,128)S(1)}, u32[]{:S(2)}, u32[]{:S(2)}) collective-permute-start(f32[64,512]{1,0:T(8,128)S(1)} %get-tuple-element.14.refs_0_), channel_id=1, source_target_pairs={{0,4},{4,0},{8,12},{12,8},{1,5},{5,1},{9,13},{13,9},{2,6},{6,2},{1... | collective-permute-start | bytes 393224 | tf_op jit(solution)/shard_map/ppermute | solution.py:28
  23.1 7.5 %collective-permute-start.6 = (f32[8,128]{1,0:T(8,128)S(1)}, f32[8,128]{1,0:T(8,128)S(1)}, u32[]{:S(2)}, u32[]{:S(2)}) collective-permute-start(f32[8,128]{1,0:T(8,128)S(1)} %pad.19.refs_4_), channel_id=1, source_target_pairs={{0,12},{4,8},{8,4},{12,0},{1,13},{5,9},{9,5},{13,1},{2,14},{6,10},... | collective-permute-start | bytes 12296 | tf_op jit(solution)/shard_map/ppermute | solution.py:28
  27.0 6.3 %collective-permute-start.5 = (f32[8,128]{1,0:T(8,128)S(1)}, f32[8,128]{1,0:T(8,128)S(1)}, u32[]{:S(2)}, u32[]{:S(2)}) collective-permute-start(f32[8,128]{1,0:T(8,128)S(1)} %pad.19.refs_4_), channel_id=1, source_target_pairs={{0,8},{4,12},{8,0},{12,4},{1,9},{5,13},{9,1},{13,5},{2,10},{6,14},... | collective-permute-start | bytes 12296 | tf_op jit(solution)/shard_map/ppermute | solution.py:28
  30.7 4.1 %collective-permute-start.4 = (f32[8,128]{1,0:T(8,128)S(1)}, f32[8,128]{1,0:T(8,128)S(1)}, u32[]{:S(2)}, u32[]{:S(2)}) collective-permute-start(f32[8,128]{1,0:T(8,128)S(1)} %pad.19.refs_4_), channel_id=1, source_target_pairs={{0,4},{4,0},{8,12},{12,8},{1,5},{5,1},{9,13},{13,9},{2,6},{6,2},{1... | collective-permute-start | bytes 12296 | tf_op jit(solution)/shard_map/ppermute | solution.py:28
  41.4 6.1 %collective-permute-start.8 = (f32[4,32,128]{2,1,0:T(8,128)S(1)}, f32[4,32,128]{2,1,0:T(8,128)S(1)}, u32[]{:S(2)}, u32[]{:S(2)}) collective-permute-start(f32[4,32,128]{2,1,0:T(8,128)S(1)} %get-tuple-element.17), channel_id=1, source_target_pairs={{0,4},{4,0},{8,12},{12,8},{1,5},{5,1},{9,13},{13,9},{2,6},{6,2},{1... | collective-permute-start | bytes 196616 | tf_op jit(solution)/shard_map/ppermute | solution.py:28
  43.4 5.9 %collective-permute-start.9 = (f32[4,32,128]{2,1,0:T(8,128)S(1)}, f32[4,32,128]{2,1,0:T(8,128)S(1)}, u32[]{:S(2)}, u32[]{:S(2)}) collective-permute-start(f32[4,32,128]{2,1,0:T(8,128)S(1)} %get-tuple-element.18), channel_id=1, source_target_pairs={{0,8},{4,12},{8,0},{12,4},{1,9},{5,13},{9,1},{13,5},{2,10},{6,14},... | collective-permute-start | bytes 196616 | tf_op jit(solution)/shard_map/ppermute | solution.py:28
  45.0 6.8 %collective-permute-start.10 = (f32[4,32,128]{2,1,0:T(8,128)S(1)}, f32[4,32,128]{2,1,0:T(8,128)S(1)}, u32[]{:S(2)}, u32[]{:S(2)}) collective-permute-start(f32[4,32,128]{2,1,0:T(8,128)S(1)} %get-tuple-element.19), channel_id=1, source_target_pairs={{0,12},{4,8},{8,4},{12,0},{1,13},{5,9},{9,5},{13,1},{2,14},{6,10},... | collective-permute-start | bytes 196616 | tf_op jit(solution)/shard_map/ppermute | solution.py:28
  45.9 16.9 %collective-permute-start.7 = (f32[4,32]{1,0:T(4,128)S(1)}, f32[4,32]{1,0:T(4,128)S(1)}, u32[]{:S(2)}, u32[]{:S(2)}) collective-permute-start(f32[4,32]{1,0:T(4,128)S(1)} %get-tuple-element.15), channel_id=1, source_target_pairs={{0,1},{1,0},{2,3},{3,2},{4,5},{5,4},{6,7},{7,6},{8,9},{9,8},{10,11... | collective-permute-start | bytes 1544 | tf_op jit(solution)/shard_map/ppermute | solution.py:28
  45.9 7.5 %collective-permute-start.11 = (f32[32,128]{1,0:T(8,128)S(1)}, f32[32,128]{1,0:T(8,128)S(1)}, u32[]{:S(2)}, u32[]{:S(2)}) collective-permute-start(f32[32,128]{1,0:T(8,128)S(1)} %get-tuple-element.20), channel_id=1, source_target_pairs={{0,2},{2,0},{4,6},{6,4},{8,10},{10,8},{12,14},{14,12},{1,3},{3,1},... | collective-permute-start | bytes 49160 | tf_op jit(solution)/shard_map/ppermute | solution.py:28
  47.4 6.0 %collective-permute-start.12 = (f32[32,128]{1,0:T(8,128)S(1)}, f32[32,128]{1,0:T(8,128)S(1)}, u32[]{:S(2)}, u32[]{:S(2)}) collective-permute-start(f32[32,128]{1,0:T(8,128)S(1)} %get-tuple-element.21), channel_id=1, source_target_pairs={{0,6},{2,4},{4,2},{6,0},{8,14},{10,12},{12,10},{14,8},{1,7},{3,5},... | collective-permute-start | bytes 49160 | tf_op jit(solution)/shard_map/ppermute | solution.py:28
  49.3 5.5 %collective-permute-start.13 = (f32[32,128]{1,0:T(8,128)S(1)}, f32[32,128]{1,0:T(8,128)S(1)}, u32[]{:S(2)}, u32[]{:S(2)}) collective-permute-start(f32[32,128]{1,0:T(8,128)S(1)} %get-tuple-element.22), channel_id=1, source_target_pairs={{0,10},{2,8},{4,14},{6,12},{8,2},{10,0},{12,6},{14,4},{1,11},{3,9}... | collective-permute-start | bytes 49160 | tf_op jit(solution)/shard_map/ppermute | solution.py:28
  51.8 6.5 %collective-permute-start.14 = (f32[32,128]{1,0:T(8,128)S(1)}, f32[32,128]{1,0:T(8,128)S(1)}, u32[]{:S(2)}, u32[]{:S(2)}) collective-permute-start(f32[32,128]{1,0:T(8,128)S(1)} %get-tuple-element.23), channel_id=1, source_target_pairs={{0,14},{2,12},{4,10},{6,8},{8,6},{10,4},{12,2},{14,0},{1,15},{3,13... | collective-permute-start | bytes 49160 | tf_op jit(solution)/shard_map/ppermute | solution.py:28
  58.4 7.6 %copy-start.7 = (f32[4,32,128]{2,1,0:T(8,128)}, f32[4,32,128]{2,1,0:T(8,128)S(1)}, u32[]{:S(2)}) copy-start(f32[4,32,128]{2,1,0:T(8,128)S(1)} %pad_maximum_fusion.refs_0_) | copy-start | bytes 196612
  58.4 6.2 %collective-permute-start.17 = (f32[4,32,128]{2,1,0:T(8,128)S(1)}, f32[4,32,128]{2,1,0:T(8,128)S(1)}, u32[]{:S(2)}, u32[]{:S(2)}) collective-permute-start(f32[4,32,128]{2,1,0:T(8,128)S(1)} %pad_maximum_fusion.refs_0_), channel_id=1, source_target_pairs={{0,12},{4,8},{8,4},{12,0},{1,13},{5,9},{9,5},{13,1},{2,14},{6,10},... | collective-permute-start | bytes 196616 | tf_op jit(solution)/shard_map/ppermute | solution.py:28
  59.5 6.4 %collective-permute-start.16 = (f32[4,32,128]{2,1,0:T(8,128)S(1)}, f32[4,32,128]{2,1,0:T(8,128)S(1)}, u32[]{:S(2)}, u32[]{:S(2)}) collective-permute-start(f32[4,32,128]{2,1,0:T(8,128)S(1)} %pad_maximum_fusion.refs_0_), channel_id=1, source_target_pairs={{0,8},{4,12},{8,0},{12,4},{1,9},{5,13},{9,1},{13,5},{2,10},{6,14},... | collective-permute-start | bytes 196616 | tf_op jit(solution)/shard_map/ppermute | solution.py:28
  60.5 5.4 %collective-permute-start.15 = (f32[4,32,128]{2,1,0:T(8,128)S(1)}, f32[4,32,128]{2,1,0:T(8,128)S(1)}, u32[]{:S(2)}, u32[]{:S(2)}) collective-permute-start(f32[4,32,128]{2,1,0:T(8,128)S(1)} %pad_maximum_fusion.refs_0_), channel_id=1, source_target_pairs={{0,4},{4,0},{8,12},{12,8},{1,5},{5,1},{9,13},{13,9},{2,6},{6,2},{1... | collective-permute-start | bytes 196616 | tf_op jit(solution)/shard_map/ppermute | solution.py:28
  64.6 1.3 %copy-start.8 = (f32[4,32,128]{2,1,0:T(8,128)}, f32[4,32,128]{2,1,0:T(8,128)S(1)}, u32[]{:S(2)}) copy-start(f32[4,32,128]{2,1,0:T(8,128)S(1)} %collective-permute-done.17.refs_3_) | copy-start | bytes 196612
  65.9 0.6 copy-start.9
  66.5 0.6 copy-start.10

commit v2 on v1

--- a/solution.py
+++ b/solution.py
@@ -52,51 +52,91 @@
     return jnp.maximum(v, jnp.log(1.0 + jnp.exp(jnp.minimum(v, 80.0))))
 
 
-def value_kernel(blocks, x_ref, rho_ref, arriving_ref, first_ref, d_ref, n_ref, sums_ref, state_ref):
-    dates, paths, _ = x_ref.shape
+def chain_kernel(x_ref, rho_ref, carried_ref):
+    carried = x_ref[0]
+    for t in range(1, x_ref.shape[0]):
+        carried = rho_ref[t : t + 1, :] * carried + x_ref[t]
+    carried_ref[...] = carried
+
+
+def chain_pass(x, rho):
+    return pl.pallas_call(
+        chain_kernel, out_shape=jax.ShapeDtypeStruct(x.shape[1:], f32), name="chain_pass"
+    )(x, rho)
+
+
+def prepare_kernel(d_ref, n_ref, x_ref, rho_ref, turned_ref, size_ref, x_out_ref, rho_out_ref):
+    turned_ref[...] = d_ref[...].T
 
     @pl.when(pl.program_id(0) == 0)
     def _():
-        carried = arriving_ref[...] * first_ref[0:1, :]
-        for t in range(dates):
-            carried = rho_ref[t : t + 1, :] * carried + x_ref[t]
-            state_ref[:, t * paths : (t + 1) * paths] = carried.T.astype(bf16)
-
-    size_t = n_ref[...].T
-    linear = jnp.dot(d_ref[...].T, state_ref[...], preferred_element_type=f32)
-    for b in range(blocks):
-        value = softplus(linear[b * block_width : (b + 1) * block_width]) * size_t[:, b : b + 1]
-        sums_ref[b : b + 1, :] = jnp.sum(value, axis=0, keepdims=True)
-
-
-def value_pass(x, rho, arriving, keep, d, n):
-    dates, paths, factors = x.shape
-    rows, trades = dates * paths, d.shape[1]
+        size_ref[...] = n_ref[...]
+        x_out_ref[...] = x_ref[...]
+        rho_out_ref[...] = rho_ref[...]
+
+
+def prepare_pass(d, n, x, rho):
+    factors, trades = d.shape
     step = min(2048, trades)
-    blocks = step // block_width
     whole = lambda *shape: pl.BlockSpec(shape, lambda i: (0,) * len(shape))
     return pl.pallas_call(
-        functools.partial(value_kernel, blocks),
+        prepare_kernel,
         grid=(trades // step,),
-        in_specs=[
-            whole(dates, paths, factors),
-            whole(dates, factors),
-            whole(paths, factors),
-            whole(8, factors),
-            pl.BlockSpec((factors, step), lambda i: (0, i)),
-            pl.BlockSpec((blocks, block_width), lambda i: (i, 0)),
+        in_specs=[pl.BlockSpec((factors, step), lambda i: (0, i)), whole(*n.shape), whole(*x.shape), whole(*rho.shape)],
+        out_specs=[pl.BlockSpec((step, factors), lambda i: (i, 0)), whole(*n.shape), whole(*x.shape), whole(*rho.shape)],
+        out_shape=[
+            jax.ShapeDtypeStruct((trades, factors), bf16),
+            jax.ShapeDtypeStruct(n.shape, f32),
+            jax.ShapeDtypeStruct(x.shape, f32),
+            jax.ShapeDtypeStruct(rho.shape, f32),
         ],
-        out_specs=[pl.BlockSpec((blocks, rows), lambda i: (i, 0)), whole(factors, rows)],
+        compiler_params=pltpu.CompilerParams(vmem_limit_bytes=8 << 20),
+        cost_estimate=pl.CostEstimate(flops=0, bytes_accessed=4 * trades * factors, transcendentals=0),
+        name="prepare_pass",
+    )(d, n, x, rho)
+
+
+def value_kernel(step, x_ref, rho_ref, arriving_ref, keep_ref, facts_ref, turned_ref, n_ref, sums_ref, state_ref):
+    dates, paths, _ = x_ref.shape
+    trades = turned_ref.shape[0]
+    blocks = step // block_width
+    carried = arriving_ref[...] * keep_ref[0].astype(f32)
+    for t in range(dates):
+        carried = rho_ref[t : t + 1, :] * carried + x_ref[t]
+        state_ref[:, t * paths : (t + 1) * paths] = carried.T.astype(bf16)
+    total = trades // block_width
+    sums_ref[total : total + 8, :128] = facts_ref[...]
+
+    @pl.loop(0, trades // step)
+    def _(c):
+        size_t = n_ref[pl.ds(pl.multiple_of(c * blocks, blocks), blocks), :].T
+        turned = turned_ref[pl.ds(pl.multiple_of(c * step, step), step), :]
+        linear = jnp.dot(turned, state_ref[...], preferred_element_type=f32)
+        lines = []
+        for b in range(blocks):
+            value = softplus(linear[b * block_width : (b + 1) * block_width]) * size_t[:, b : b + 1]
+            lines.append(jnp.sum(value, axis=0, keepdims=True))
+        sums_ref[pl.ds(pl.multiple_of(c * blocks, blocks), blocks), :] = jnp.concatenate(lines, axis=0)
+
+
+def value_pass(x, rho, arriving, keep, facts, turned, n):
+    dates, paths, factors = x.shape
+    rows, trades = dates * paths, turned.shape[0]
+    vmem = pl.BlockSpec(memory_space=pltpu.VMEM)
+    return pl.pallas_call(
+        functools.partial(value_kernel, min(2048, trades)),
+        in_specs=[vmem, vmem, vmem, pl.BlockSpec(memory_space=pltpu.SMEM), vmem, vmem, vmem],
+        out_specs=[vmem, vmem],
         out_shape=[
-            jax.ShapeDtypeStruct((trades // block_width, rows), f32),
+            jax.ShapeDtypeStruct((trades // block_width + 8, rows), f32),
             jax.ShapeDtypeStruct((factors, rows), bf16),
         ],
-        compiler_params=pltpu.CompilerParams(vmem_limit_bytes=50 << 20),
+        compiler_params=pltpu.CompilerParams(vmem_limit_bytes=32 << 20),
         cost_estimate=pl.CostEstimate(
             flops=2 * rows * trades * factors, bytes_accessed=2 * trades * factors, transcendentals=2 * rows * trades
         ),
         name="value_pass",
-    )(x, rho, arriving, keep, d, n)
+    )(x, rho, arriving, keep, facts, turned, n)
 
 
 def split_dot(selector, value):
@@ -109,8 +149,10 @@
     return dot(low) + dot(middle) + dot(high)
 
 
-def net_stage(shards, cpty_dev, dates, me, sums, small, upstream_ref, exposure_ref):
+def net_stage(shards, cpty_dev, dates, me, sums, upstream_ref, exposure_ref):
     blocks, rows = sums[0].shape
+    blocks -= 8
+    small = [part.at[blocks : blocks + 8, :128] for part in sums]
     paths = rows // dates
     cpties = shards * cpty_dev
     shift = cpty_dev.bit_length() - 1
@@ -127,7 +169,7 @@
 
         row = label(small[k][dates + 1 : dates + 2, :blocks])
         pick = lax.broadcasted_iota(jnp.int32, (cpties, blocks), 0) == row
-        part = split_dot(jnp.where(pick, 1.0, 0.0), sums[k][...])
+        part = split_dot(jnp.where(pick, 1.0, 0.0), sums[k][:blocks])
         netted = part if netted is None else netted + part
         if k == 0:
             column = label(tall[:blocks, dates + 1 : dates + 2])
@@ -169,11 +211,9 @@
 
 def pull_net_kernel(shards, cpty_dev, dates, blocks, me_ref, state_ref, rho_ref, d_ref, n_ref, *refs):
     sums, refs = refs[:shards], refs[shards:]
-    small, refs = refs[:shards], refs[shards:]
     exposure_ref, refs = refs[0], refs[1:]
     chain, refs = refs[:shards], refs[shards:]
-    message, refs = refs[:shards], refs[shards:]
-    upstream_ref, half_ref, total_ref, chained_ref, message_ref = refs
+    upstream_ref, half_ref, total_ref, chained_ref = refs
     rows = state_ref.shape[1]
     paths = rows // dates
     i = pl.program_id(0)
@@ -183,7 +223,7 @@
     def _():
         half_ref[...] = state_ref[...] * 0.5
         total_ref[...] = jnp.zeros_like(total_ref)
-        net_stage(shards, cpty_dev, dates, me, sums, small, upstream_ref, exposure_ref)
+        net_stage(shards, cpty_dev, dates, me, sums, upstream_ref, exposure_ref)
 
     upstream = upstream_ref[pl.ds(pl.multiple_of(i * blocks, blocks), blocks), :]
     pull_step(blocks, upstream, half_ref, d_ref, n_ref, total_ref)
@@ -195,15 +235,13 @@
             adjoint = total_ref[:, t * paths : (t + 1) * paths].T + carried
             chained_ref[t] = adjoint
             carried = rho_ref[t : t + 1, :] * adjoint
-        message_ref[...] = carried
         piece = paths // shards
         for k in range(shards):
             at = pl.ds(pl.multiple_of((me ^ k) * piece, piece), piece)
             chain[k][...] = chained_ref[:, at, :]
-            message[k][...] = message_ref[at, :]
-
-
-def pull_net_pass(shards, dates, cpty_dev, me, state, rho, d, n, sums, small):
+
+
+def pull_net_pass(shards, dates, cpty_dev, me, state, rho, d, n, sums):
     factors, rows = state.shape
     trades = d.shape[1]
     paths = rows // dates
@@ -222,29 +260,24 @@
                 pl.BlockSpec((factors, step), lambda i, s: (0, i)),
                 pl.BlockSpec((blocks, block_width), lambda i, s: (i, 0)),
             ]
-            + [whole(*part.shape) for part in sums]
-            + [whole(*part.shape) for part in small],
-            out_specs=[whole(dates, cpty_dev)]
-            + [whole(dates, piece, factors)] * shards
-            + [whole(piece, factors)] * shards,
+            + [whole(*part.shape) for part in sums],
+            out_specs=[whole(dates, cpty_dev)] + [whole(dates, piece, factors)] * shards,
             scratch_shapes=[
-                pltpu.VMEM(sums[0].shape, f32),
+                pltpu.VMEM((trades // block_width, rows), f32),
                 pltpu.VMEM((factors, rows), bf16),
                 pltpu.VMEM((factors, rows), f32),
                 pltpu.VMEM((dates, paths, factors), f32),
-                pltpu.VMEM((paths, factors), f32),
             ],
         ),
         out_shape=[jax.ShapeDtypeStruct((dates, cpty_dev), f32)]
-        + [jax.ShapeDtypeStruct((dates, piece, factors), f32)] * shards
-        + [jax.ShapeDtypeStruct((piece, factors), f32)] * shards,
-        compiler_params=pltpu.CompilerParams(vmem_limit_bytes=50 << 20),
+        + [jax.ShapeDtypeStruct((dates, piece, factors), f32)] * shards,
+        compiler_params=pltpu.CompilerParams(vmem_limit_bytes=32 << 20),
         cost_estimate=pl.CostEstimate(
             flops=4 * rows * trades * factors, bytes_accessed=2 * trades * factors, transcendentals=rows * trades
         ),
         name="pull_net_pass",
-    )(me, state, rho, d, n, *sums, *small)
-    return out[0], out[1 : 1 + shards], out[1 + shards :]
+    )(me, state, rho, d, n, *sums)
+    return out[0], out[1:]
 
 
 def pull_kernel(blocks, state_ref, d_ref, n_ref, upstream_ref, direct_ref, half_ref, total_ref):
@@ -308,6 +341,7 @@
             out_specs=whole(dates, shards * size, factors),
         ),
         out_shape=jax.ShapeDtypeStruct((dates, shards * size, factors), f32),
+        compiler_params=pltpu.CompilerParams(vmem_limit_bytes=4 << 20),
         name="place",
     )(me, *pieces)
 
@@ -326,34 +360,29 @@
     shards = lax.axis_size("trade")
     cpty_dev = ceiling.shape[0]
     n = size.reshape(-1, block_width)
-    blocks = n.shape[0]
     me = lax.axis_index("trade").astype(jnp.int32)[None]
-    later = lax.axis_index("date") > 0
-    _, carried = local_chain(x, rho)
-    arriving = swap(carried, ("date",), (2,), (1,))
-    keep = jnp.broadcast_to(jnp.where(later, 1.0, 0.0).astype(f32), (8, factors))
-
+    date = lax.axis_index("date").astype(jnp.int32)
+    over = lambda value, k: swap(value, ("trade",), (shards,), (k,))
+
+    arriving = swap(chain_pass(x, rho), ("date",), (2,), (1,))
+    turned, n_near, x_near, rho_near = prepare_pass(d, n, x, rho)
     wide = lambda part: jnp.pad(part, ((0, 0), (0, 128 - part.shape[1])))
     facts = jnp.concatenate([wide(mass), wide(ceiling[None, :]), wide(obligor.astype(f32)[None, :])], axis=0)
     facts = jnp.pad(facts, ((0, 8 - facts.shape[0]), (0, 0)))
-    small = [facts] + [swap(facts, ("trade",), (shards,), (k,)) for k in range(1, shards)]
-
-    sums, state = value_pass(x, rho, arriving, keep, d, n)
-    sums = [sums] + [swap(sums, ("trade",), (shards,), (k,)) for k in range(1, shards)]
-    exposure, chain, message = pull_net_pass(shards, dates, cpty_dev, me, state, rho, d, n, sums, small)
-    total_paths = paths * lax.axis_size("path")
-    exposure_profile = (exposure + swap(exposure, ("path",), (2,), (1,))) / total_paths
-
-    chain = [chain[0]] + [swap(chain[k], ("trade",), (shards,), (k,)) for k in range(1, shards)]
-    message = [swap(message[k], ("trade", "date"), (shards, 2), (k, 1)) for k in range(shards)]
-    total = functools.reduce(jnp.add, chain)
-    reached = jnp.where(later, 0.0, functools.reduce(jnp.add, message))
-    rows = []
-    for t in reversed(range(dates)):
-        rows.append(total[t] + reached)
-        reached = rho[t][None, :] * reached
-    own = jnp.stack(rows[::-1])
-    pieces = [own] + [swap(own, ("trade",), (shards,), (k,)) for k in range(1, shards)]
+    sums, state = value_pass(x_near, rho_near, arriving, date[None], facts, turned, n_near)
+
+    sums = [sums] + [over(sums, k) for k in range(1, shards)]
+    exposure, chain = pull_net_pass(shards, dates, cpty_dev, me, state, rho, d, n, sums)
+    total = functools.reduce(jnp.add, [chain[0]] + [over(chain[k], k) for k in range(1, shards)])
+
+    message = swap(rho[0][None, :] * total[0], ("date",), (2,), (1,))
+    weights = [jnp.where(date > 0, 0.0, jnp.ones((factors,), f32))]
+    for t in reversed(range(1, dates)):
+        weights.append(rho[t] * weights[-1])
+    own = total + jnp.stack(weights[::-1])[:, None, :] * message[None]
+    own, exposure = lax.optimization_barrier((own, exposure))
+    pieces = [own] + [over(own, k) for k in range(1, shards)]
+    exposure_profile = (exposure + swap(exposure, ("path",), (2,), (1,))) / (paths * lax.axis_size("path"))
     return exposure_profile, place(me, pieces)
 
 
@@ -365,7 +394,10 @@
     value = local_chain(x, rho)
     identity = (jnp.ones_like(value[0]), jnp.zeros_like(value[1]))
     _, arriving = entering(value, "date", compose, identity, False)
-    sums, state = value_pass(x, rho, arriving, jnp.ones((8, factors), f32), d, n)
+    turned, n_near, x_near, rho_near = prepare_pass(d, n, x, rho)
+    keep = jnp.ones((1,), jnp.int32)
+    sums, state = value_pass(x_near, rho_near, arriving, keep, jnp.zeros((8, 128), f32), turned, n_near)
+    sums = sums[: n.shape[0]]
     cpties = cpty_dev * lax.axis_size("trade")
     ownership = (obligor[:, None] == jnp.arange(cpties, dtype=jnp.int32)[None, :]).astype(f32)
     partial = lax.dot_general(ownership, sums, (((0,), (0,)), ((), ())), precision=highest)

time: 69.2 us -> 63 us (0.910)
  starting transfers between devices: 30 us -> 16.3 us
  waiting for transfers between devices: 15.6 us -> 24.5 us
  local copies, waits for them, and re-layouts: 6.04 us -> 4.01 us
  Pallas kernels: 14.7 us -> 15.9 us
    ppermute x18 -> x12, starting transfers between devices: 30 us -> 16.3 us  [swap(): return lax.ppermute(value, axes, pairs)]
    ppermute x18 -> x12, waiting for transfers between devices: 15.6 us -> 24.5 us  [swap(): return lax.ppermute(value, axes, pairs)]
    pallas_call x1 -> x3, Pallas kernels: 6.61 us -> 8.79 us  [the longest x1 6.22 us: value_pass(): pl.pallas_call(functools.partial(value_kernel, min(2048, trades)), in_spe...]
    unnamed x28 -> x18, local copies, waits for them, and re-layouts: 5.23 us -> 4.01 us
    add x2, other arithmetic: 0.97 us -> 0.03 us  [the longest x1 0.02 us: near(): functools.reduce(jnp.add, [chain[0]] + [over(chain[k], k) for k in range(...]
    pallas_call x1, Pallas kernels: 1.65 us -> 0.72 us  [place(): pl.pallas_call(functools.partial(place_kernel, shards), grid_spec=pltpu.P...]
    mul x1 -> x0, local copies, waits for them, and re-layouts: 0.8 us -> none  [local_chain(): carried = rho[t][None, :] * carried + x[t]]
  transfers between devices with their start and end apart: 18 -> 12, of which waited for: 8 -> 8; matrix products, arithmetic and copies ran while one was open for 1% -> 2% of each run, Pallas kernels for 0% -> 2%
where the time goes in v2:
time: 63 us; the launch traced here: 62.7 us
  waiting for transfers between devices  24.5 us (39%)
  starting transfers between devices  16.3 us (26%)
  Pallas kernels  15.9 us (25%)
  local copies, waits for them, and re-layouts  4.01 us (6%)
  other arithmetic  1.3 us (2%)
  between operations  0.78 us (1%)
    ppermute x12, waiting for transfers between devices, swap(): return lax.ppermute(value, axes, pairs)  24.5 us
    ppermute x12, starting transfers between devices, swap(): return lax.ppermute(value, axes, pairs)  16.3 us
    pallas_call x1, Pallas kernels, pull_net_pass(): pl.pallas_call(functools.partial(pull_net_kernel, shards, cpty_dev, dates...  6.4 us
    pallas_call x1, Pallas kernels, value_pass(): pl.pallas_call(functools.partial(value_kernel, min(2048, trades)), in_spe...  6.22 us
    unnamed x18, local copies, waits for them, and re-layouts  4.01 us
    pallas_call x1, Pallas kernels, chain_pass(): pl.pallas_call(chain_kernel, out_shape=jax.ShapeDtypeStruct(x.shape[1:],...  1.61 us
  transfers between devices with their start and end apart: 12, of which 8 were waited for; matrix products, arithmetic and copies ran while one was open for 2% of the time, Pallas kernels for 2%

profile of v2, /device:TPU:0, one launch (start us, length us, event | category | flops | bytes accessed | tf_op | source)
XLA Modules:
  0.0 62.7 jit_solution(15979129549015827993)
XLA Ops:
  0.6 1.6 %chain_pass.1 = f32[128,128]{1,0:T(8,128)} custom-call(f32[4,128,128]{2,1,0:T(8,128)} %x_ref.3, f32[4,128]{1,0:T(4,128)} %rho_ref.5), custom_call_target="tpu_custom_call" | custom-call | tf_op jit(solution)/shard_map/chain_pass/pallas_call | solution.py:63
  2.3 2.9 %collective-permute-start = (f32[128,128]{1,0:T(8,128)}, f32[128,128]{1,0:T(8,128)S(1)}, u32[]{:S(2)}, u32[]{:S(2)}) collective-permute-start(f32[128,128]{1,0:T(8,128)} %chain_pass.1), channel_id=1, source_target_pairs={{0,2},{2,0},{1,3},{3,1},{4,6},{6,4},{5,7},{7,5},{8,10},{10,8},{9,1... | collective-permute-start | bytes 196616 | tf_op jit(solution)/shard_map/ppermute | solution.py:28
  5.2 0.7 %convert_bitcast_fusion = f32[1,64]{1,0:T(1,128)S(1)} fusion(s32[64]{0:T(128)} %param.11), kind=kLoop, calls=%fused_computation.17 | loop fusion | flops 64 | bytes 512 | tf_op jit(solution)/shard_map/broadcast_in_dim | solution.py:370
  5.9 1.6 %copy-done = bf16[128,8192]{1,0:T(8,128)(2,1)S(1)} copy-done((bf16[128,8192]{1,0:T(8,128)(2,1)S(1)}, bf16[128,8192]{1,0:T(8,128)(2,1)}, u32[]{:S(2)}) %copy-start) | copy-done | bytes 2097176
  7.5 0.9 %copy-done.2 = f32[4,128,128]{2,1,0:T(8,128)S(1)} copy-done((f32[4,128,128]{2,1,0:T(8,128)S(1)}, f32[4,128,128]{2,1,0:T(8,128)}, u32[]{:S(2)}) %copy-start.2) | copy-done | bytes 262168
  8.4 0.8 %copy-done.3 = f32[8192]{0:T(1024)S(1)} copy-done((f32[8192]{0:T(1024)S(1)}, f32[8192]{0:T(1024)}, u32[]{:S(2)}) %copy-start.3) | copy-done | bytes 32792
  9.2 0.7 %copy-done.5 = f32[4,128]{1,0:T(4,128)S(1)} copy-done((f32[4,128]{1,0:T(4,128)S(1)}, f32[4,128]{1,0:T(4,128)}, u32[]{:S(2)}) %copy-start.5) | copy-done | bytes 2072
  9.8 1.0 %prepare_pass.1 = (bf16[8192,128]{1,0:T(8,128)(2,1)S(1)}, f32[64,128]{1,0:T(8,128)S(1)}, f32[4,128,128]{2,1,0:T(8,128)S(1)}, f32[4,128]{1,0:T(4,128)S(1)}) custom-call(bf16[128,8192]{1,0:T(8,128)(2,1)S(1)} %copy-done, f32[64,128]{1,0:T(8,128)S(1)} %bitcast.12, f32[4,128,128]{2,1,0:T(8,128)S(1)} %copy-done.2, f32[4,128]{1,0:T(4,128)S(1)} %copy-done.5), custom_call_target="tpu_custom_call" | custom-call | bytes 4194304 | tf_op jit(solution)/shard_map/prepare_pass/pallas_call | solution.py:82
  10.9 0.0 copy-start.1
  10.9 6.2 %value_pass.1 = (f32[72,512]{1,0:T(8,128)S(1)}, bf16[128,512]{1,0:T(8,128)(2,1)S(1)}) custom-call(f32[4,128,128]{2,1,0:T(8,128)S(1)} %get-tuple-element.15.x_ref, f32[4,128]{1,0:T(4,128)S(1)} %get-tuple-element.16.rho_ref, f32[128,128]{1,0:T(8,128)S(1)} %collective-permute-done.arriving_ref, s32[1]{0:T(128)} %bitcast.2.keep_ref, ...), custom_call_target="tpu_custom_call" | custom-call | flops 1073741824 | bytes 2097152 | tf_op jit(solution)/shard_map/value_pass/pallas_call | solution.py:126
  17.1 1.6 %collective-permute-start.1 = (f32[72,512]{1,0:T(8,128)S(1)}, f32[72,512]{1,0:T(8,128)S(1)}, u32[]{:S(2)}, u32[]{:S(2)}) collective-permute-start(f32[72,512]{1,0:T(8,128)S(1)} %get-tuple-element.20.refs_0_), channel_id=1, source_target_pairs={{0,4},{4,0},{8,12},{12,8},{1,5},{5,1},{9,13},{13,9},{2,6},{6,2},{1... | collective-permute-start | bytes 442376 | tf_op jit(solution)/shard_map/ppermute | solution.py:28
  18.8 2.6 %collective-permute-start.2 = (f32[72,512]{1,0:T(8,128)S(1)}, f32[72,512]{1,0:T(8,128)S(1)}, u32[]{:S(2)}, u32[]{:S(2)}) collective-permute-start(f32[72,512]{1,0:T(8,128)S(1)} %get-tuple-element.20.refs_0_), channel_id=1, source_target_pairs={{0,8},{4,12},{8,0},{12,4},{1,9},{5,13},{9,1},{13,5},{2,10},{6,14},... | collective-permute-start | bytes 442376 | tf_op jit(solution)/shard_map/ppermute | solution.py:28
  21.4 0.2 collective-permute-start.3
  21.6 2.8 %collective-permute-done.1.refs_1_ = f32[72,512]{1,0:T(8,128)S(1)} collective-permute-done((f32[72,512]{1,0:T(8,128)S(1)}, f32[72,512]{1,0:T(8,128)S(1)}, u32[]{:S(2)}, u32[]{:S(2)}) %collective-permute-start.1) | collective-permute-done | bytes 147488 | tf_op jit(solution)/shard_map/ppermute | solution.py:28
  24.3 8.3 %collective-permute-done.2.refs_2_ = f32[72,512]{1,0:T(8,128)S(1)} collective-permute-done((f32[72,512]{1,0:T(8,128)S(1)}, f32[72,512]{1,0:T(8,128)S(1)}, u32[]{:S(2)}, u32[]{:S(2)}) %collective-permute-start.2) | collective-permute-done | bytes 147488 | tf_op jit(solution)/shard_map/ppermute | solution.py:28
  32.7 6.4 %pull_net_pass.1 = (f32[4,32]{1,0:T(4,128)S(1)}, f32[4,32,128]{2,1,0:T(8,128)S(1)}, f32[4,32,128]{2,1,0:T(8,128)S(1)}, f32[4,32,128]{2,1,0:T(8,128)S(1)}, f32[4,32,128]{2,1,0:T(8,128)S(1)}) custom-call(s32[1]{0:T(128)} %bitcast.me_ref, bf16[128,512]{1,0:T(8,128)(2,1)S(1)} %get-tuple-element.19.state_ref, f32[4,128]{1,0:T(4,128)S(1)} %copy-done.6, ...), custom_call_target="tpu_custom_call" | custom-call | flops 2147483648 | bytes 2097152 | tf_op jit(solution)/shard_map/pull_net_pass/pallas_call | solution.py:252
  39.1 2.2 %collective-permute-start.4 = (f32[4,32,128]{2,1,0:T(8,128)S(1)}, f32[4,32,128]{2,1,0:T(8,128)S(1)}, u32[]{:S(2)}, u32[]{:S(2)}) collective-permute-start(f32[4,32,128]{2,1,0:T(8,128)S(1)} %get-tuple-element.22), channel_id=1, source_target_pairs={{0,4},{4,0},{8,12},{12,8},{1,5},{5,1},{9,13},{13,9},{2,6},{6,2},{1... | collective-permute-start | bytes 196616 | tf_op jit(solution)/shard_map/ppermute | solution.py:28
  41.3 1.1 %collective-permute-start.5 = (f32[4,32,128]{2,1,0:T(8,128)S(1)}, f32[4,32,128]{2,1,0:T(8,128)S(1)}, u32[]{:S(2)}, u32[]{:S(2)}) collective-permute-start(f32[4,32,128]{2,1,0:T(8,128)S(1)} %get-tuple-element.23), channel_id=1, source_target_pairs={{0,8},{4,12},{8,0},{12,4},{1,9},{5,13},{9,1},{13,5},{2,10},{6,14},... | collective-permute-start | bytes 196616 | tf_op jit(solution)/shard_map/ppermute | solution.py:28
  42.4 1.4 %collective-permute-start.6 = (f32[4,32,128]{2,1,0:T(8,128)S(1)}, f32[4,32,128]{2,1,0:T(8,128)S(1)}, u32[]{:S(2)}, u32[]{:S(2)}) collective-permute-start(f32[4,32,128]{2,1,0:T(8,128)S(1)} %get-tuple-element.24), channel_id=1, source_target_pairs={{0,12},{4,8},{8,4},{12,0},{1,13},{5,9},{9,5},{13,1},{2,14},{6,10},... | collective-permute-start | bytes 196616 | tf_op jit(solution)/shard_map/ppermute | solution.py:28
  43.8 0.3 collective-permute-done.4
  44.1 3.5 %collective-permute-done.5 = f32[4,32,128]{2,1,0:T(8,128)S(1)} collective-permute-done((f32[4,32,128]{2,1,0:T(8,128)S(1)}, f32[4,32,128]{2,1,0:T(8,128)S(1)}, u32[]{:S(2)}, u32[]{:S(2)}) %collective-permute-start.5) | collective-permute-done | bytes 65568 | tf_op jit(solution)/shard_map/ppermute | solution.py:28
  47.6 0.9 %collective-permute-done.6 = f32[4,32,128]{2,1,0:T(8,128)S(1)} collective-permute-done((f32[4,32,128]{2,1,0:T(8,128)S(1)}, f32[4,32,128]{2,1,0:T(8,128)S(1)}, u32[]{:S(2)}, u32[]{:S(2)}) %collective-permute-start.6) | collective-permute-done | bytes 65568 | tf_op jit(solution)/shard_map/ppermute | solution.py:28
  48.5 0.6 collective-permute-start.7
  49.1 3.2 %collective-permute-done.7 = f32[32,128]{1,0:T(8,128)S(1)} collective-permute-done((f32[32,128]{1,0:T(8,128)S(1)}, f32[32,128]{1,0:T(8,128)S(1)}, u32[]{:S(2)}, u32[]{:S(2)}) %collective-permute-start.7) | collective-permute-done | bytes 16416 | tf_op jit(solution)/shard_map/ppermute | solution.py:28
  52.4 0.1 collective-permute-start.8
  52.4 1.8 %collective-permute-start.10 = (f32[4,32,128]{2,1,0:T(8,128)S(1)}, f32[4,32,128]{2,1,0:T(8,128)S(1)}, u32[]{:S(2)}, u32[]{:S(2)}) collective-permute-start(f32[4,32,128]{2,1,0:T(8,128)S(1)} %multiply_add_fusion.refs_0_), channel_id=1, source_target_pairs={{0,8},{4,12},{8,0},{12,4},{1,9},{5,13},{9,1},{13,5},{2,10},{6,14},... | collective-permute-start | bytes 196616 | tf_op jit(solution)/shard_map/ppermute | solution.py:28
  54.3 1.7 %collective-permute-start.11 = (f32[4,32,128]{2,1,0:T(8,128)S(1)}, f32[4,32,128]{2,1,0:T(8,128)S(1)}, u32[]{:S(2)}, u32[]{:S(2)}) collective-permute-start(f32[4,32,128]{2,1,0:T(8,128)S(1)} %multiply_add_fusion.refs_0_), channel_id=1, source_target_pairs={{0,12},{4,8},{8,4},{12,0},{1,13},{5,9},{9,5},{13,1},{2,14},{6,10},... | collective-permute-start | bytes 196616 | tf_op jit(solution)/shard_map/ppermute | solution.py:28
  55.9 0.1 collective-permute-start.9
  56.0 0.6 add_multiply_fusion
  56.6 4.6 %collective-permute-done.10.refs_2_ = f32[4,32,128]{2,1,0:T(8,128)S(1)} collective-permute-done((f32[4,32,128]{2,1,0:T(8,128)S(1)}, f32[4,32,128]{2,1,0:T(8,128)S(1)}, u32[]{:S(2)}, u32[]{:S(2)}) %collective-permute-start.10) | collective-permute-done | bytes 65568 | tf_op jit(solution)/shard_map/ppermute | solution.py:28
  61.1 0.9 %collective-permute-done.9.refs_1_ = f32[4,32,128]{2,1,0:T(8,128)S(1)} collective-permute-done((f32[4,32,128]{2,1,0:T(8,128)S(1)}, f32[4,32,128]{2,1,0:T(8,128)S(1)}, u32[]{:S(2)}, u32[]{:S(2)}) %collective-permute-start.9) | collective-permute-done | bytes 65568 | tf_op jit(solution)/shard_map/ppermute | solution.py:28
  62.0 0.7 %place.1 = f32[4,128,128]{2,1,0:T(8,128)} custom-call(s32[1]{0:T(128)} %bitcast.me_ref, f32[4,32,128]{2,1,0:T(8,128)S(1)} %multiply_add_fusion.refs_0_, f32[4,32,128]{2,1,0:T(8,128)S(1)} %collective-permute-done.9.refs_1_, f32[4,32,128]{2,1,0:T(8,128)S(1)} %collective-permute-done.10.refs_2_, f32[4,32,128]{2,1,0:T(8,128)S(1)} %collective-permute-done.11.refs_3_), custom_call_target="tpu_custom_call" | custom-call | tf_op jit(solution)/shard_map/place/pallas_call | solution.py:335
  (25 shorter events, 0.1 us)
Async XLA Ops:
  0.6 10.2 %copy-start.8 = (f32[32]{0:T(128)S(1)}, f32[32]{0:T(128)}, u32[]{:S(2)}) copy-start(f32[32]{0:T(128)} %param.12) | copy-start | bytes 388
  0.6 10.2 %copy-start.7 = (f32[4,32]{1,0:T(4,128)S(1)}, f32[4,32]{1,0:T(4,128)}, u32[]{:S(2)}) copy-start(f32[4,32]{1,0:T(4,128)} %param.13) | copy-start | bytes 1540
  2.3 8.6 %collective-permute-start = (f32[128,128]{1,0:T(8,128)}, f32[128,128]{1,0:T(8,128)S(1)}, u32[]{:S(2)}, u32[]{:S(2)}) collective-permute-start(f32[128,128]{1,0:T(8,128)} %chain_pass.1), channel_id=1, source_target_pairs={{0,2},{2,0},{1,3},{3,1},{4,6},{6,4},{5,7},{7,5},{8,10},{10,8},{9,1... | collective-permute-start | bytes 196616 | tf_op jit(solution)/shard_map/ppermute | solution.py:28
  5.9 1.6 %copy-start = (bf16[128,8192]{1,0:T(8,128)(2,1)S(1)}, bf16[128,8192]{1,0:T(8,128)(2,1)}, u32[]{:S(2)}) copy-start(bf16[128,8192]{1,0:T(8,128)(2,1)} %d_ref.3) | copy-start | bytes 6291460
  7.4 0.9 %copy-start.2 = (f32[4,128,128]{2,1,0:T(8,128)S(1)}, f32[4,128,128]{2,1,0:T(8,128)}, u32[]{:S(2)}) copy-start(f32[4,128,128]{2,1,0:T(8,128)} %x_ref.3) | copy-start | bytes 786436
  8.4 0.8 %copy-start.3 = (f32[8192]{0:T(1024)S(1)}, f32[8192]{0:T(1024)}, u32[]{:S(2)}) copy-start(f32[8192]{0:T(1024)} %param.10) | copy-start | bytes 98308
  9.2 0.7 %copy-start.5 = (f32[4,128]{1,0:T(4,128)S(1)}, f32[4,128]{1,0:T(4,128)}, u32[]{:S(2)}) copy-start(f32[4,128]{1,0:T(4,128)} %rho_ref.5) | copy-start | bytes 6148
  10.9 21.8 %copy-start.1 = (bf16[128,8192]{1,0:T(8,128)(2,1)S(1)}, bf16[128,8192]{1,0:T(8,128)(2,1)}, u32[]{:S(2)}) copy-start(bf16[128,8192]{1,0:T(8,128)(2,1)} %d_ref.3) | copy-start | bytes 6291460
  10.9 21.8 %copy-start.4 = (f32[8192]{0:T(1024)S(1)}, f32[8192]{0:T(1024)}, u32[]{:S(2)}) copy-start(f32[8192]{0:T(1024)} %param.10) | copy-start | bytes 98308
  10.9 21.8 %copy-start.6 = (f32[4,128]{1,0:T(4,128)S(1)}, f32[4,128]{1,0:T(4,128)}, u32[]{:S(2)}) copy-start(f32[4,128]{1,0:T(4,128)} %rho_ref.5) | copy-start | bytes 6148
  17.1 7.2 %collective-permute-start.1 = (f32[72,512]{1,0:T(8,128)S(1)}, f32[72,512]{1,0:T(8,128)S(1)}, u32[]{:S(2)}, u32[]{:S(2)}) collective-permute-start(f32[72,512]{1,0:T(8,128)S(1)} %get-tuple-element.20.refs_0_), channel_id=1, source_target_pairs={{0,4},{4,0},{8,12},{12,8},{1,5},{5,1},{9,13},{13,9},{2,6},{6,2},{1... | collective-permute-start | bytes 442376 | tf_op jit(solution)/shard_map/ppermute | solution.py:28
  18.8 13.9 %collective-permute-start.2 = (f32[72,512]{1,0:T(8,128)S(1)}, f32[72,512]{1,0:T(8,128)S(1)}, u32[]{:S(2)}, u32[]{:S(2)}) collective-permute-start(f32[72,512]{1,0:T(8,128)S(1)} %get-tuple-element.20.refs_0_), channel_id=1, source_target_pairs={{0,8},{4,12},{8,0},{12,4},{1,9},{5,13},{9,1},{13,5},{2,10},{6,14},... | collective-permute-start | bytes 442376 | tf_op jit(solution)/shard_map/ppermute | solution.py:28
  21.4 11.3 %collective-permute-start.3 = (f32[72,512]{1,0:T(8,128)S(1)}, f32[72,512]{1,0:T(8,128)S(1)}, u32[]{:S(2)}, u32[]{:S(2)}) collective-permute-start(f32[72,512]{1,0:T(8,128)S(1)} %get-tuple-element.20.refs_0_), channel_id=1, source_target_pairs={{0,12},{4,8},{8,4},{12,0},{1,13},{5,9},{9,5},{13,1},{2,14},{6,10},... | collective-permute-start | bytes 442376 | tf_op jit(solution)/shard_map/ppermute | solution.py:28
  39.1 5.0 %collective-permute-start.4 = (f32[4,32,128]{2,1,0:T(8,128)S(1)}, f32[4,32,128]{2,1,0:T(8,128)S(1)}, u32[]{:S(2)}, u32[]{:S(2)}) collective-permute-start(f32[4,32,128]{2,1,0:T(8,128)S(1)} %get-tuple-element.22), channel_id=1, source_target_pairs={{0,4},{4,0},{8,12},{12,8},{1,5},{5,1},{9,13},{13,9},{2,6},{6,2},{1... | collective-permute-start | bytes 196616 | tf_op jit(solution)/shard_map/ppermute | solution.py:28
  41.3 6.3 %collective-permute-start.5 = (f32[4,32,128]{2,1,0:T(8,128)S(1)}, f32[4,32,128]{2,1,0:T(8,128)S(1)}, u32[]{:S(2)}, u32[]{:S(2)}) collective-permute-start(f32[4,32,128]{2,1,0:T(8,128)S(1)} %get-tuple-element.23), channel_id=1, source_target_pairs={{0,8},{4,12},{8,0},{12,4},{1,9},{5,13},{9,1},{13,5},{2,10},{6,14},... | collective-permute-start | bytes 196616 | tf_op jit(solution)/shard_map/ppermute | solution.py:28
  42.4 6.1 %collective-permute-start.6 = (f32[4,32,128]{2,1,0:T(8,128)S(1)}, f32[4,32,128]{2,1,0:T(8,128)S(1)}, u32[]{:S(2)}, u32[]{:S(2)}) collective-permute-start(f32[4,32,128]{2,1,0:T(8,128)S(1)} %get-tuple-element.24), channel_id=1, source_target_pairs={{0,12},{4,8},{8,4},{12,0},{1,13},{5,9},{9,5},{13,1},{2,14},{6,10},... | collective-permute-start | bytes 196616 | tf_op jit(solution)/shard_map/ppermute | solution.py:28
  48.5 3.8 %collective-permute-start.7 = (f32[32,128]{1,0:T(8,128)S(1)}, f32[32,128]{1,0:T(8,128)S(1)}, u32[]{:S(2)}, u32[]{:S(2)}) collective-permute-start(f32[32,128]{1,0:T(8,128)S(1)} %fusion), channel_id=1, source_target_pairs={{0,2},{2,0},{1,3},{3,1},{4,6},{6,4},{5,7},{7,5},{8,10},{10,8},{9,1... | collective-permute-start | bytes 49160 | tf_op jit(solution)/shard_map/ppermute | solution.py:28
  52.4 3.6 %collective-permute-start.8 = (f32[4,32]{1,0:T(4,128)S(1)}, f32[4,32]{1,0:T(4,128)S(1)}, u32[]{:S(2)}, u32[]{:S(2)}) collective-permute-start(f32[4,32]{1,0:T(4,128)S(1)} %get-tuple-element.26), channel_id=1, source_target_pairs={{0,1},{1,0},{2,3},{3,2},{4,5},{5,4},{6,7},{7,6},{8,9},{9,8},{10,11... | collective-permute-start | bytes 1544 | tf_op jit(solution)/shard_map/ppermute | solution.py:28
  52.4 8.7 %collective-permute-start.10 = (f32[4,32,128]{2,1,0:T(8,128)S(1)}, f32[4,32,128]{2,1,0:T(8,128)S(1)}, u32[]{:S(2)}, u32[]{:S(2)}) collective-permute-start(f32[4,32,128]{2,1,0:T(8,128)S(1)} %multiply_add_fusion.refs_0_), channel_id=1, source_target_pairs={{0,8},{4,12},{8,0},{12,4},{1,9},{5,13},{9,1},{13,5},{2,10},{6,14},... | collective-permute-start | bytes 196616 | tf_op jit(solution)/shard_map/ppermute | solution.py:28
  54.3 6.9 %collective-permute-start.11 = (f32[4,32,128]{2,1,0:T(8,128)S(1)}, f32[4,32,128]{2,1,0:T(8,128)S(1)}, u32[]{:S(2)}, u32[]{:S(2)}) collective-permute-start(f32[4,32,128]{2,1,0:T(8,128)S(1)} %multiply_add_fusion.refs_0_), channel_id=1, source_target_pairs={{0,12},{4,8},{8,4},{12,0},{1,13},{5,9},{9,5},{13,1},{2,14},{6,10},... | collective-permute-start | bytes 196616 | tf_op jit(solution)/shard_map/ppermute | solution.py:28
  55.9 6.1 %collective-permute-start.9 = (f32[4,32,128]{2,1,0:T(8,128)S(1)}, f32[4,32,128]{2,1,0:T(8,128)S(1)}, u32[]{:S(2)}, u32[]{:S(2)}) collective-permute-start(f32[4,32,128]{2,1,0:T(8,128)S(1)} %multiply_add_fusion.refs_0_), channel_id=1, source_target_pairs={{0,4},{4,0},{8,12},{12,8},{1,5},{5,1},{9,13},{13,9},{2,6},{6,2},{1... | collective-permute-start | bytes 196616 | tf_op jit(solution)/shard_map/ppermute | solution.py:28

commit v3 on v2

v3 whole, which is shorter than its diff:
```python
import functools

import jax
import jax.numpy as jnp
from jax import lax
from jax.experimental import pallas as pl
from jax.experimental.pallas import tpu as pltpu
from jax.sharding import PartitionSpec as P

block_width = 128
highest = lax.Precision.HIGHEST
f32 = jnp.float32
bf16 = jnp.bfloat16


def swap(value, axes, sizes, flips):
    count = 1
    for size in sizes:
        count *= size
    pairs = []
    for flat in range(count):
        rest, target, scale = flat, 0, 1
        for size, flip in zip(reversed(sizes), reversed(flips)):
            target += ((rest % size) ^ flip) * scale
            rest //= size
            scale *= size
        pairs.append((flat, target))
    return lax.ppermute(value, axes, pairs)


def entering(value, axis, combine, identity, reverse):
    length, index = (lax.axis_size(axis), lax.axis_index(axis))
    everything = jax.tree.map(lambda part: lax.all_gather(part, axis), value)
    before = jax.tree.map(
        lambda part, zero: jnp.broadcast_to(jnp.asarray(zero, part.dtype), part.shape),
        value,
        identity,
    )
    for k in range(length):
        at = length - 1 - k if reverse else k
        reached = at > index if reverse else at < index
        new = combine(before, jax.tree.map(lambda part: part[at], everything))
        before = jax.tree.map(lambda a, b: jnp.where(reached, a, b), new, before)
    return before


def compose(earlier, later):
    return (later[0] * earlier[0], later[0] * earlier[1] + later[1])


def softplus(v):
    return jnp.maximum(v, jnp.log(1.0 + jnp.exp(jnp.minimum(v, 80.0))))


def far_copy(*parts):
    return [pltpu.with_memory_space_constraint(part, pltpu.HBM) for part in parts]


def chain_kernel(x_hbm, rho_hbm, carried_ref, x_ref, rho_ref, sems):
    dates = x_ref.shape[0]
    copies = [pltpu.make_async_copy(x_hbm.at[t], x_ref.at[t], sems.at[t]) for t in range(dates)]
    copies.append(pltpu.make_async_copy(rho_hbm, rho_ref, sems.at[dates]))
    for copy in copies:
        copy.start()
    copies[dates].wait()
    copies[0].wait()
    carried = x_ref[0]
    for t in range(1, dates):
        copies[t].wait()
        carried = rho_ref[t : t + 1, :] * carried + x_ref[t]
    carried_ref[...] = carried


def chain_pass(x, rho):
    return pl.pallas_call(
        chain_kernel,
        in_specs=[pl.BlockSpec(memory_space=pltpu.HBM)] * 2,
        out_specs=[pl.BlockSpec(memory_space=pltpu.VMEM)] * 3,
        out_shape=[
            jax.ShapeDtypeStruct(x.shape[1:], f32),
            jax.ShapeDtypeStruct(x.shape, f32),
            jax.ShapeDtypeStruct(rho.shape, f32),
        ],
        scratch_shapes=[pltpu.SemaphoreType.DMA((x.shape[0] + 1,))],
        compiler_params=pltpu.CompilerParams(vmem_limit_bytes=4 << 20),
        name="chain_pass",
    )(*far_copy(x, rho))


def prepare_kernel(step, d_hbm, n_hbm, mass_hbm, ceiling_hbm, obligor_hbm, *refs):
    turned_ref, n_ref, facts_ref, d_ref, mass_ref, ceiling_ref, obligor_ref, sems = refs
    pieces = d_ref.shape[1] // step
    copies = []
    for c in range(pieces):
        part = pl.ds(c * step, step)
        copies.append(pltpu.make_async_copy(d_hbm.at[:, part], d_ref.at[:, part], sems.at[c]))
    small = ((n_hbm, n_ref), (mass_hbm, mass_ref), (ceiling_hbm, ceiling_ref), (obligor_hbm, obligor_ref))
    for k, (source, target) in enumerate(small):
        copies.append(pltpu.make_async_copy(source, target, sems.at[pieces + k]))
    for copy in copies:
        copy.start()
    for c in range(pieces):
        copies[c].wait()
        turned_ref[c * step : (c + 1) * step, :] = d_ref[:, c * step : (c + 1) * step].T
    for copy in copies[pieces:]:
        copy.wait()
    dates, cpties = mass_ref.shape
    facts_ref[...] = jnp.zeros_like(facts_ref)
    facts_ref[:dates, :cpties] = mass_ref[...]
    facts_ref[dates : dates + 1, :cpties] = ceiling_ref[...]
    facts_ref[dates + 1 : dates + 2, : obligor_ref.shape[1]] = obligor_ref[...].astype(f32)


def prepare_pass(d, n, mass, ceiling, obligor):
    factors, trades = d.shape
    step = min(2048, trades)
    hbm = pl.BlockSpec(memory_space=pltpu.HBM)
    vmem = pl.BlockSpec(memory_space=pltpu.VMEM)
    ceiling, obligor = ceiling[None, :], obligor[None, :]
    return pl.pallas_call(
        functools.partial(prepare_kernel, step),
        in_specs=[hbm] * 5,
        out_specs=[vmem] * 3,
        out_shape=[
            jax.ShapeDtypeStruct((trades, factors), bf16),
            jax.ShapeDtypeStruct(n.shape, f32),
            jax.ShapeDtypeStruct((8, 128), f32),
        ],
        scratch_shapes=[
            pltpu.VMEM(d.shape, bf16),
            pltpu.VMEM(mass.shape, f32),
            pltpu.VMEM(ceiling.shape, f32),
            pltpu.VMEM(obligor.shape, jnp.int32),
            pltpu.SemaphoreType.DMA((trades // step + 4,)),
        ],
        compiler_params=pltpu.CompilerParams(vmem_limit_bytes=8 << 20),
        cost_estimate=pl.CostEstimate(flops=0, bytes_accessed=4 * trades * factors, transcendentals=0),
        name="prepare_pass",
    )(*far_copy(d, n, mass, ceiling, obligor))


def state_stage(x_ref, rho_ref, arriving_ref, keep_ref, state_refs):
    dates, paths, _ = x_ref.shape
    columns = [(ref, at) for ref in state_refs[::-1] for at in range(0, ref.shape[1], paths)]
    carried = arriving_ref[...] * keep_ref[0].astype(f32)
    for t, (ref, at) in enumerate(columns):
        carried = rho_ref[t : t + 1, :] * carried + x_ref[t]
        ref[:, at : at + paths] = carried.T.astype(bf16)


def sum_stage(step, state_ref, turned_ref, n_ref, sums_ref):
    blocks = step // block_width

    @pl.loop(0, turned_ref.shape[0] // step)
    def _(c):
        size_t = n_ref[pl.ds(pl.multiple_of(c * blocks, blocks), blocks), :].T
        turned = turned_ref[pl.ds(pl.multiple_of(c * step, step), step), :]
        linear = jnp.dot(turned, state_ref[...], preferred_element_type=f32)
        lines = []
        for b in range(blocks):
            value = softplus(linear[b * block_width : (b + 1) * block_width]) * size_t[:, b : b + 1]
            lines.append(jnp.sum(value, axis=0, keepdims=True))
        sums_ref[pl.ds(pl.multiple_of(c * blocks, blocks), blocks), :] = jnp.concatenate(lines, axis=0)


def first_value_kernel(step, x_ref, rho_ref, arriving_ref, keep_ref, facts_ref, turned_ref, n_ref, sums_ref, *state_refs):
    state_stage(x_ref, rho_ref, arriving_ref, keep_ref, state_refs)
    total = n_ref.shape[0]
    sums_ref[total:, :128] = facts_ref[...]
    sum_stage(step, state_refs[0], turned_ref, n_ref, sums_ref)


def value_cost(rows, trades, factors):
    return pl.CostEstimate(
        flops=2 * rows * trades * factors, bytes_accessed=2 * trades * factors, transcendentals=2 * rows * trades
    )


def first_value_pass(groups, x, rho, arriving, keep, facts, turned, n):
    dates, paths, factors = x.shape
    trades = turned.shape[0]
    rows = dates // groups * paths
    vmem = pl.BlockSpec(memory_space=pltpu.VMEM)
    out = pl.pallas_call(
        functools.partial(first_value_kernel, min(2048, trades)),
        in_specs=[vmem, vmem, vmem, pl.BlockSpec(memory_space=pltpu.SMEM), vmem, vmem, vmem],
        out_specs=[vmem] * (1 + groups),
        out_shape=[jax.ShapeDtypeStruct((n.shape[0] + 8, rows), f32)]
        + [jax.ShapeDtypeStruct((factors, rows), bf16)] * groups,
        compiler_params=pltpu.CompilerParams(vmem_limit_bytes=24 << 20),
        cost_estimate=value_cost(rows, trades, factors),
        name="first_value_pass",
    )(x, rho, arriving, keep, facts, turned, n)
    return out[0], out[1:]


def value_pass(state, turned, n):
    factors, rows = state.shape
    trades = turned.shape[0]
    vmem = pl.BlockSpec(memory_space=pltpu.VMEM)
    return pl.pallas_call(
        functools.partial(sum_stage, min(2048, trades)),
        in_specs=[vmem] * 3,
        out_specs=vmem,
        out_shape=jax.ShapeDtypeStruct((n.shape[0], rows), f32),
        compiler_params=pltpu.CompilerParams(vmem_limit_bytes=24 << 20),
        cost_estimate=value_cost(rows, trades, factors),
        name="value_pass",
    )(state, turned, n)


def split_dot(selector, value):
    selector = selector.astype(bf16)
    high = value.astype(bf16)
    rest = value - high.astype(f32)
    middle = rest.astype(bf16)
    low = (rest - middle.astype(f32)).astype(bf16)
    dot = functools.partial(jnp.dot, selector, preferred_element_type=f32)
    return dot(low) + dot(middle) + dot(high)


def net_stage(cpty_dev, dates, first, me, sums, facts, upstream_ref):
    shards = len(sums)
    blocks, rows = upstream_ref.shape
    count = rows // 128
    cpties = shards * cpty_dev
    shift = cpty_dev.bit_length() - 1

    def label(owner):
        owner = owner.astype(jnp.int32)
        return (((owner >> shift) ^ me) << shift) + (owner & (cpty_dev - 1))

    columns = [facts[k].T for k in range(shards)]
    netted = None
    for k in range(shards):
        row = label(facts[k][dates + 1 : dates + 2, :blocks])
        pick = lax.broadcasted_iota(jnp.int32, (cpties, blocks), 0) == row
        part = split_dot(jnp.where(pick, 1.0, 0.0), sums[k][:blocks])
        netted = part if netted is None else netted + part
    column = label(columns[0][:blocks, dates + 1 : dates + 2])
    own = jnp.where(lax.broadcasted_iota(jnp.int32, (blocks, cpties), 1) == column, 1.0, 0.0)
    adjoint, totals = [], []
    for k in range(shards):
        shifted = netted[k * cpty_dev : (k + 1) * cpty_dev] - columns[k][:cpty_dev, dates : dates + 1]
        slope = 0.5 * jnp.tanh(0.5 * shifted) + 0.5
        parts = []
        for t in range(count):
            mass = columns[k][:cpty_dev, first + t : first + t + 1]
            parts.append(slope[:, t * 128 : (t + 1) * 128] * mass)
        adjoint.append(jnp.concatenate(parts, axis=1))
        if k == 0:
            exposed = softplus(shifted)
            for t in range(count):
                totals.append(jnp.sum(exposed[:, t * 128 : (t + 1) * 128], axis=1, keepdims=True))
    upstream_ref[...] = split_dot(own, jnp.concatenate(adjoint, axis=0))
    return totals


def pull_stage(step, state_ref, turned_ref, d_ref, n_ref, upstream_ref, half_ref, total_ref):
    blocks = step // block_width
    half_ref[...] = state_ref[...] * 0.5
    total_ref[...] = jnp.zeros_like(total_ref)

    @pl.loop(0, d_ref.shape[1] // step)
    def _(c):
        lines = pl.ds(pl.multiple_of(c * blocks, blocks), blocks)
        trades = pl.ds(pl.multiple_of(c * step, step), step)
        size_t = 0.5 * n_ref[lines, :].T
        upstream = upstream_ref[lines, :]
        linear = jnp.dot(turned_ref[trades, :], half_ref[...], preferred_element_type=f32)
        parts = []
        for b in range(blocks):
            slope = jnp.tanh(linear[b * block_width : (b + 1) * block_width])
            size = size_t[:, b : b + 1]
            parts.append(((slope * size + size) * upstream[b : b + 1, :]).astype(bf16))
        total_ref[...] += jnp.dot(d_ref[:, trades], jnp.concatenate(parts, axis=0), preferred_element_type=f32)


def write_table(table_ref, totals, first):
    lane = lax.broadcasted_iota(jnp.int32, (totals[0].shape[0], 128), 1)
    table = jnp.zeros(lane.shape, f32)
    for t, total in enumerate(totals):
        table = jnp.where(lane == t, total, table)
    table_ref[first : first + len(totals), :] = table.T[: len(totals)]


def late_pull_kernel(step, shards, cpty_dev, dates, first, me_ref, state_ref, turned_ref, d_ref, n_ref, *refs):
    sums, refs = refs[:shards], refs[shards:]
    exposure_ref, facts_ref, direct_ref, upstream_ref, half_ref, total_ref = refs
    blocks = n_ref.shape[0]
    facts = [part[blocks : blocks + 8, :128] for part in sums]
    for k in range(shards):
        facts_ref[8 * k : 8 * (k + 1), :] = facts[k]
    totals = net_stage(cpty_dev, dates, first, me_ref[0], sums, facts, upstream_ref)
    write_table(exposure_ref, totals, 0)
    pull_stage(step, state_ref, turned_ref, d_ref, n_ref, upstream_ref, half_ref, total_ref)
    paths = direct_ref.shape[1]
    for t in range(direct_ref.shape[0]):
        direct_ref[t] = total_ref[:, t * paths : (t + 1) * paths].T


def early_pull_kernel(step, shards, cpty_dev, me_ref, state_ref, turned_ref, d_ref, n_ref, rho_ref, facts_ref, late_exposure_ref, late_ref, *refs):
    sums, refs = refs[:shards], refs[shards:]
    exposure_ref, refs = refs[0], refs[1:]
    chain, refs = refs[:shards], refs[shards:]
    upstream_ref, half_ref, total_ref, chained_ref = refs
    dates, paths, factors = chained_ref.shape
    early = dates - late_ref.shape[0]
    me = me_ref[0]
    facts = [facts_ref[8 * k : 8 * (k + 1), :] for k in range(shards)]
    totals = net_stage(cpty_dev, dates, 0, me, sums, facts, upstream_ref)
    write_table(exposure_ref, totals, 0)
    exposure_ref[early:dates, :] = late_exposure_ref[...]
    pull_stage(step, state_ref, turned_ref, d_ref, n_ref, upstream_ref, half_ref, total_ref)
    carried = jnp.zeros((paths, factors), f32)
    for t in reversed(range(dates)):
        direct = late_ref[t - early] if t >= early else total_ref[:, t * paths : (t + 1) * paths].T
        adjoint = direct + carried
        chained_ref[t] = adjoint
        carried = rho_ref[t : t + 1, :] * adjoint
    piece = paths // shards
    for k in range(shards):
        at = pl.ds(pl.multiple_of((me ^ k) * piece, piece), piece)
        chain[k][...] = chained_ref[:, at, :]


def pull_cost(rows, trades, factors):
    return pl.CostEstimate(
        flops=4 * rows * trades * factors, bytes_accessed=4 * trades * factors, transcendentals=rows * trades
    )


def pull_scratch(blocks, factors, rows):
    return [pltpu.VMEM((blocks, rows), f32), pltpu.VMEM((factors, rows), bf16), pltpu.VMEM((factors, rows), f32)]


def late_pull_pass(dates, paths, cpty_dev, me, state, turned, d, n, sums):
    factors, rows = state.shape
    trades = d.shape[1]
    shards = len(sums)
    count = rows // paths
    vmem = pl.BlockSpec(memory_space=pltpu.VMEM)
    return pl.pallas_call(
        functools.partial(late_pull_kernel, min(2048, trades), shards, cpty_dev, dates, dates - count),
        in_specs=[pl.BlockSpec(memory_space=pltpu.SMEM)] + [vmem] * (4 + shards),
        out_specs=[vmem] * 3,
        out_shape=[
            jax.ShapeDtypeStruct((count, cpty_dev), f32),
            jax.ShapeDtypeStruct((8 * shards, 128), f32),
            jax.ShapeDtypeStruct((count, paths, factors), f32),
        ],
        scratch_shapes=pull_scratch(n.shape[0], factors, rows),
        compiler_params=pltpu.CompilerParams(vmem_limit_bytes=24 << 20),
        cost_estimate=pull_cost(rows, trades, factors),
        name="late_pull_pass",
    )(me, state, turned, d, n, *sums)


def early_pull_pass(dates, paths, cpty_dev, me, state, turned, d, n, rho, facts, late_exposure, late, sums):
    factors, rows = state.shape
    trades = d.shape[1]
    shards = len(sums)
    piece = paths // shards
    vmem = pl.BlockSpec(memory_space=pltpu.VMEM)
    out = pl.pallas_call(
        functools.partial(early_pull_kernel, min(2048, trades), shards, cpty_dev),
        in_specs=[pl.BlockSpec(memory_space=pltpu.SMEM)] + [vmem] * (8 + shards),
        out_specs=[vmem] * (1 + shards),
        out_shape=[jax.ShapeDtypeStruct((dates, cpty_dev), f32)]
        + [jax.ShapeDtypeStruct((dates, piece, factors), f32)] * shards,
        scratch_shapes=pull_scratch(n.shape[0], factors, rows) + [pltpu.VMEM((dates, paths, factors), f32)],
        compiler_params=pltpu.CompilerParams(vmem_limit_bytes=24 << 20),
        cost_estimate=pull_cost(rows, trades, factors),
        name="early_pull_pass",
    )(me, state, turned, d, n, rho, facts, late_exposure, late, *sums)
    return out[0], out[1:]


def pull_kernel(step, state_ref, turned_ref, d_ref, n_ref, upstream_ref, direct_ref, half_ref, total_ref):
    pull_stage(step, state_ref, turned_ref, d_ref, n_ref, upstream_ref, half_ref, total_ref)
    dates, paths, _ = direct_ref.shape
    for t in range(dates):
        direct_ref[t] = total_ref[:, t * paths : (t + 1) * paths].T


def pull_pass(dates, state, turned, d, n, upstream):
    factors, rows = state.shape
    trades = d.shape[1]
    vmem = pl.BlockSpec(memory_space=pltpu.VMEM)
    return pl.pallas_call(
        functools.partial(pull_kernel, min(2048, trades)),
        in_specs=[vmem] * 5,
        out_specs=vmem,
        out_shape=jax.ShapeDtypeStruct((dates, rows // dates, factors), f32),
        scratch_shapes=pull_scratch(n.shape[0], factors, rows)[1:],
        compiler_params=pltpu.CompilerParams(vmem_limit_bytes=32 << 20),
        name="pull_pass",
    )(state, turned, d, n, upstream)


def place_kernel(shards, me_ref, *refs):
    pieces, out_ref = refs[:shards], refs[shards]
    size = pieces[0].shape[1]
    for k in range(shards):
        at = pl.ds(pl.multiple_of((me_ref[0] ^ k) * size, size), size)
        out_ref[:, at, :] = pieces[k][...]


def place(me, pieces):
    shards = len(pieces)
    dates, size, factors = pieces[0].shape
    whole = lambda *shape: pl.BlockSpec(shape, lambda i, s: (0,) * len(shape))
    return pl.pallas_call(
        functools.partial(place_kernel, shards),
        grid_spec=pltpu.PrefetchScalarGridSpec(
            num_scalar_prefetch=1,
            grid=(1,),
            in_specs=[whole(dates, size, factors)] * shards,
            out_specs=whole(dates, shards * size, factors),
        ),
        out_shape=jax.ShapeDtypeStruct((dates, shards * size, factors), f32),
        compiler_params=pltpu.CompilerParams(vmem_limit_bytes=4 << 20),
        name="place",
    )(me, *pieces)


def local_chain(x, rho):
    carried = x[0]
    gain = rho[0]
    for t in range(1, x.shape[0]):
        carried = rho[t][None, :] * carried + x[t]
        gain = rho[t] * gain
    return gain, carried


def near(x, rho, d, size, obligor, ceiling, mass):
    dates, paths, factors = x.shape
    shards = lax.axis_size("trade")
    cpty_dev = ceiling.shape[0]
    n = size.reshape(-1, block_width)
    me = lax.axis_index("trade").astype(jnp.int32)[None]
    date = lax.axis_index("date").astype(jnp.int32)
    over = lambda value, k: swap(value, ("trade",), (shards,), (k,))

    carried, x, rho_near = chain_pass(x, rho)
    arriving = swap(carried, ("date",), (2,), (1,))
    turned, n, facts = prepare_pass(d, n, mass, ceiling, obligor)
    sums, (late_state, early_state) = first_value_pass(2, x, rho_near, arriving, date[None], facts, turned, n)
    late_sums = [sums] + [over(sums, k) for k in range(1, shards)]
    sums = value_pass(early_state, turned, n)
    early_sums = [sums] + [over(sums, k) for k in range(1, shards)]
    exposure, facts, late = late_pull_pass(dates, paths, cpty_dev, me, late_state, turned, d, n, late_sums)
    exposure, chain = early_pull_pass(
        dates, paths, cpty_dev, me, early_state, turned, d, n, rho_near, facts, exposure, late, early_sums
    )
    total = functools.reduce(jnp.add, [chain[0]] + [over(chain[k], k) for k in range(1, shards)])

    message = swap(rho[0][None, :] * total[0], ("date",), (2,), (1,))
    weights = [jnp.where(date > 0, 0.0, jnp.ones((factors,), f32))]
    for t in reversed(range(1, dates)):
        weights.append(rho[t] * weights[-1])
    own = total + jnp.stack(weights[::-1])[:, None, :] * message[None]
    own, exposure = lax.optimization_barrier((own, exposure))
    pieces = [own] + [over(own, k) for k in range(1, shards)]
    exposure_profile = (exposure + swap(exposure, ("path",), (2,), (1,))) / (paths * lax.axis_size("path"))
    return exposure_profile, place(me, pieces)


def far(x, rho, d, size, obligor, ceiling, mass):
    dates, paths, factors = x.shape
    rows = dates * paths
    cpty_dev = ceiling.shape[0]
    n = size.reshape(-1, block_width)
    value = local_chain(x, rho)
    identity = (jnp.ones_like(value[0]), jnp.zeros_like(value[1]))
    _, arriving = entering(value, "date", compose, identity, False)
    turned, n, facts = prepare_pass(d, n, mass, ceiling, obligor)
    sums, (state,) = first_value_pass(1, x, rho, arriving, jnp.ones((1,), jnp.int32), facts, turned, n)
    sums = sums[: n.shape[0]]
    cpties = cpty_dev * lax.axis_size("trade")
    ownership = (obligor[:, None] == jnp.arange(cpties, dtype=jnp.int32)[None, :]).astype(f32)
    partial = lax.dot_general(ownership, sums, (((0,), (0,)), ((), ())), precision=highest)
    netted = lax.psum_scatter(partial, "trade", scatter_dimension=0, tiled=True)
    shifted = (netted - ceiling[:, None]).reshape(cpty_dev, dates, paths)
    exposure = jnp.sum(jax.nn.softplus(shifted), axis=2).T
    exposure_profile = lax.psum(exposure, "path") / (paths * lax.axis_size("path"))
    adjoint = (mass.T[:, :, None] * jax.nn.sigmoid(shifted)).reshape(cpty_dev, rows)
    gathered = lax.all_gather(adjoint, "trade", axis=0, tiled=True)
    upstream = jnp.dot(ownership, gathered, precision=highest)
    direct = lax.psum(pull_pass(dates, state, turned, d, n, upstream), "trade")

    gain = jnp.ones((factors,), f32)
    message = jnp.zeros((paths, factors), f32)
    for t in reversed(range(dates)):
        message = rho[t][None, :] * (direct[t] + message)
        gain = rho[t] * gain
    _, message = entering((gain, message), "date", compose, identity, True)
    adjoints = []
    for t in reversed(range(dates)):
        adjoint = direct[t] + message
        adjoints.append(adjoint)
        message = rho[t][None, :] * adjoint
    return exposure_profile, jnp.stack(adjoints[::-1])


def solution(mesh):
    close = mesh.shape["date"] == 2 and mesh.shape["trade"] == 4 and mesh.shape["path"] == 2
    return jax.shard_map(
        near if close else far,
        mesh=mesh,
        in_specs=(
            P(("grp", "date"), "path", None),
            P(("grp", "date"), None),
            P(None, ("grp", "trade")),
            P(("grp", "trade")),
            P(("grp", "trade")),
            P(("grp", "trade")),
            P(("grp", "date"), "trade"),
        ),
        out_specs=(P(("grp", "date"), "trade"), P(("grp", "date"), "path", None)),
        check_vma=False,
    )
```

time: 63 us -> 55.3 us (0.88)
  waiting for transfers between devices: 24.5 us -> 12.4 us
  starting transfers between devices: 16.3 us -> 22.7 us
  local copies, waits for them, and re-layouts: 4.01 us -> 0.01 us
  Pallas kernels: 15.9 us -> 18.6 us
  other arithmetic: 1.3 us -> 0.63 us
    ppermute x12 -> x15, waiting for transfers between devices: 24.5 us -> 12.4 us  [swap(): return lax.ppermute(value, axes, pairs)]
    ppermute x12 -> x15, starting transfers between devices: 16.3 us -> 22.7 us  [swap(): return lax.ppermute(value, axes, pairs)]
    unnamed x18 -> x4, local copies, waits for them, and re-layouts: 4.01 us -> 0.01 us
    pallas_call x4 -> x6, Pallas kernels: 15.2 us -> 17.8 us  [the longest x1 4.11 us: early_pull_pass(): pl.pallas_call(functools.partial(early_pull_kernel, min(2048, trades), sh...]
    broadcast_in_dim x1 -> x0, other arithmetic: 0.66 us -> none  [near(): obligor.astype(f32)[None, :]]
  transfers between devices with their start and end apart: 12 -> 15, of which waited for: 8 -> 7; matrix products, arithmetic and copies ran while one was open for 2% -> 1% of each run, Pallas kernels for 2% -> 17%
where the time goes in v3:
time: 55.3 us; the launch traced here: 55.1 us
  starting transfers between devices  22.7 us (41%)
  Pallas kernels  18.6 us (34%)
  waiting for transfers between devices  12.4 us (22%)
  between operations  0.76 us (1%)
  other arithmetic  0.63 us (1%)
    ppermute x15, starting transfers between devices, swap(): return lax.ppermute(value, axes, pairs)  22.7 us
    ppermute x15, waiting for transfers between devices, swap(): return lax.ppermute(value, axes, pairs)  12.4 us
    pallas_call x1, Pallas kernels, early_pull_pass(): pl.pallas_call(functools.partial(early_pull_kernel, min(2048, trades), sh...  4.11 us
    pallas_call x1, Pallas kernels, late_pull_pass(): pl.pallas_call(functools.partial(late_pull_kernel, min(2048, trades), sha...  4.09 us
    pallas_call x1, Pallas kernels, first_value_pass(): pl.pallas_call(functools.partial(first_value_kernel, min(2048, trades)),...  3.44 us
    pallas_call x1, Pallas kernels, value_pass(): pl.pallas_call(functools.partial(sum_stage, min(2048, trades)), in_specs=...  3.31 us
    pallas_call x1, Pallas kernels, prepare_pass(): pl.pallas_call(functools.partial(prepare_kernel, step), in_specs=[hbm] *...  1.89 us
  transfers between devices with their start and end apart: 15, of which 7 were waited for; matrix products, arithmetic and copies ran while one was open for 1% of the time, Pallas kernels for 17%

profile of v3, /device:TPU:0, one launch (start us, length us, event | category | flops | bytes accessed | tf_op | source)
XLA Modules:
  0.0 55.1 jit_solution(12028600359814150051)
XLA Ops:
  0.6 1.0 %chain_pass.1 = (f32[128,128]{1,0:T(8,128)S(1)}, f32[4,128,128]{2,1,0:T(8,128)S(1)}, f32[4,128]{1,0:T(4,128)S(1)}) custom-call(f32[4,128,128]{2,1,0:T(8,128)} %x_hbm.1, f32[4,128]{1,0:T(4,128)} %rho_hbm.1), custom_call_target="tpu_custom_call" | custom-call | tf_op jit(solution)/shard_map/chain_pass/pallas_call | solution.py:75
  1.6 3.0 %collective-permute-start = (f32[128,128]{1,0:T(8,128)S(1)}, f32[128,128]{1,0:T(8,128)S(1)}, u32[]{:S(2)}, u32[]{:S(2)}) collective-permute-start(f32[128,128]{1,0:T(8,128)S(1)} %get-tuple-element.23), channel_id=1, source_target_pairs={{0,2},{2,0},{1,3},{3,1},{4,6},{6,4},{5,7},{7,5},{8,10},{10,8},{9,1... | collective-permute-start | bytes 196616 | tf_op jit(solution)/shard_map/ppermute | solution.py:28
  4.6 1.9 %prepare_pass.1 = (bf16[8192,128]{1,0:T(8,128)(2,1)S(1)}, f32[64,128]{1,0:T(8,128)S(1)}, f32[8,128]{1,0:T(8,128)S(1)}) custom-call(bf16[128,8192]{1,0:T(8,128)(2,1)} %d_ref.3, f32[64,128]{1,0:T(8,128)} %bitcast.11, f32[4,32]{1,0:T(4,128)} %mass_hbm.1, f32[1,32]{1,0:T(1,128)} %bitcast.12, s32[1,64]{1,0:T(1,128)} %bitcast.13), custom_call_target="tpu_custom_call" | custom-call | bytes 4194304 | tf_op jit(solution)/shard_map/prepare_pass/pallas_call | solution.py:120
  6.5 0.4 collective-permute-done.arriving_ref
  6.9 3.4 %first_value_pass.1 = (f32[72,256]{1,0:T(8,128)S(1)}, bf16[128,256]{1,0:T(8,128)(2,1)S(1)}, bf16[128,256]{1,0:T(8,128)(2,1)S(1)}) custom-call(f32[4,128,128]{2,1,0:T(8,128)S(1)} %get-tuple-element.21.x_ref, f32[4,128]{1,0:T(4,128)S(1)} %get-tuple-element.22.rho_ref, f32[128,128]{1,0:T(8,128)S(1)} %collective-permute-done.arriving_ref, s32[1]{0:T(128)} %bitcast.1.keep_ref, ...), custom_call_target="tpu_custom_call" | custom-call | flops 536870912 | bytes 2097152 | tf_op jit(solution)/shard_map/first_value_pass/pallas_call | solution.py:184
  10.3 2.2 %collective-permute-start.1 = (f32[72,256]{1,0:T(8,128)S(1)}, f32[72,256]{1,0:T(8,128)S(1)}, u32[]{:S(2)}, u32[]{:S(2)}) collective-permute-start(f32[72,256]{1,0:T(8,128)S(1)} %get-tuple-element.29.refs_0_), channel_id=1, source_target_pairs={{0,4},{4,0},{8,12},{12,8},{1,5},{5,1},{9,13},{13,9},{2,6},{6,2},{1... | collective-permute-start | bytes 221192 | tf_op jit(solution)/shard_map/ppermute | solution.py:28
  12.5 2.6 %collective-permute-start.2 = (f32[72,256]{1,0:T(8,128)S(1)}, f32[72,256]{1,0:T(8,128)S(1)}, u32[]{:S(2)}, u32[]{:S(2)}) collective-permute-start(f32[72,256]{1,0:T(8,128)S(1)} %get-tuple-element.29.refs_0_), channel_id=1, source_target_pairs={{0,8},{4,12},{8,0},{12,4},{1,9},{5,13},{9,1},{13,5},{2,10},{6,14},... | collective-permute-start | bytes 221192 | tf_op jit(solution)/shard_map/ppermute | solution.py:28
  15.1 0.0 collective-permute-start.3
  15.1 3.3 %value_pass.1.refs_0_ = f32[64,256]{1,0:T(8,128)S(1)} custom-call(bf16[128,256]{1,0:T(8,128)(2,1)S(1)} %get-tuple-element.27.state_ref, bf16[8192,128]{1,0:T(8,128)(2,1)S(1)} %get-tuple-element.25.turned_ref, f32[64,128]{1,0:T(8,128)S(1)} %get-tuple-element.26.n_ref), custom_call_target="tpu_custom_call" | custom-call | flops 536870912 | bytes 2097152 | tf_op jit(solution)/shard_map/value_pass/pallas_call | solution.py:201
  18.4 1.0 %collective-permute-start.4 = (f32[64,256]{1,0:T(8,128)S(1)}, f32[64,256]{1,0:T(8,128)S(1)}, u32[]{:S(2)}, u32[]{:S(2)}) collective-permute-start(f32[64,256]{1,0:T(8,128)S(1)} %value_pass.1.refs_0_), channel_id=1, source_target_pairs={{0,4},{4,0},{8,12},{12,8},{1,5},{5,1},{9,13},{13,9},{2,6},{6,2},{1... | collective-permute-start | bytes 196616 | tf_op jit(solution)/shard_map/ppermute | solution.py:28
  19.4 3.5 %collective-permute-start.5 = (f32[64,256]{1,0:T(8,128)S(1)}, f32[64,256]{1,0:T(8,128)S(1)}, u32[]{:S(2)}, u32[]{:S(2)}) collective-permute-start(f32[64,256]{1,0:T(8,128)S(1)} %value_pass.1.refs_0_), channel_id=1, source_target_pairs={{0,8},{4,12},{8,0},{12,4},{1,9},{5,13},{9,1},{13,5},{2,10},{6,14},... | collective-permute-start | bytes 196616 | tf_op jit(solution)/shard_map/ppermute | solution.py:28
  22.9 0.0 collective-permute-done.1.refs_1_
  22.9 0.0 collective-permute-start.6
  22.9 0.0 collective-permute-done.2.refs_2_
  22.9 4.1 %late_pull_pass.1 = (f32[2,32]{1,0:T(2,128)S(1)}, f32[32,128]{1,0:T(8,128)S(1)}, f32[2,128,128]{2,1,0:T(8,128)S(1)}) custom-call(s32[1]{0:T(128)} %bitcast.me_ref, bf16[128,256]{1,0:T(8,128)(2,1)S(1)} %get-tuple-element.28.state_ref, bf16[8192,128]{1,0:T(8,128)(2,1)S(1)} %get-tuple-element.25.turned_ref, bf16[128,8192]{1,0:T(8,128)(2,1)S(1)} %copy-done, ...), custom_call_target="tpu_custom_call" | custom-call | flops 1073741824 | bytes 4194304 | tf_op jit(solution)/shard_map/late_pull_pass/pallas_call | solution.py:343
  27.0 1.9 %collective-permute-done.6.refs_3_ = f32[64,256]{1,0:T(8,128)S(1)} collective-permute-done((f32[64,256]{1,0:T(8,128)S(1)}, f32[64,256]{1,0:T(8,128)S(1)}, u32[]{:S(2)}, u32[]{:S(2)}) %collective-permute-start.6) | collective-permute-done | bytes 65568 | tf_op jit(solution)/shard_map/ppermute | solution.py:28
  28.9 4.1 %early_pull_pass.1 = (f32[4,32]{1,0:T(4,128)S(1)}, f32[4,32,128]{2,1,0:T(8,128)S(1)}, f32[4,32,128]{2,1,0:T(8,128)S(1)}, f32[4,32,128]{2,1,0:T(8,128)S(1)}, f32[4,32,128]{2,1,0:T(8,128)S(1)}) custom-call(s32[1]{0:T(128)} %bitcast.me_ref, bf16[128,256]{1,0:T(8,128)(2,1)S(1)} %get-tuple-element.27.state_ref, ...), custom_call_target="tpu_custom_call" | custom-call | flops 1073741824 | bytes 4194304 | tf_op jit(solution)/shard_map/early_pull_pass/pallas_call | solution.py:365
  33.0 0.1 collective-permute-start.7
  33.1 2.5 %collective-permute-start.8 = (f32[4,32,128]{2,1,0:T(8,128)S(1)}, f32[4,32,128]{2,1,0:T(8,128)S(1)}, u32[]{:S(2)}, u32[]{:S(2)}) collective-permute-start(f32[4,32,128]{2,1,0:T(8,128)S(1)} %get-tuple-element.35), channel_id=1, source_target_pairs={{0,8},{4,12},{8,0},{12,4},{1,9},{5,13},{9,1},{13,5},{2,10},{6,14},... | collective-permute-start | bytes 196616 | tf_op jit(solution)/shard_map/ppermute | solution.py:28
  35.6 1.9 %collective-permute-start.9 = (f32[4,32,128]{2,1,0:T(8,128)S(1)}, f32[4,32,128]{2,1,0:T(8,128)S(1)}, u32[]{:S(2)}, u32[]{:S(2)}) collective-permute-start(f32[4,32,128]{2,1,0:T(8,128)S(1)} %get-tuple-element.36), channel_id=1, source_target_pairs={{0,12},{4,8},{8,4},{12,0},{1,13},{5,9},{9,5},{13,1},{2,14},{6,10},... | collective-permute-start | bytes 196616 | tf_op jit(solution)/shard_map/ppermute | solution.py:28
  37.5 1.1 %collective-permute-done.7 = f32[4,32,128]{2,1,0:T(8,128)S(1)} collective-permute-done((f32[4,32,128]{2,1,0:T(8,128)S(1)}, f32[4,32,128]{2,1,0:T(8,128)S(1)}, u32[]{:S(2)}, u32[]{:S(2)}) %collective-permute-start.7) | collective-permute-done | bytes 65568 | tf_op jit(solution)/shard_map/ppermute | solution.py:28
  38.6 3.1 %collective-permute-done.9 = f32[4,32,128]{2,1,0:T(8,128)S(1)} collective-permute-done((f32[4,32,128]{2,1,0:T(8,128)S(1)}, f32[4,32,128]{2,1,0:T(8,128)S(1)}, u32[]{:S(2)}, u32[]{:S(2)}) %collective-permute-start.9) | collective-permute-done | bytes 65568 | tf_op jit(solution)/shard_map/ppermute | solution.py:28
  41.7 1.6 %collective-permute-start.10 = (f32[32,128]{1,0:T(8,128)S(1)}, f32[32,128]{1,0:T(8,128)S(1)}, u32[]{:S(2)}, u32[]{:S(2)}) collective-permute-start(f32[32,128]{1,0:T(8,128)S(1)} %fusion), channel_id=1, source_target_pairs={{0,2},{2,0},{1,3},{3,1},{4,6},{6,4},{5,7},{7,5},{8,10},{10,8},{9,1... | collective-permute-start | bytes 49160 | tf_op jit(solution)/shard_map/ppermute | solution.py:28
  43.3 2.2 %collective-permute-done.10 = f32[32,128]{1,0:T(8,128)S(1)} collective-permute-done((f32[32,128]{1,0:T(8,128)S(1)}, f32[32,128]{1,0:T(8,128)S(1)}, u32[]{:S(2)}, u32[]{:S(2)}) %collective-permute-start.10) | collective-permute-done | bytes 16416 | tf_op jit(solution)/shard_map/ppermute | solution.py:28
  45.5 0.1 collective-permute-start.11
  45.6 0.1 collective-permute-start.12
  45.7 2.5 %collective-permute-start.13 = (f32[4,32,128]{2,1,0:T(8,128)S(1)}, f32[4,32,128]{2,1,0:T(8,128)S(1)}, u32[]{:S(2)}, u32[]{:S(2)}) collective-permute-start(f32[4,32,128]{2,1,0:T(8,128)S(1)} %multiply_add_fusion.refs_0_), channel_id=1, source_target_pairs={{0,8},{4,12},{8,0},{12,4},{1,9},{5,13},{9,1},{13,5},{2,10},{6,14},... | collective-permute-start | bytes 196616 | tf_op jit(solution)/shard_map/ppermute | solution.py:28
  48.1 1.9 %collective-permute-start.14 = (f32[4,32,128]{2,1,0:T(8,128)S(1)}, f32[4,32,128]{2,1,0:T(8,128)S(1)}, u32[]{:S(2)}, u32[]{:S(2)}) collective-permute-start(f32[4,32,128]{2,1,0:T(8,128)S(1)} %multiply_add_fusion.refs_0_), channel_id=1, source_target_pairs={{0,12},{4,8},{8,4},{12,0},{1,13},{5,9},{9,5},{13,1},{2,14},{6,10},... | collective-permute-start | bytes 196616 | tf_op jit(solution)/shard_map/ppermute | solution.py:28
  50.0 0.6 %add_multiply_fusion = f32[4,32]{1,0:T(4,128)} fusion(f32[4,32]{1,0:T(4,128)S(1)} %get-tuple-element.38, f32[4,32]{1,0:T(4,128)S(1)} %collective-permute-done.11), kind=kLoop, calls=%fused_computation.5 | loop fusion | flops 256 | bytes 1536 | tf_op jit(solution)/shard_map/div | solution.py:465
  50.6 0.5 collective-permute-done.12.refs_1_
  51.2 3.2 %collective-permute-done.13.refs_2_ = f32[4,32,128]{2,1,0:T(8,128)S(1)} collective-permute-done((f32[4,32,128]{2,1,0:T(8,128)S(1)}, f32[4,32,128]{2,1,0:T(8,128)S(1)}, u32[]{:S(2)}, u32[]{:S(2)}) %collective-permute-start.13) | collective-permute-done | bytes 65568 | tf_op jit(solution)/shard_map/ppermute | solution.py:28
  54.4 0.7 %place.1 = f32[4,128,128]{2,1,0:T(8,128)} custom-call(s32[1]{0:T(128)} %bitcast.me_ref, f32[4,32,128]{2,1,0:T(8,128)S(1)} %multiply_add_fusion.refs_0_, f32[4,32,128]{2,1,0:T(8,128)S(1)} %collective-permute-done.12.refs_1_, f32[4,32,128]{2,1,0:T(8,128)S(1)} %collective-permute-done.13.refs_2_, f32[4,32,128]{2,1,0:T(8,128)S(1)} %collective-permute-done.14.refs_3_), custom_call_target="tpu_custom_call" | custom-call | tf_op jit(solution)/shard_map/place/pallas_call | solution.py:413
  (16 shorter events, 0.1 us)
Async XLA Ops:
  1.6 5.2 %collective-permute-start = (f32[128,128]{1,0:T(8,128)S(1)}, f32[128,128]{1,0:T(8,128)S(1)}, u32[]{:S(2)}, u32[]{:S(2)}) collective-permute-start(f32[128,128]{1,0:T(8,128)S(1)} %get-tuple-element.23), channel_id=1, source_target_pairs={{0,2},{2,0},{1,3},{3,1},{4,6},{6,4},{5,7},{7,5},{8,10},{10,8},{9,1... | collective-permute-start | bytes 196616 | tf_op jit(solution)/shard_map/ppermute | solution.py:28
  10.3 12.5 %collective-permute-start.1 = (f32[72,256]{1,0:T(8,128)S(1)}, f32[72,256]{1,0:T(8,128)S(1)}, u32[]{:S(2)}, u32[]{:S(2)}) collective-permute-start(f32[72,256]{1,0:T(8,128)S(1)} %get-tuple-element.29.refs_0_), channel_id=1, source_target_pairs={{0,4},{4,0},{8,12},{12,8},{1,5},{5,1},{9,13},{13,9},{2,6},{6,2},{1... | collective-permute-start | bytes 221192 | tf_op jit(solution)/shard_map/ppermute | solution.py:28
  12.5 10.4 %collective-permute-start.2 = (f32[72,256]{1,0:T(8,128)S(1)}, f32[72,256]{1,0:T(8,128)S(1)}, u32[]{:S(2)}, u32[]{:S(2)}) collective-permute-start(f32[72,256]{1,0:T(8,128)S(1)} %get-tuple-element.29.refs_0_), channel_id=1, source_target_pairs={{0,8},{4,12},{8,0},{12,4},{1,9},{5,13},{9,1},{13,5},{2,10},{6,14},... | collective-permute-start | bytes 221192 | tf_op jit(solution)/shard_map/ppermute | solution.py:28
  15.1 7.8 %collective-permute-start.3 = (f32[72,256]{1,0:T(8,128)S(1)}, f32[72,256]{1,0:T(8,128)S(1)}, u32[]{:S(2)}, u32[]{:S(2)}) collective-permute-start(f32[72,256]{1,0:T(8,128)S(1)} %get-tuple-element.29.refs_0_), channel_id=1, source_target_pairs={{0,12},{4,8},{8,4},{12,0},{1,13},{5,9},{9,5},{13,1},{2,14},{6,10},... | collective-permute-start | bytes 221192 | tf_op jit(solution)/shard_map/ppermute | solution.py:28
  15.1 7.8 %copy-start = (bf16[128,8192]{1,0:T(8,128)(2,1)S(1)}, bf16[128,8192]{1,0:T(8,128)(2,1)}, u32[]{:S(2)}) copy-start(bf16[128,8192]{1,0:T(8,128)(2,1)} %d_ref.3) | copy-start | bytes 6291460
  18.4 8.6 %collective-permute-start.4 = (f32[64,256]{1,0:T(8,128)S(1)}, f32[64,256]{1,0:T(8,128)S(1)}, u32[]{:S(2)}, u32[]{:S(2)}) collective-permute-start(f32[64,256]{1,0:T(8,128)S(1)} %value_pass.1.refs_0_), channel_id=1, source_target_pairs={{0,4},{4,0},{8,12},{12,8},{1,5},{5,1},{9,13},{13,9},{2,6},{6,2},{1... | collective-permute-start | bytes 196616 | tf_op jit(solution)/shard_map/ppermute | solution.py:28
  19.4 7.6 %collective-permute-start.5 = (f32[64,256]{1,0:T(8,128)S(1)}, f32[64,256]{1,0:T(8,128)S(1)}, u32[]{:S(2)}, u32[]{:S(2)}) collective-permute-start(f32[64,256]{1,0:T(8,128)S(1)} %value_pass.1.refs_0_), channel_id=1, source_target_pairs={{0,8},{4,12},{8,0},{12,4},{1,9},{5,13},{9,1},{13,5},{2,10},{6,14},... | collective-permute-start | bytes 196616 | tf_op jit(solution)/shard_map/ppermute | solution.py:28
  22.9 6.1 %collective-permute-start.6 = (f32[64,256]{1,0:T(8,128)S(1)}, f32[64,256]{1,0:T(8,128)S(1)}, u32[]{:S(2)}, u32[]{:S(2)}) collective-permute-start(f32[64,256]{1,0:T(8,128)S(1)} %value_pass.1.refs_0_), channel_id=1, source_target_pairs={{0,12},{4,8},{8,4},{12,0},{1,13},{5,9},{9,5},{13,1},{2,14},{6,10},... | collective-permute-start | bytes 196616 | tf_op jit(solution)/shard_map/ppermute | solution.py:28
  28.9 8.6 %copy-start.1 = (f32[4,128]{1,0:T(4,128)S(1)}, f32[4,128]{1,0:T(4,128)}, u32[]{:S(2)}) copy-start(f32[4,128]{1,0:T(4,128)} %rho_hbm.1) | copy-start | bytes 6148
  33.0 5.5 %collective-permute-start.7 = (f32[4,32,128]{2,1,0:T(8,128)S(1)}, f32[4,32,128]{2,1,0:T(8,128)S(1)}, u32[]{:S(2)}, u32[]{:S(2)}) collective-permute-start(f32[4,32,128]{2,1,0:T(8,128)S(1)} %get-tuple-element.34), channel_id=1, source_target_pairs={{0,4},{4,0},{8,12},{12,8},{1,5},{5,1},{9,13},{13,9},{2,6},{6,2},{1... | collective-permute-start | bytes 196616 | tf_op jit(solution)/shard_map/ppermute | solution.py:28
  33.1 5.5 %collective-permute-start.8 = (f32[4,32,128]{2,1,0:T(8,128)S(1)}, f32[4,32,128]{2,1,0:T(8,128)S(1)}, u32[]{:S(2)}, u32[]{:S(2)}) collective-permute-start(f32[4,32,128]{2,1,0:T(8,128)S(1)} %get-tuple-element.35), channel_id=1, source_target_pairs={{0,8},{4,12},{8,0},{12,4},{1,9},{5,13},{9,1},{13,5},{2,10},{6,14},... | collective-permute-start | bytes 196616 | tf_op jit(solution)/shard_map/ppermute | solution.py:28
  35.6 6.1 %collective-permute-start.9 = (f32[4,32,128]{2,1,0:T(8,128)S(1)}, f32[4,32,128]{2,1,0:T(8,128)S(1)}, u32[]{:S(2)}, u32[]{:S(2)}) collective-permute-start(f32[4,32,128]{2,1,0:T(8,128)S(1)} %get-tuple-element.36), channel_id=1, source_target_pairs={{0,12},{4,8},{8,4},{12,0},{1,13},{5,9},{9,5},{13,1},{2,14},{6,10},... | collective-permute-start | bytes 196616 | tf_op jit(solution)/shard_map/ppermute | solution.py:28
  41.7 3.8 %collective-permute-start.10 = (f32[32,128]{1,0:T(8,128)S(1)}, f32[32,128]{1,0:T(8,128)S(1)}, u32[]{:S(2)}, u32[]{:S(2)}) collective-permute-start(f32[32,128]{1,0:T(8,128)S(1)} %fusion), channel_id=1, source_target_pairs={{0,2},{2,0},{1,3},{3,1},{4,6},{6,4},{5,7},{7,5},{8,10},{10,8},{9,1... | collective-permute-start | bytes 49160 | tf_op jit(solution)/shard_map/ppermute | solution.py:28
  45.5 4.5 %collective-permute-start.11 = (f32[4,32]{1,0:T(4,128)S(1)}, f32[4,32]{1,0:T(4,128)S(1)}, u32[]{:S(2)}, u32[]{:S(2)}) collective-permute-start(f32[4,32]{1,0:T(4,128)S(1)} %get-tuple-element.38), channel_id=1, source_target_pairs={{0,1},{1,0},{2,3},{3,2},{4,5},{5,4},{6,7},{7,6},{8,9},{9,8},{10,11... | collective-permute-start | bytes 1544 | tf_op jit(solution)/shard_map/ppermute | solution.py:28
  45.6 5.6 %collective-permute-start.12 = (f32[4,32,128]{2,1,0:T(8,128)S(1)}, f32[4,32,128]{2,1,0:T(8,128)S(1)}, u32[]{:S(2)}, u32[]{:S(2)}) collective-permute-start(f32[4,32,128]{2,1,0:T(8,128)S(1)} %multiply_add_fusion.refs_0_), channel_id=1, source_target_pairs={{0,4},{4,0},{8,12},{12,8},{1,5},{5,1},{9,13},{13,9},{2,6},{6,2},{1... | collective-permute-start | bytes 196616 | tf_op jit(solution)/shard_map/ppermute | solution.py:28
  45.7 8.7 %collective-permute-start.13 = (f32[4,32,128]{2,1,0:T(8,128)S(1)}, f32[4,32,128]{2,1,0:T(8,128)S(1)}, u32[]{:S(2)}, u32[]{:S(2)}) collective-permute-start(f32[4,32,128]{2,1,0:T(8,128)S(1)} %multiply_add_fusion.refs_0_), channel_id=1, source_target_pairs={{0,8},{4,12},{8,0},{12,4},{1,9},{5,13},{9,1},{13,5},{2,10},{6,14},... | collective-permute-start | bytes 196616 | tf_op jit(solution)/shard_map/ppermute | solution.py:28
  48.1 6.2 %collective-permute-start.14 = (f32[4,32,128]{2,1,0:T(8,128)S(1)}, f32[4,32,128]{2,1,0:T(8,128)S(1)}, u32[]{:S(2)}, u32[]{:S(2)}) collective-permute-start(f32[4,32,128]{2,1,0:T(8,128)S(1)} %multiply_add_fusion.refs_0_), channel_id=1, source_target_pairs={{0,12},{4,8},{8,4},{12,0},{1,13},{5,9},{9,5},{13,1},{2,14},{6,10},... | collective-permute-start | bytes 196616 | tf_op jit(solution)/shard_map/ppermute | solution.py:28

commit v4 on v3

--- a/solution.py
+++ b/solution.py
@@ -11,6 +11,7 @@
 highest = lax.Precision.HIGHEST
 f32 = jnp.float32
 bf16 = jnp.bfloat16
+VALUE_STEP = 2048
 
 
 def swap(value, axes, sizes, flips):
@@ -139,17 +140,14 @@
     )(*far_copy(d, n, mass, ceiling, obligor))
 
 
-def state_stage(x_ref, rho_ref, arriving_ref, keep_ref, state_refs):
+def value_kernel(step, x_ref, rho_ref, arriving_ref, keep_ref, facts_ref, turned_ref, n_ref, sums_ref, state_ref):
     dates, paths, _ = x_ref.shape
-    columns = [(ref, at) for ref in state_refs[::-1] for at in range(0, ref.shape[1], paths)]
+    blocks = step // block_width
     carried = arriving_ref[...] * keep_ref[0].astype(f32)
-    for t, (ref, at) in enumerate(columns):
+    for t in range(dates):
         carried = rho_ref[t : t + 1, :] * carried + x_ref[t]
-        ref[:, at : at + paths] = carried.T.astype(bf16)
-
-
-def sum_stage(step, state_ref, turned_ref, n_ref, sums_ref):
-    blocks = step // block_width
+        state_ref[:, t * paths : (t + 1) * paths] = carried.T.astype(bf16)
+    sums_ref[n_ref.shape[0] :, :128] = facts_ref[...]
 
     @pl.loop(0, turned_ref.shape[0] // step)
     def _(c):
@@ -163,49 +161,56 @@
         sums_ref[pl.ds(pl.multiple_of(c * blocks, blocks), blocks), :] = jnp.concatenate(lines, axis=0)
 
 
-def first_value_kernel(step, x_ref, rho_ref, arriving_ref, keep_ref, facts_ref, turned_ref, n_ref, sums_ref, *state_refs):
-    state_stage(x_ref, rho_ref, arriving_ref, keep_ref, state_refs)
-    total = n_ref.shape[0]
-    sums_ref[total:, :128] = facts_ref[...]
-    sum_stage(step, state_refs[0], turned_ref, n_ref, sums_ref)
-
-
-def value_cost(rows, trades, factors):
-    return pl.CostEstimate(
-        flops=2 * rows * trades * factors, bytes_accessed=2 * trades * factors, transcendentals=2 * rows * trades
-    )
-
-
-def first_value_pass(groups, x, rho, arriving, keep, facts, turned, n):
+def value_pass(x, rho, arriving, keep, facts, turned, n):
     dates, paths, factors = x.shape
-    trades = turned.shape[0]
-    rows = dates // groups * paths
+    rows, trades = dates * paths, turned.shape[0]
     vmem = pl.BlockSpec(memory_space=pltpu.VMEM)
-    out = pl.pallas_call(
-        functools.partial(first_value_kernel, min(2048, trades)),
+    return pl.pallas_call(
+        functools.partial(value_kernel, min(VALUE_STEP, trades)),
         in_specs=[vmem, vmem, vmem, pl.BlockSpec(memory_space=pltpu.SMEM), vmem, vmem, vmem],
-        out_specs=[vmem] * (1 + groups),
-        out_shape=[jax.ShapeDtypeStruct((n.shape[0] + 8, rows), f32)]
-        + [jax.ShapeDtypeStruct((factors, rows), bf16)] * groups,
-        compiler_params=pltpu.CompilerParams(vmem_limit_bytes=24 << 20),
-        cost_estimate=value_cost(rows, trades, factors),
-        name="first_value_pass",
+        out_specs=[vmem] * 2,
+        out_shape=[
+            jax.ShapeDtypeStruct((n.shape[0] + 8, rows), f32),
+            jax.ShapeDtypeStruct((factors, rows), bf16),
+        ],
+        compiler_params=pltpu.CompilerParams(vmem_limit_bytes=32 << 20),
+        cost_estimate=pl.CostEstimate(
+            flops=2 * rows * trades * factors, bytes_accessed=2 * trades * factors, transcendentals=2 * rows * trades
+        ),
+        name="value_pass",
     )(x, rho, arriving, keep, facts, turned, n)
-    return out[0], out[1:]
-
-
-def value_pass(state, turned, n):
+
+
+def slope_kernel(step, state_ref, turned_ref, n_ref, slope_ref, half_ref):
+    blocks = step // block_width
+    half_ref[...] = state_ref[...] * 0.5
+
+    @pl.loop(0, turned_ref.shape[0] // step)
+    def _(c):
+        size_t = 0.5 * n_ref[pl.ds(pl.multiple_of(c * blocks, blocks), blocks), :].T
+        turned = turned_ref[pl.ds(pl.multiple_of(c * step, step), step), :]
+        linear = jnp.dot(turned, half_ref[...], preferred_element_type=f32)
+        for b in range(blocks):
+            size = size_t[:, b : b + 1]
+            slope = jnp.tanh(linear[b * block_width : (b + 1) * block_width]) * size + size
+            slope_ref[pl.ds(pl.multiple_of(c * step + b * block_width, block_width), block_width), :] = slope
+
+
+def slope_pass(state, turned, n):
     factors, rows = state.shape
     trades = turned.shape[0]
     vmem = pl.BlockSpec(memory_space=pltpu.VMEM)
     return pl.pallas_call(
-        functools.partial(sum_stage, min(2048, trades)),
+        functools.partial(slope_kernel, min(2048, trades)),
         in_specs=[vmem] * 3,
         out_specs=vmem,
-        out_shape=jax.ShapeDtypeStruct((n.shape[0], rows), f32),
-        compiler_params=pltpu.CompilerParams(vmem_limit_bytes=24 << 20),
-        cost_estimate=value_cost(rows, trades, factors),
-        name="value_pass",
+        out_shape=jax.ShapeDtypeStruct((trades, rows), f32),
+        scratch_shapes=[pltpu.VMEM((factors, rows), bf16)],
+        compiler_params=pltpu.CompilerParams(vmem_limit_bytes=16 << 20),
+        cost_estimate=pl.CostEstimate(
+            flops=2 * rows * trades * factors, bytes_accessed=4 * trades * rows, transcendentals=rows * trades
+        ),
+        name="slope_pass",
     )(state, turned, n)
 
 
@@ -219,10 +224,10 @@
     return dot(low) + dot(middle) + dot(high)
 
 
-def net_stage(cpty_dev, dates, first, me, sums, facts, upstream_ref):
+def net_stage(cpty_dev, dates, me, sums, upstream_ref):
     shards = len(sums)
     blocks, rows = upstream_ref.shape
-    count = rows // 128
+    paths = rows // dates
     cpties = shards * cpty_dev
     shift = cpty_dev.bit_length() - 1
 
@@ -230,10 +235,10 @@
         owner = owner.astype(jnp.int32)
         return (((owner >> shift) ^ me) << shift) + (owner & (cpty_dev - 1))
 
-    columns = [facts[k].T for k in range(shards)]
+    columns = [part[blocks : blocks + 8, :128].T for part in sums]
     netted = None
     for k in range(shards):
-        row = label(facts[k][dates + 1 : dates + 2, :blocks])
+        row = label(sums[k][blocks + dates + 1 : blocks + dates + 2, :blocks])
         pick = lax.broadcasted_iota(jnp.int32, (cpties, blocks), 0) == row
         part = split_dot(jnp.where(pick, 1.0, 0.0), sums[k][:blocks])
         netted = part if netted is None else netted + part
@@ -244,78 +249,49 @@
         shifted = netted[k * cpty_dev : (k + 1) * cpty_dev] - columns[k][:cpty_dev, dates : dates + 1]
         slope = 0.5 * jnp.tanh(0.5 * shifted) + 0.5
         parts = []
-        for t in range(count):
-            mass = columns[k][:cpty_dev, first + t : first + t + 1]
-            parts.append(slope[:, t * 128 : (t + 1) * 128] * mass)
+        for t in range(dates):
+            parts.append(slope[:, t * paths : (t + 1) * paths] * columns[k][:cpty_dev, t : t + 1])
         adjoint.append(jnp.concatenate(parts, axis=1))
         if k == 0:
             exposed = softplus(shifted)
-            for t in range(count):
-                totals.append(jnp.sum(exposed[:, t * 128 : (t + 1) * 128], axis=1, keepdims=True))
+            for t in range(dates):
+                totals.append(jnp.sum(exposed[:, t * paths : (t + 1) * paths], axis=1, keepdims=True))
     upstream_ref[...] = split_dot(own, jnp.concatenate(adjoint, axis=0))
     return totals
 
 
-def pull_stage(step, state_ref, turned_ref, d_ref, n_ref, upstream_ref, half_ref, total_ref):
+def pull_stage(step, slope_ref, d_ref, upstream_ref, total_ref):
     blocks = step // block_width
-    half_ref[...] = state_ref[...] * 0.5
     total_ref[...] = jnp.zeros_like(total_ref)
 
     @pl.loop(0, d_ref.shape[1] // step)
     def _(c):
-        lines = pl.ds(pl.multiple_of(c * blocks, blocks), blocks)
-        trades = pl.ds(pl.multiple_of(c * step, step), step)
-        size_t = 0.5 * n_ref[lines, :].T
-        upstream = upstream_ref[lines, :]
-        linear = jnp.dot(turned_ref[trades, :], half_ref[...], preferred_element_type=f32)
+        upstream = upstream_ref[pl.ds(pl.multiple_of(c * blocks, blocks), blocks), :]
         parts = []
         for b in range(blocks):
-            slope = jnp.tanh(linear[b * block_width : (b + 1) * block_width])
-            size = size_t[:, b : b + 1]
-            parts.append(((slope * size + size) * upstream[b : b + 1, :]).astype(bf16))
+            slope = slope_ref[pl.ds(pl.multiple_of(c * step + b * block_width, block_width), block_width), :]
+            parts.append((slope * upstream[b : b + 1, :]).astype(bf16))
+        trades = pl.ds(pl.multiple_of(c * step, step), step)
         total_ref[...] += jnp.dot(d_ref[:, trades], jnp.concatenate(parts, axis=0), preferred_element_type=f32)
 
 
-def write_table(table_ref, totals, first):
-    lane = lax.broadcasted_iota(jnp.int32, (totals[0].shape[0], 128), 1)
+def net_pull_kernel(step, cpty_dev, shards, me_ref, slope_ref, d_ref, rho_ref, *refs):
+    sums, refs = refs[:shards], refs[shards:]
+    exposure_ref, refs = refs[0], refs[1:]
+    chain, refs = refs[:shards], refs[shards:]
+    upstream_ref, total_ref, chained_ref = refs
+    dates, paths, factors = chained_ref.shape
+    me = me_ref[0]
+    totals = net_stage(cpty_dev, dates, me, sums, upstream_ref)
+    lane = lax.broadcasted_iota(jnp.int32, (cpty_dev, 128), 1)
     table = jnp.zeros(lane.shape, f32)
     for t, total in enumerate(totals):
         table = jnp.where(lane == t, total, table)
-    table_ref[first : first + len(totals), :] = table.T[: len(totals)]
-
-
-def late_pull_kernel(step, shards, cpty_dev, dates, first, me_ref, state_ref, turned_ref, d_ref, n_ref, *refs):
-    sums, refs = refs[:shards], refs[shards:]
-    exposure_ref, facts_ref, direct_ref, upstream_ref, half_ref, total_ref = refs
-    blocks = n_ref.shape[0]
-    facts = [part[blocks : blocks + 8, :128] for part in sums]
-    for k in range(shards):
-        facts_ref[8 * k : 8 * (k + 1), :] = facts[k]
-    totals = net_stage(cpty_dev, dates, first, me_ref[0], sums, facts, upstream_ref)
-    write_table(exposure_ref, totals, 0)
-    pull_stage(step, state_ref, turned_ref, d_ref, n_ref, upstream_ref, half_ref, total_ref)
-    paths = direct_ref.shape[1]
-    for t in range(direct_ref.shape[0]):
-        direct_ref[t] = total_ref[:, t * paths : (t + 1) * paths].T
-
-
-def early_pull_kernel(step, shards, cpty_dev, me_ref, state_ref, turned_ref, d_ref, n_ref, rho_ref, facts_ref, late_exposure_ref, late_ref, *refs):
-    sums, refs = refs[:shards], refs[shards:]
-    exposure_ref, refs = refs[0], refs[1:]
-    chain, refs = refs[:shards], refs[shards:]
-    upstream_ref, half_ref, total_ref, chained_ref = refs
-    dates, paths, factors = chained_ref.shape
-    early = dates - late_ref.shape[0]
-    me = me_ref[0]
-    facts = [facts_ref[8 * k : 8 * (k + 1), :] for k in range(shards)]
-    totals = net_stage(cpty_dev, dates, 0, me, sums, facts, upstream_ref)
-    write_table(exposure_ref, totals, 0)
-    exposure_ref[early:dates, :] = late_exposure_ref[...]
-    pull_stage(step, state_ref, turned_ref, d_ref, n_ref, upstream_ref, half_ref, total_ref)
+    exposure_ref[...] = table.T[:dates]
+    pull_stage(step, slope_ref, d_ref, upstream_ref, total_ref)
     carried = jnp.zeros((paths, factors), f32)
     for t in reversed(range(dates)):
-        direct = late_ref[t - early] if t >= early else total_ref[:, t * paths : (t + 1) * paths].T
-        adjoint = direct + carried
+        adjoint = total_ref[:, t * paths : (t + 1) * paths].T + carried
         chained_ref[t] = adjoint
         carried = rho_ref[t : t + 1, :] * adjoint
     piece = paths // shards
@@ -324,78 +300,53 @@
         chain[k][...] = chained_ref[:, at, :]
 
 
-def pull_cost(rows, trades, factors):
-    return pl.CostEstimate(
-        flops=4 * rows * trades * factors, bytes_accessed=4 * trades * factors, transcendentals=rows * trades
-    )
-
-
-def pull_scratch(blocks, factors, rows):
-    return [pltpu.VMEM((blocks, rows), f32), pltpu.VMEM((factors, rows), bf16), pltpu.VMEM((factors, rows), f32)]
-
-
-def late_pull_pass(dates, paths, cpty_dev, me, state, turned, d, n, sums):
-    factors, rows = state.shape
-    trades = d.shape[1]
-    shards = len(sums)
-    count = rows // paths
-    vmem = pl.BlockSpec(memory_space=pltpu.VMEM)
-    return pl.pallas_call(
-        functools.partial(late_pull_kernel, min(2048, trades), shards, cpty_dev, dates, dates - count),
-        in_specs=[pl.BlockSpec(memory_space=pltpu.SMEM)] + [vmem] * (4 + shards),
-        out_specs=[vmem] * 3,
-        out_shape=[
-            jax.ShapeDtypeStruct((count, cpty_dev), f32),
-            jax.ShapeDtypeStruct((8 * shards, 128), f32),
-            jax.ShapeDtypeStruct((count, paths, factors), f32),
-        ],
-        scratch_shapes=pull_scratch(n.shape[0], factors, rows),
-        compiler_params=pltpu.CompilerParams(vmem_limit_bytes=24 << 20),
-        cost_estimate=pull_cost(rows, trades, factors),
-        name="late_pull_pass",
-    )(me, state, turned, d, n, *sums)
-
-
-def early_pull_pass(dates, paths, cpty_dev, me, state, turned, d, n, rho, facts, late_exposure, late, sums):
-    factors, rows = state.shape
-    trades = d.shape[1]
+def net_pull_pass(dates, cpty_dev, me, slope, d, rho, sums):
+    trades, rows = slope.shape
+    factors = d.shape[0]
+    paths = rows // dates
     shards = len(sums)
     piece = paths // shards
     vmem = pl.BlockSpec(memory_space=pltpu.VMEM)
     out = pl.pallas_call(
-        functools.partial(early_pull_kernel, min(2048, trades), shards, cpty_dev),
-        in_specs=[pl.BlockSpec(memory_space=pltpu.SMEM)] + [vmem] * (8 + shards),
+        functools.partial(net_pull_kernel, min(2048, trades), cpty_dev, shards),
+        in_specs=[pl.BlockSpec(memory_space=pltpu.SMEM)] + [vmem] * (3 + shards),
         out_specs=[vmem] * (1 + shards),
         out_shape=[jax.ShapeDtypeStruct((dates, cpty_dev), f32)]
         + [jax.ShapeDtypeStruct((dates, piece, factors), f32)] * shards,
-        scratch_shapes=pull_scratch(n.shape[0], factors, rows) + [pltpu.VMEM((dates, paths, factors), f32)],
-        compiler_params=pltpu.CompilerParams(vmem_limit_bytes=24 << 20),
-        cost_estimate=pull_cost(rows, trades, factors),
-        name="early_pull_pass",
-    )(me, state, turned, d, n, rho, facts, late_exposure, late, *sums)
+        scratch_shapes=[
+            pltpu.VMEM((trades // block_width, rows), f32),
+            pltpu.VMEM((factors, rows), f32),
+            pltpu.VMEM((dates, paths, factors), f32),
+        ],
+        compiler_params=pltpu.CompilerParams(vmem_limit_bytes=16 << 20),
+        cost_estimate=pl.CostEstimate(
+            flops=2 * rows * trades * factors, bytes_accessed=4 * trades * rows, transcendentals=0
+        ),
+        name="net_pull_pass",
+    )(me, slope, d, rho, *sums)
     return out[0], out[1:]
 
 
-def pull_kernel(step, state_ref, turned_ref, d_ref, n_ref, upstream_ref, direct_ref, half_ref, total_ref):
-    pull_stage(step, state_ref, turned_ref, d_ref, n_ref, upstream_ref, half_ref, total_ref)
+def pull_kernel(step, slope_ref, d_ref, upstream_ref, direct_ref, total_ref):
+    pull_stage(step, slope_ref, d_ref, upstream_ref, total_ref)
     dates, paths, _ = direct_ref.shape
     for t in range(dates):
         direct_ref[t] = total_ref[:, t * paths : (t + 1) * paths].T
 
 
-def pull_pass(dates, state, turned, d, n, upstream):
-    factors, rows = state.shape
-    trades = d.shape[1]
+def pull_pass(dates, slope, d, upstream):
+    trades, rows = slope.shape
+    factors = d.shape[0]
     vmem = pl.BlockSpec(memory_space=pltpu.VMEM)
     return pl.pallas_call(
         functools.partial(pull_kernel, min(2048, trades)),
-        in_specs=[vmem] * 5,
+        in_specs=[vmem] * 3,
         out_specs=vmem,
         out_shape=jax.ShapeDtypeStruct((dates, rows // dates, factors), f32),
-        scratch_shapes=pull_scratch(n.shape[0], factors, rows)[1:],
-        compiler_params=pltpu.CompilerParams(vmem_limit_bytes=32 << 20),
+        scratch_shapes=[pltpu.VMEM((factors, rows), f32)],
+        compiler_params=pltpu.CompilerParams(vmem_limit_bytes=16 << 20),
         name="pull_pass",
-    )(state, turned, d, n, upstream)
+    )(slope, d, upstream)
 
 
 def place_kernel(shards, me_ref, *refs):
@@ -445,14 +396,10 @@
     carried, x, rho_near = chain_pass(x, rho)
     arriving = swap(carried, ("date",), (2,), (1,))
     turned, n, facts = prepare_pass(d, n, mass, ceiling, obligor)
-    sums, (late_state, early_state) = first_value_pass(2, x, rho_near, arriving, date[None], facts, turned, n)
-    late_sums = [sums] + [over(sums, k) for k in range(1, shards)]
-    sums = value_pass(early_state, turned, n)
-    early_sums = [sums] + [over(sums, k) for k in range(1, shards)]
-    exposure, facts, late = late_pull_pass(dates, paths, cpty_dev, me, late_state, turned, d, n, late_sums)
-    exposure, chain = early_pull_pass(
-        dates, paths, cpty_dev, me, early_state, turned, d, n, rho_near, facts, exposure, late, early_sums
-    )
+    sums, state = value_pass(x, rho_near, arriving, date[None], facts, turned, n)
+    sums = [sums] + [over(sums, k) for k in range(1, shards)]
+    slope = slope_pass(state, turned, n)
+    exposure, chain = net_pull_pass(dates, cpty_dev, me, slope, d, rho_near, sums)
     total = functools.reduce(jnp.add, [chain[0]] + [over(chain[k], k) for k in range(1, shards)])
 
     message = swap(rho[0][None, :] * total[0], ("date",), (2,), (1,))
@@ -475,7 +422,7 @@
     identity = (jnp.ones_like(value[0]), jnp.zeros_like(value[1]))
     _, arriving = entering(value, "date", compose, identity, False)
     turned, n, facts = prepare_pass(d, n, mass, ceiling, obligor)
-    sums, (state,) = first_value_pass(1, x, rho, arriving, jnp.ones((1,), jnp.int32), facts, turned, n)
+    sums, state = value_pass(x, rho, arriving, jnp.ones((1,), jnp.int32), facts, turned, n)
     sums = sums[: n.shape[0]]
     cpties = cpty_dev * lax.axis_size("trade")
     ownership = (obligor[:, None] == jnp.arange(cpties, dtype=jnp.int32)[None, :]).astype(f32)
@@ -487,7 +434,7 @@
     adjoint = (mass.T[:, :, None] * jax.nn.sigmoid(shifted)).reshape(cpty_dev, rows)
     gathered = lax.all_gather(adjoint, "trade", axis=0, tiled=True)
     upstream = jnp.dot(ownership, gathered, precision=highest)
-    direct = lax.psum(pull_pass(dates, state, turned, d, n, upstream), "trade")
+    direct = lax.psum(pull_pass(dates, slope_pass(state, turned, n), d, upstream), "trade")
 
     gain = jnp.ones((factors,), f32)
     message = jnp.zeros((paths, factors), f32)

time: 55.3 us -> 55.1 us (level)
  waiting for transfers between devices: 12.4 us -> 19.8 us
  starting transfers between devices: 22.7 us -> 17.5 us
  Pallas kernels: 18.6 us -> 16.2 us
    ppermute x15 -> x12, waiting for transfers between devices: 12.4 us -> 19.8 us  [swap(): return lax.ppermute(value, axes, pairs)]
    ppermute x15 -> x12, starting transfers between devices: 22.7 us -> 17.5 us  [swap(): return lax.ppermute(value, axes, pairs)]
    pallas_call x4 -> x3, Pallas kernels: 15 us -> 12.6 us  [the longest x1 6.25 us: value_pass(): pl.pallas_call(functools.partial(value_kernel, min(VALUE_STEP, trades)),...]
  transfers between devices with their start and end apart: 15 -> 12, of which waited for: 7 -> 7; matrix products, arithmetic and copies ran while one was open for 1% -> 1% of each run, Pallas kernels for 17% -> 10%
where the time goes in v4:
time: 55.1 us; the launch traced here: 54.9 us
  waiting for transfers between devices  19.8 us (36%)
  starting transfers between devices  17.5 us (32%)
  Pallas kernels  16.2 us (29%)
  between operations  0.72 us (1%)
  other arithmetic  0.63 us (1%)
    ppermute x12, waiting for transfers between devices, swap(): return lax.ppermute(value, axes, pairs)  19.8 us
    ppermute x12, starting transfers between devices, swap(): return lax.ppermute(value, axes, pairs)  17.5 us
    pallas_call x1, Pallas kernels, value_pass(): pl.pallas_call(functools.partial(value_kernel, min(VALUE_STEP, trades)),...  6.25 us
    pallas_call x1, Pallas kernels, slope_pass(): pl.pallas_call(functools.partial(slope_kernel, min(2048, trades)), in_spe...  3.42 us
    pallas_call x1, Pallas kernels, net_pull_pass(): pl.pallas_call(functools.partial(net_pull_kernel, min(2048, trades), cpty...  2.92 us
    pallas_call x1, Pallas kernels, prepare_pass(): pl.pallas_call(functools.partial(prepare_kernel, step), in_specs=[hbm] *...  1.89 us
  transfers between devices with their start and end apart: 12, of which 7 were waited for; matrix products, arithmetic and copies ran while one was open for 1% of the time, Pallas kernels for 10%

profile of v4, /device:TPU:0, one launch (start us, length us, event | category | flops | bytes accessed | tf_op | source)
XLA Modules:
  0.0 54.9 jit_solution(4300925771013513947)
XLA Ops:
  0.6 1.0 %chain_pass.1 = (f32[128,128]{1,0:T(8,128)S(1)}, f32[4,128,128]{2,1,0:T(8,128)S(1)}, f32[4,128]{1,0:T(4,128)S(1)}) custom-call(f32[4,128,128]{2,1,0:T(8,128)} %x_hbm.1, f32[4,128]{1,0:T(4,128)} %rho_hbm.1), custom_call_target="tpu_custom_call" | custom-call | tf_op jit(solution)/shard_map/chain_pass/pallas_call | solution.py:76
  1.6 3.0 %collective-permute-start = (f32[128,128]{1,0:T(8,128)S(1)}, f32[128,128]{1,0:T(8,128)S(1)}, u32[]{:S(2)}, u32[]{:S(2)}) collective-permute-start(f32[128,128]{1,0:T(8,128)S(1)} %get-tuple-element.19), channel_id=1, source_target_pairs={{0,2},{2,0},{1,3},{3,1},{4,6},{6,4},{5,7},{7,5},{8,10},{10,8},{9,1... | collective-permute-start | bytes 196616 | tf_op jit(solution)/shard_map/ppermute | solution.py:29
  4.6 1.9 %prepare_pass.1 = (bf16[8192,128]{1,0:T(8,128)(2,1)S(1)}, f32[64,128]{1,0:T(8,128)S(1)}, f32[8,128]{1,0:T(8,128)S(1)}) custom-call(bf16[128,8192]{1,0:T(8,128)(2,1)} %d_ref.1, f32[64,128]{1,0:T(8,128)} %bitcast.11, f32[4,32]{1,0:T(4,128)} %mass_hbm.1, f32[1,32]{1,0:T(1,128)} %bitcast.12, s32[1,64]{1,0:T(1,128)} %bitcast.13), custom_call_target="tpu_custom_call" | custom-call | bytes 4194304 | tf_op jit(solution)/shard_map/prepare_pass/pallas_call | solution.py:121
  6.5 0.4 collective-permute-done.arriving_ref
  6.9 6.3 %value_pass.1 = (f32[72,512]{1,0:T(8,128)S(1)}, bf16[128,512]{1,0:T(8,128)(2,1)S(1)}) custom-call(f32[4,128,128]{2,1,0:T(8,128)S(1)} %get-tuple-element.17.x_ref, f32[4,128]{1,0:T(4,128)S(1)} %get-tuple-element.18.rho_ref, f32[128,128]{1,0:T(8,128)S(1)} %collective-permute-done.arriving_ref, s32[1]{0:T(128)} %bitcast.1.keep_ref, ...), custom_call_target="tpu_custom_call" | custom-call | flops 1073741824 | bytes 2097152 | tf_op jit(solution)/shard_map/value_pass/pallas_call | solution.py:168
  13.1 2.1 %collective-permute-start.1 = (f32[72,512]{1,0:T(8,128)S(1)}, f32[72,512]{1,0:T(8,128)S(1)}, u32[]{:S(2)}, u32[]{:S(2)}) collective-permute-start(f32[72,512]{1,0:T(8,128)S(1)} %get-tuple-element.24.refs_0_), channel_id=1, source_target_pairs={{0,4},{4,0},{8,12},{12,8},{1,5},{5,1},{9,13},{13,9},{2,6},{6,2},{1... | collective-permute-start | bytes 442376 | tf_op jit(solution)/shard_map/ppermute | solution.py:29
  15.3 2.5 %collective-permute-start.2 = (f32[72,512]{1,0:T(8,128)S(1)}, f32[72,512]{1,0:T(8,128)S(1)}, u32[]{:S(2)}, u32[]{:S(2)}) collective-permute-start(f32[72,512]{1,0:T(8,128)S(1)} %get-tuple-element.24.refs_0_), channel_id=1, source_target_pairs={{0,8},{4,12},{8,0},{12,4},{1,9},{5,13},{9,1},{13,5},{2,10},{6,14},... | collective-permute-start | bytes 442376 | tf_op jit(solution)/shard_map/ppermute | solution.py:29
  17.8 0.0 collective-permute-start.3
  17.8 3.4 %slope_pass.1.slope_ref = f32[8192,512]{1,0:T(8,128)S(1)} custom-call(bf16[128,512]{1,0:T(8,128)(2,1)S(1)} %get-tuple-element.23.state_ref, bf16[8192,128]{1,0:T(8,128)(2,1)S(1)} %get-tuple-element.21.turned_ref, f32[64,128]{1,0:T(8,128)S(1)} %get-tuple-element.22.n_ref), custom_call_target="tpu_custom_call" | custom-call | flops 1073741824 | bytes 16777216 | tf_op jit(solution)/shard_map/slope_pass/pallas_call | solution.py:203
  21.2 0.0 collective-permute-done.1.refs_1_
  21.3 7.0 %collective-permute-done.2.refs_2_ = f32[72,512]{1,0:T(8,128)S(1)} collective-permute-done((f32[72,512]{1,0:T(8,128)S(1)}, f32[72,512]{1,0:T(8,128)S(1)}, u32[]{:S(2)}, u32[]{:S(2)}) %collective-permute-start.2) | collective-permute-done | bytes 147488 | tf_op jit(solution)/shard_map/ppermute | solution.py:29
  28.3 0.0 collective-permute-done.3.refs_3_
  28.3 0.0 copy-done
  28.3 2.9 %net_pull_pass.1 = (f32[4,32]{1,0:T(4,128)S(1)}, f32[4,32,128]{2,1,0:T(8,128)S(1)}, f32[4,32,128]{2,1,0:T(8,128)S(1)}, f32[4,32,128]{2,1,0:T(8,128)S(1)}, f32[4,32,128]{2,1,0:T(8,128)S(1)}) custom-call(s32[1]{0:T(128)} %bitcast.me_ref, f32[8192,512]{1,0:T(8,128)S(1)} %slope_pass.1.slope_ref, bf16[128,8192]{1,0:T(8,128)(2,1)S(1)} %copy-done, ...), custom_call_target="tpu_custom_call" | custom-call | flops 1073741824 | bytes 16777216 | tf_op jit(solution)/shard_map/net_pull_pass/pallas_call | solution.py:310
  31.2 2.2 %collective-permute-start.4 = (f32[4,32,128]{2,1,0:T(8,128)S(1)}, f32[4,32,128]{2,1,0:T(8,128)S(1)}, u32[]{:S(2)}, u32[]{:S(2)}) collective-permute-start(f32[4,32,128]{2,1,0:T(8,128)S(1)} %get-tuple-element.26), channel_id=1, source_target_pairs={{0,4},{4,0},{8,12},{12,8},{1,5},{5,1},{9,13},{13,9},{2,6},{6,2},{1... | collective-permute-start | bytes 196616 | tf_op jit(solution)/shard_map/ppermute | solution.py:29
  33.4 1.0 %collective-permute-start.5 = (f32[4,32,128]{2,1,0:T(8,128)S(1)}, f32[4,32,128]{2,1,0:T(8,128)S(1)}, u32[]{:S(2)}, u32[]{:S(2)}) collective-permute-start(f32[4,32,128]{2,1,0:T(8,128)S(1)} %get-tuple-element.27), channel_id=1, source_target_pairs={{0,8},{4,12},{8,0},{12,4},{1,9},{5,13},{9,1},{13,5},{2,10},{6,14},... | collective-permute-start | bytes 196616 | tf_op jit(solution)/shard_map/ppermute | solution.py:29
  34.5 1.4 %collective-permute-start.6 = (f32[4,32,128]{2,1,0:T(8,128)S(1)}, f32[4,32,128]{2,1,0:T(8,128)S(1)}, u32[]{:S(2)}, u32[]{:S(2)}) collective-permute-start(f32[4,32,128]{2,1,0:T(8,128)S(1)} %get-tuple-element.28), channel_id=1, source_target_pairs={{0,12},{4,8},{8,4},{12,0},{1,13},{5,9},{9,5},{13,1},{2,14},{6,10},... | collective-permute-start | bytes 196616 | tf_op jit(solution)/shard_map/ppermute | solution.py:29
  35.9 0.0 collective-permute-done.4
  35.9 3.4 %collective-permute-done.5 = f32[4,32,128]{2,1,0:T(8,128)S(1)} collective-permute-done((f32[4,32,128]{2,1,0:T(8,128)S(1)}, f32[4,32,128]{2,1,0:T(8,128)S(1)}, u32[]{:S(2)}, u32[]{:S(2)}) %collective-permute-start.5) | collective-permute-done | bytes 65568 | tf_op jit(solution)/shard_map/ppermute | solution.py:29
  39.3 1.3 %collective-permute-done.6 = f32[4,32,128]{2,1,0:T(8,128)S(1)} collective-permute-done((f32[4,32,128]{2,1,0:T(8,128)S(1)}, f32[4,32,128]{2,1,0:T(8,128)S(1)}, u32[]{:S(2)}, u32[]{:S(2)}) %collective-permute-start.6) | collective-permute-done | bytes 65568 | tf_op jit(solution)/shard_map/ppermute | solution.py:29
  40.7 1.6 %collective-permute-start.7 = (f32[32,128]{1,0:T(8,128)S(1)}, f32[32,128]{1,0:T(8,128)S(1)}, u32[]{:S(2)}, u32[]{:S(2)}) collective-permute-start(f32[32,128]{1,0:T(8,128)S(1)} %fusion), channel_id=1, source_target_pairs={{0,2},{2,0},{1,3},{3,1},{4,6},{6,4},{5,7},{7,5},{8,10},{10,8},{9,1... | collective-permute-start | bytes 49160 | tf_op jit(solution)/shard_map/ppermute | solution.py:29
  42.3 2.2 %collective-permute-done.7 = f32[32,128]{1,0:T(8,128)S(1)} collective-permute-done((f32[32,128]{1,0:T(8,128)S(1)}, f32[32,128]{1,0:T(8,128)S(1)}, u32[]{:S(2)}, u32[]{:S(2)}) %collective-permute-start.7) | collective-permute-done | bytes 16416 | tf_op jit(solution)/shard_map/ppermute | solution.py:29
  44.5 0.1 collective-permute-start.8
  44.6 1.2 %collective-permute-start.10 = (f32[4,32,128]{2,1,0:T(8,128)S(1)}, f32[4,32,128]{2,1,0:T(8,128)S(1)}, u32[]{:S(2)}, u32[]{:S(2)}) collective-permute-start(f32[4,32,128]{2,1,0:T(8,128)S(1)} %multiply_add_fusion.refs_0_), channel_id=1, source_target_pairs={{0,8},{4,12},{8,0},{12,4},{1,9},{5,13},{9,1},{13,5},{2,10},{6,14},... | collective-permute-start | bytes 196616 | tf_op jit(solution)/shard_map/ppermute | solution.py:29
  45.7 2.0 %collective-permute-start.11 = (f32[4,32,128]{2,1,0:T(8,128)S(1)}, f32[4,32,128]{2,1,0:T(8,128)S(1)}, u32[]{:S(2)}, u32[]{:S(2)}) collective-permute-start(f32[4,32,128]{2,1,0:T(8,128)S(1)} %multiply_add_fusion.refs_0_), channel_id=1, source_target_pairs={{0,12},{4,8},{8,4},{12,0},{1,13},{5,9},{9,5},{13,1},{2,14},{6,10},... | collective-permute-start | bytes 196616 | tf_op jit(solution)/shard_map/ppermute | solution.py:29
  47.7 0.4 collective-permute-start.9
  48.1 0.0 collective-permute-done.8
  48.1 0.6 %add_multiply_fusion = f32[4,32]{1,0:T(4,128)} fusion(f32[4,32]{1,0:T(4,128)S(1)} %get-tuple-element.30, f32[4,32]{1,0:T(4,128)S(1)} %collective-permute-done.8), kind=kLoop, calls=%fused_computation.5 | loop fusion | flops 256 | bytes 1536 | tf_op jit(solution)/shard_map/div | solution.py:412
  48.7 4.4 %collective-permute-done.10.refs_2_ = f32[4,32,128]{2,1,0:T(8,128)S(1)} collective-permute-done((f32[4,32,128]{2,1,0:T(8,128)S(1)}, f32[4,32,128]{2,1,0:T(8,128)S(1)}, u32[]{:S(2)}, u32[]{:S(2)}) %collective-permute-start.10) | collective-permute-done | bytes 65568 | tf_op jit(solution)/shard_map/ppermute | solution.py:29
  53.1 0.0 collective-permute-done.11.refs_3_
  53.1 1.0 %collective-permute-done.9.refs_1_ = f32[4,32,128]{2,1,0:T(8,128)S(1)} collective-permute-done((f32[4,32,128]{2,1,0:T(8,128)S(1)}, f32[4,32,128]{2,1,0:T(8,128)S(1)}, u32[]{:S(2)}, u32[]{:S(2)}) %collective-permute-start.9) | collective-permute-done | bytes 65568 | tf_op jit(solution)/shard_map/ppermute | solution.py:29
  54.2 0.7 %place.1 = f32[4,128,128]{2,1,0:T(8,128)} custom-call(s32[1]{0:T(128)} %bitcast.me_ref, f32[4,32,128]{2,1,0:T(8,128)S(1)} %multiply_add_fusion.refs_0_, f32[4,32,128]{2,1,0:T(8,128)S(1)} %collective-permute-done.9.refs_1_, f32[4,32,128]{2,1,0:T(8,128)S(1)} %collective-permute-done.10.refs_2_, f32[4,32,128]{2,1,0:T(8,128)S(1)} %collective-permute-done.11.refs_3_), custom_call_target="tpu_custom_call" | custom-call | tf_op jit(solution)/shard_map/place/pallas_call | solution.py:364
  (9 shorter events, 0.1 us)
Async XLA Ops:
  1.6 5.2 %collective-permute-start = (f32[128,128]{1,0:T(8,128)S(1)}, f32[128,128]{1,0:T(8,128)S(1)}, u32[]{:S(2)}, u32[]{:S(2)}) collective-permute-start(f32[128,128]{1,0:T(8,128)S(1)} %get-tuple-element.19), channel_id=1, source_target_pairs={{0,2},{2,0},{1,3},{3,1},{4,6},{6,4},{5,7},{7,5},{8,10},{10,8},{9,1... | collective-permute-start | bytes 196616 | tf_op jit(solution)/shard_map/ppermute | solution.py:29
  13.1 8.1 %collective-permute-start.1 = (f32[72,512]{1,0:T(8,128)S(1)}, f32[72,512]{1,0:T(8,128)S(1)}, u32[]{:S(2)}, u32[]{:S(2)}) collective-permute-start(f32[72,512]{1,0:T(8,128)S(1)} %get-tuple-element.24.refs_0_), channel_id=1, source_target_pairs={{0,4},{4,0},{8,12},{12,8},{1,5},{5,1},{9,13},{13,9},{2,6},{6,2},{1... | collective-permute-start | bytes 442376 | tf_op jit(solution)/shard_map/ppermute | solution.py:29
  15.3 13.0 %collective-permute-start.2 = (f32[72,512]{1,0:T(8,128)S(1)}, f32[72,512]{1,0:T(8,128)S(1)}, u32[]{:S(2)}, u32[]{:S(2)}) collective-permute-start(f32[72,512]{1,0:T(8,128)S(1)} %get-tuple-element.24.refs_0_), channel_id=1, source_target_pairs={{0,8},{4,12},{8,0},{12,4},{1,9},{5,13},{9,1},{13,5},{2,10},{6,14},... | collective-permute-start | bytes 442376 | tf_op jit(solution)/shard_map/ppermute | solution.py:29
  17.8 10.5 %collective-permute-start.3 = (f32[72,512]{1,0:T(8,128)S(1)}, f32[72,512]{1,0:T(8,128)S(1)}, u32[]{:S(2)}, u32[]{:S(2)}) collective-permute-start(f32[72,512]{1,0:T(8,128)S(1)} %get-tuple-element.24.refs_0_), channel_id=1, source_target_pairs={{0,12},{4,8},{8,4},{12,0},{1,13},{5,9},{9,5},{13,1},{2,14},{6,10},... | collective-permute-start | bytes 442376 | tf_op jit(solution)/shard_map/ppermute | solution.py:29
  17.8 10.5 %copy-start = (bf16[128,8192]{1,0:T(8,128)(2,1)S(1)}, bf16[128,8192]{1,0:T(8,128)(2,1)}, u32[]{:S(2)}) copy-start(bf16[128,8192]{1,0:T(8,128)(2,1)} %d_ref.1) | copy-start | bytes 6291460
  28.3 7.6 %copy-start.1 = (f32[4,128]{1,0:T(4,128)S(1)}, f32[4,128]{1,0:T(4,128)}, u32[]{:S(2)}) copy-start(f32[4,128]{1,0:T(4,128)} %rho_hbm.1) | copy-start | bytes 6148
  31.2 4.7 %collective-permute-start.4 = (f32[4,32,128]{2,1,0:T(8,128)S(1)}, f32[4,32,128]{2,1,0:T(8,128)S(1)}, u32[]{:S(2)}, u32[]{:S(2)}) collective-permute-start(f32[4,32,128]{2,1,0:T(8,128)S(1)} %get-tuple-element.26), channel_id=1, source_target_pairs={{0,4},{4,0},{8,12},{12,8},{1,5},{5,1},{9,13},{13,9},{2,6},{6,2},{1... | collective-permute-start | bytes 196616 | tf_op jit(solution)/shard_map/ppermute | solution.py:29
  33.4 5.9 %collective-permute-start.5 = (f32[4,32,128]{2,1,0:T(8,128)S(1)}, f32[4,32,128]{2,1,0:T(8,128)S(1)}, u32[]{:S(2)}, u32[]{:S(2)}) collective-permute-start(f32[4,32,128]{2,1,0:T(8,128)S(1)} %get-tuple-element.27), channel_id=1, source_target_pairs={{0,8},{4,12},{8,0},{12,4},{1,9},{5,13},{9,1},{13,5},{2,10},{6,14},... | collective-permute-start | bytes 196616 | tf_op jit(solution)/shard_map/ppermute | solution.py:29
  34.5 6.2 %collective-permute-start.6 = (f32[4,32,128]{2,1,0:T(8,128)S(1)}, f32[4,32,128]{2,1,0:T(8,128)S(1)}, u32[]{:S(2)}, u32[]{:S(2)}) collective-permute-start(f32[4,32,128]{2,1,0:T(8,128)S(1)} %get-tuple-element.28), channel_id=1, source_target_pairs={{0,12},{4,8},{8,4},{12,0},{1,13},{5,9},{9,5},{13,1},{2,14},{6,10},... | collective-permute-start | bytes 196616 | tf_op jit(solution)/shard_map/ppermute | solution.py:29
  40.7 3.8 %collective-permute-start.7 = (f32[32,128]{1,0:T(8,128)S(1)}, f32[32,128]{1,0:T(8,128)S(1)}, u32[]{:S(2)}, u32[]{:S(2)}) collective-permute-start(f32[32,128]{1,0:T(8,128)S(1)} %fusion), channel_id=1, source_target_pairs={{0,2},{2,0},{1,3},{3,1},{4,6},{6,4},{5,7},{7,5},{8,10},{10,8},{9,1... | collective-permute-start | bytes 49160 | tf_op jit(solution)/shard_map/ppermute | solution.py:29
  44.5 3.6 %collective-permute-start.8 = (f32[4,32]{1,0:T(4,128)S(1)}, f32[4,32]{1,0:T(4,128)S(1)}, u32[]{:S(2)}, u32[]{:S(2)}) collective-permute-start(f32[4,32]{1,0:T(4,128)S(1)} %get-tuple-element.30), channel_id=1, source_target_pairs={{0,1},{1,0},{2,3},{3,2},{4,5},{5,4},{6,7},{7,6},{8,9},{9,8},{10,11... | collective-permute-start | bytes 1544 | tf_op jit(solution)/shard_map/ppermute | solution.py:29
  44.6 8.5 %collective-permute-start.10 = (f32[4,32,128]{2,1,0:T(8,128)S(1)}, f32[4,32,128]{2,1,0:T(8,128)S(1)}, u32[]{:S(2)}, u32[]{:S(2)}) collective-permute-start(f32[4,32,128]{2,1,0:T(8,128)S(1)} %multiply_add_fusion.refs_0_), channel_id=1, source_target_pairs={{0,8},{4,12},{8,0},{12,4},{1,9},{5,13},{9,1},{13,5},{2,10},{6,14},... | collective-permute-start | bytes 196616 | tf_op jit(solution)/shard_map/ppermute | solution.py:29
  45.7 7.4 %collective-permute-start.11 = (f32[4,32,128]{2,1,0:T(8,128)S(1)}, f32[4,32,128]{2,1,0:T(8,128)S(1)}, u32[]{:S(2)}, u32[]{:S(2)}) collective-permute-start(f32[4,32,128]{2,1,0:T(8,128)S(1)} %multiply_add_fusion.refs_0_), channel_id=1, source_target_pairs={{0,12},{4,8},{8,4},{12,0},{1,13},{5,9},{9,5},{13,1},{2,14},{6,10},... | collective-permute-start | bytes 196616 | tf_op jit(solution)/shard_map/ppermute | solution.py:29
  47.7 6.4 %collective-permute-start.9 = (f32[4,32,128]{2,1,0:T(8,128)S(1)}, f32[4,32,128]{2,1,0:T(8,128)S(1)}, u32[]{:S(2)}, u32[]{:S(2)}) collective-permute-start(f32[4,32,128]{2,1,0:T(8,128)S(1)} %multiply_add_fusion.refs_0_), channel_id=1, source_target_pairs={{0,4},{4,0},{8,12},{12,8},{1,5},{5,1},{9,13},{13,9},{2,6},{6,2},{1... | collective-permute-start | bytes 196616 | tf_op jit(solution)/shard_map/ppermute | solution.py:29

commit v5 on v4

--- a/solution.py
+++ b/solution.py
@@ -12,6 +12,8 @@
 f32 = jnp.float32
 bf16 = jnp.bfloat16
 VALUE_STEP = 2048
+SUMS_ORDER = (0, 3, 1, 2)
+PLACE_ORDER = (0, 1, 3, 2)
 
 
 def swap(value, axes, sizes, flips):
@@ -147,7 +149,9 @@
     for t in range(dates):
         carried = rho_ref[t : t + 1, :] * carried + x_ref[t]
         state_ref[:, t * paths : (t + 1) * paths] = carried.T.astype(bf16)
-    sums_ref[n_ref.shape[0] :, :128] = facts_ref[...]
+    total = n_ref.shape[0]
+    tiles = state_ref.shape[1] // 128
+    sums_ref[tiles * total :, :] = facts_ref[...]
 
     @pl.loop(0, turned_ref.shape[0] // step)
     def _(c):
@@ -158,7 +162,10 @@
         for b in range(blocks):
             value = softplus(linear[b * block_width : (b + 1) * block_width]) * size_t[:, b : b + 1]
             lines.append(jnp.sum(value, axis=0, keepdims=True))
-        sums_ref[pl.ds(pl.multiple_of(c * blocks, blocks), blocks), :] = jnp.concatenate(lines, axis=0)
+        sums = jnp.concatenate(lines, axis=0)
+        for q in range(tiles):
+            at = pl.ds(pl.multiple_of(q * total + c * blocks, blocks), blocks)
+            sums_ref[at, :] = sums[:, q * 128 : (q + 1) * 128]
 
 
 def value_pass(x, rho, arriving, keep, facts, turned, n):
@@ -170,7 +177,7 @@
         in_specs=[vmem, vmem, vmem, pl.BlockSpec(memory_space=pltpu.SMEM), vmem, vmem, vmem],
         out_specs=[vmem] * 2,
         out_shape=[
-            jax.ShapeDtypeStruct((n.shape[0] + 8, rows), f32),
+            jax.ShapeDtypeStruct((rows // 128 * n.shape[0] + 8, 128), f32),
             jax.ShapeDtypeStruct((factors, rows), bf16),
         ],
         compiler_params=pltpu.CompilerParams(vmem_limit_bytes=32 << 20),
@@ -235,12 +242,15 @@
         owner = owner.astype(jnp.int32)
         return (((owner >> shift) ^ me) << shift) + (owner & (cpty_dev - 1))
 
-    columns = [part[blocks : blocks + 8, :128].T for part in sums]
+    tiles = rows // 128
+    last = tiles * blocks
+    columns = [part[last:, :].T for part in sums]
     netted = None
     for k in range(shards):
-        row = label(sums[k][blocks + dates + 1 : blocks + dates + 2, :blocks])
+        row = label(sums[k][last + dates + 1 : last + dates + 2, :blocks])
         pick = lax.broadcasted_iota(jnp.int32, (cpties, blocks), 0) == row
-        part = split_dot(jnp.where(pick, 1.0, 0.0), sums[k][:blocks])
+        slabs = [sums[k][q * blocks : (q + 1) * blocks] for q in range(tiles)]
+        part = split_dot(jnp.where(pick, 1.0, 0.0), jnp.concatenate(slabs, axis=1))
         netted = part if netted is None else netted + part
     column = label(columns[0][:blocks, dates + 1 : dates + 2])
     own = jnp.where(lax.broadcasted_iota(jnp.int32, (blocks, cpties), 1) == column, 1.0, 0.0)
@@ -276,7 +286,7 @@
 
 
 def net_pull_kernel(step, cpty_dev, shards, me_ref, slope_ref, d_ref, rho_ref, *refs):
-    sums, refs = refs[:shards], refs[shards:]
+    sums, refs = [refs[SUMS_ORDER.index(k)] for k in range(shards)], refs[shards:]
     exposure_ref, refs = refs[0], refs[1:]
     chain, refs = refs[:shards], refs[shards:]
     upstream_ref, total_ref, chained_ref = refs
@@ -323,7 +333,7 @@
             flops=2 * rows * trades * factors, bytes_accessed=4 * trades * rows, transcendentals=0
         ),
         name="net_pull_pass",
-    )(me, slope, d, rho, *sums)
+    )(me, slope, d, rho, *[sums[k] for k in SUMS_ORDER])
     return out[0], out[1:]
 
 
@@ -350,7 +360,7 @@
 
 
 def place_kernel(shards, me_ref, *refs):
-    pieces, out_ref = refs[:shards], refs[shards]
+    pieces, out_ref = [refs[PLACE_ORDER.index(k)] for k in range(shards)], refs[shards]
     size = pieces[0].shape[1]
     for k in range(shards):
         at = pl.ds(pl.multiple_of((me_ref[0] ^ k) * size, size), size)
@@ -372,7 +382,7 @@
         out_shape=jax.ShapeDtypeStruct((dates, shards * size, factors), f32),
         compiler_params=pltpu.CompilerParams(vmem_limit_bytes=4 << 20),
         name="place",
-    )(me, *pieces)
+    )(me, *[pieces[k] for k in PLACE_ORDER])
 
 
 def local_chain(x, rho):
@@ -394,13 +404,17 @@
     over = lambda value, k: swap(value, ("trade",), (shards,), (k,))
 
     carried, x, rho_near = chain_pass(x, rho)
+    def spread(value):
+        return [value] + [over(value, k) for k in range(1, shards)]
+
+    carried, x, rho_near = chain_pass(x, rho)
     arriving = swap(carried, ("date",), (2,), (1,))
     turned, n, facts = prepare_pass(d, n, mass, ceiling, obligor)
     sums, state = value_pass(x, rho_near, arriving, date[None], facts, turned, n)
-    sums = [sums] + [over(sums, k) for k in range(1, shards)]
+    sums = spread(sums)
     slope = slope_pass(state, turned, n)
     exposure, chain = net_pull_pass(dates, cpty_dev, me, slope, d, rho_near, sums)
-    total = functools.reduce(jnp.add, [chain[0]] + [over(chain[k], k) for k in range(1, shards)])
+    total = chain[0] + over(chain[3], 3) + over(chain[2], 2) + over(chain[1], 1)
 
     message = swap(rho[0][None, :] * total[0], ("date",), (2,), (1,))
     weights = [jnp.where(date > 0, 0.0, jnp.ones((factors,), f32))]
@@ -408,7 +422,7 @@
         weights.append(rho[t] * weights[-1])
     own = total + jnp.stack(weights[::-1])[:, None, :] * message[None]
     own, exposure = lax.optimization_barrier((own, exposure))
-    pieces = [own] + [over(own, k) for k in range(1, shards)]
+    pieces = spread(own)
     exposure_profile = (exposure + swap(exposure, ("path",), (2,), (1,))) / (paths * lax.axis_size("path"))
     return exposure_profile, place(me, pieces)
 
@@ -423,7 +437,8 @@
     _, arriving = entering(value, "date", compose, identity, False)
     turned, n, facts = prepare_pass(d, n, mass, ceiling, obligor)
     sums, state = value_pass(x, rho, arriving, jnp.ones((1,), jnp.int32), facts, turned, n)
-    sums = sums[: n.shape[0]]
+    tiles = rows // 128
+    sums = sums[:-8].reshape(tiles, n.shape[0], 128).transpose(1, 0, 2).reshape(n.shape[0], rows)
     cpties = cpty_dev * lax.axis_size("trade")
     ownership = (obligor[:, None] == jnp.arange(cpties, dtype=jnp.int32)[None, :]).astype(f32)
     partial = lax.dot_general(ownership, sums, (((0,), (0,)), ((), ())), precision=highest)

time: 55.1 us -> 55 us (level)
  waiting for transfers between devices: 19.8 us -> 16.6 us
  Pallas kernels: 16.2 us -> 17.8 us
  starting transfers between devices: 17.5 us -> 18.4 us
  local copies, waits for them, and re-layouts: 0.01 us -> 0.71 us
    ppermute x12, waiting for transfers between devices: 19.8 us -> 16.6 us  [swap(): return lax.ppermute(value, axes, pairs)]
    pallas_call x1 -> x2, Pallas kernels: 0.99 us -> 2.6 us  [chain_pass(): pl.pallas_call(chain_kernel, in_specs=[pl.BlockSpec(memory_space=pltpu.HB...]
    ppermute x12, starting transfers between devices: 17.5 us -> 18.4 us  [swap(): return lax.ppermute(value, axes, pairs)]
    unnamed x4 -> x6, local copies, waits for them, and re-layouts: 0.01 us -> 0.7 us
  transfers between devices with their start and end apart: 12 -> 12, of which waited for: 7 -> 9; matrix products, arithmetic and copies ran while one was open for 1% -> 1% of each run, Pallas kernels for 10% -> 10%
where the time goes in v5:
time: 55 us; the launch traced here: 54.8 us
  starting transfers between devices  18.4 us (33%)
  Pallas kernels  17.8 us (32%)
  waiting for transfers between devices  16.6 us (30%)
  between operations  0.72 us (1%)
  local copies, waits for them, and re-layouts  0.71 us (1%)
  other arithmetic  0.63 us (1%)
    ppermute x12, starting transfers between devices, swap(): return lax.ppermute(value, axes, pairs)  18.4 us
    ppermute x12, waiting for transfers between devices, swap(): return lax.ppermute(value, axes, pairs)  16.6 us
    pallas_call x1, Pallas kernels, value_pass(): pl.pallas_call(functools.partial(value_kernel, min(VALUE_STEP, trades)),...  6.22 us
    pallas_call x1, Pallas kernels, slope_pass(): pl.pallas_call(functools.partial(slope_kernel, min(2048, trades)), in_spe...  3.4 us
    pallas_call x1, Pallas kernels, net_pull_pass(): pl.pallas_call(functools.partial(net_pull_kernel, min(2048, trades), cpty...  2.92 us
    pallas_call x2, Pallas kernels, chain_pass(): pl.pallas_call(chain_kernel, in_specs=[pl.BlockSpec(memory_space=pltpu.HB...  2.6 us
    pallas_call x1, Pallas kernels, prepare_pass(): pl.pallas_call(functools.partial(prepare_kernel, step), in_specs=[hbm] *...  1.89 us
  transfers between devices with their start and end apart: 12, of which 9 were waited for; matrix products, arithmetic and copies ran while one was open for 1% of the time, Pallas kernels for 10%

profile of v5, /device:TPU:0, one launch (start us, length us, event | category | flops | bytes accessed | tf_op | source)
XLA Modules:
  0.0 54.8 jit_solution(5396084621869821496)
XLA Ops:
  0.6 1.6 %chain_pass.2 = (f32[128,128]{1,0:T(8,128)}, f32[4,128,128]{2,1,0:T(8,128)S(1)}, f32[4,128]{1,0:T(4,128)}) custom-call(f32[4,128,128]{2,1,0:T(8,128)} %x_hbm.1, f32[4,128]{1,0:T(4,128)} %rho_hbm.3), custom_call_target="tpu_custom_call" | custom-call | tf_op jit(solution)/shard_map/chain_pass/pallas_call | solution.py:78
  2.3 0.0 copy-start.1
  2.3 0.7 %copy-done.1 = f32[4,128,128]{2,1,0:T(8,128)} copy-done((f32[4,128,128]{2,1,0:T(8,128)}, f32[4,128,128]{2,1,0:T(8,128)S(1)}, u32[]{:S(2)}) %copy-start.1) | copy-done | bytes 262168
  3.0 1.0 %chain_pass.3 = (f32[128,128]{1,0:T(8,128)S(1)}, f32[4,128,128]{2,1,0:T(8,128)S(1)}, f32[4,128]{1,0:T(4,128)S(1)}) custom-call(f32[4,128,128]{2,1,0:T(8,128)} %copy-done.1, f32[4,128]{1,0:T(4,128)} %rho_hbm.3), custom_call_target="tpu_custom_call" | custom-call | tf_op jit(solution)/shard_map/chain_pass/pallas_call | solution.py:78
  3.9 3.0 %collective-permute-start = (f32[128,128]{1,0:T(8,128)S(1)}, f32[128,128]{1,0:T(8,128)S(1)}, u32[]{:S(2)}, u32[]{:S(2)}) collective-permute-start(f32[128,128]{1,0:T(8,128)S(1)} %get-tuple-element.21), channel_id=1, source_target_pairs={{0,2},{2,0},{1,3},{3,1},{4,6},{6,4},{5,7},{7,5},{8,10},{10,8},{9,1... | collective-permute-start | bytes 196616 | tf_op jit(solution)/shard_map/ppermute | solution.py:31
  7.0 1.9 %prepare_pass.1 = (bf16[8192,128]{1,0:T(8,128)(2,1)S(1)}, f32[64,128]{1,0:T(8,128)S(1)}, f32[8,128]{1,0:T(8,128)S(1)}) custom-call(bf16[128,8192]{1,0:T(8,128)(2,1)} %d_ref.1, f32[64,128]{1,0:T(8,128)} %bitcast.11, f32[4,32]{1,0:T(4,128)} %mass_hbm.1, f32[1,32]{1,0:T(1,128)} %bitcast.12, s32[1,64]{1,0:T(1,128)} %bitcast.13), custom_call_target="tpu_custom_call" | custom-call | bytes 4194304 | tf_op jit(solution)/shard_map/prepare_pass/pallas_call | solution.py:123
  8.8 0.4 collective-permute-done.arriving_ref
  9.2 6.2 %value_pass.1 = (f32[264,128]{1,0:T(8,128)S(1)}, bf16[128,512]{1,0:T(8,128)(2,1)S(1)}) custom-call(f32[4,128,128]{2,1,0:T(8,128)S(1)} %get-tuple-element.19.x_ref, f32[4,128]{1,0:T(4,128)S(1)} %get-tuple-element.20.rho_ref, f32[128,128]{1,0:T(8,128)S(1)} %collective-permute-done.arriving_ref, s32[1]{0:T(128)} %bitcast.1.keep_ref, ...), custom_call_target="tpu_custom_call" | custom-call | flops 1073741824 | bytes 2097152 | tf_op jit(solution)/shard_map/value_pass/pallas_call | solution.py:175
  15.4 4.2 %collective-permute-start.1 = (f32[264,128]{1,0:T(8,128)S(1)}, f32[264,128]{1,0:T(8,128)S(1)}, u32[]{:S(2)}, u32[]{:S(2)}) collective-permute-start(f32[264,128]{1,0:T(8,128)S(1)} %get-tuple-element.26.refs_0_), channel_id=1, source_target_pairs={{0,12},{4,8},{8,4},{12,0},{1,13},{5,9},{9,5},{13,1},{2,14},{6,10},... | collective-permute-start | bytes 405512 | tf_op jit(solution)/shard_map/ppermute | solution.py:31
  19.6 0.0 collective-permute-start.2
  19.6 0.6 %collective-permute-start.3 = (f32[264,128]{1,0:T(8,128)S(1)}, f32[264,128]{1,0:T(8,128)S(1)}, u32[]{:S(2)}, u32[]{:S(2)}) collective-permute-start(f32[264,128]{1,0:T(8,128)S(1)} %get-tuple-element.26.refs_0_), channel_id=1, source_target_pairs={{0,8},{4,12},{8,0},{12,4},{1,9},{5,13},{9,1},{13,5},{2,10},{6,14},... | collective-permute-start | bytes 405512 | tf_op jit(solution)/shard_map/ppermute | solution.py:31
  20.3 3.4 %slope_pass.1.slope_ref = f32[8192,512]{1,0:T(8,128)S(1)} custom-call(bf16[128,512]{1,0:T(8,128)(2,1)S(1)} %get-tuple-element.25.state_ref, bf16[8192,128]{1,0:T(8,128)(2,1)S(1)} %get-tuple-element.23.turned_ref, f32[64,128]{1,0:T(8,128)S(1)} %get-tuple-element.24.n_ref), custom_call_target="tpu_custom_call" | custom-call | flops 1073741824 | bytes 16777216 | tf_op jit(solution)/shard_map/slope_pass/pallas_call | solution.py:210
  23.7 0.6 %collective-permute-done.1.refs_1_ = f32[264,128]{1,0:T(8,128)S(1)} collective-permute-done((f32[264,128]{1,0:T(8,128)S(1)}, f32[264,128]{1,0:T(8,128)S(1)}, u32[]{:S(2)}, u32[]{:S(2)}) %collective-permute-start.1) | collective-permute-done | bytes 135200 | tf_op jit(solution)/shard_map/ppermute | solution.py:31
  24.2 1.5 %collective-permute-done.2.refs_2_ = f32[264,128]{1,0:T(8,128)S(1)} collective-permute-done((f32[264,128]{1,0:T(8,128)S(1)}, f32[264,128]{1,0:T(8,128)S(1)}, u32[]{:S(2)}, u32[]{:S(2)}) %collective-permute-start.2) | collective-permute-done | bytes 135200 | tf_op jit(solution)/shard_map/ppermute | solution.py:31
  25.7 4.2 %collective-permute-done.3.refs_3_ = f32[264,128]{1,0:T(8,128)S(1)} collective-permute-done((f32[264,128]{1,0:T(8,128)S(1)}, f32[264,128]{1,0:T(8,128)S(1)}, u32[]{:S(2)}, u32[]{:S(2)}) %collective-permute-start.3) | collective-permute-done | bytes 135200 | tf_op jit(solution)/shard_map/ppermute | solution.py:31
  29.9 2.9 %net_pull_pass.1 = (f32[4,32]{1,0:T(4,128)S(1)}, f32[4,32,128]{2,1,0:T(8,128)S(1)}, f32[4,32,128]{2,1,0:T(8,128)S(1)}, f32[4,32,128]{2,1,0:T(8,128)S(1)}, f32[4,32,128]{2,1,0:T(8,128)S(1)}) custom-call(s32[1]{0:T(128)} %bitcast.me_ref, f32[8192,512]{1,0:T(8,128)S(1)} %slope_pass.1.slope_ref, bf16[128,8192]{1,0:T(8,128)(2,1)S(1)} %copy-done, ...), custom_call_target="tpu_custom_call" | custom-call | flops 1073741824 | bytes 16777216 | tf_op jit(solution)/shard_map/net_pull_pass/pallas_call | solution.py:320
  32.9 3.0 %collective-permute-start.4 = (f32[4,32,128]{2,1,0:T(8,128)S(1)}, f32[4,32,128]{2,1,0:T(8,128)S(1)}, u32[]{:S(2)}, u32[]{:S(2)}) collective-permute-start(f32[4,32,128]{2,1,0:T(8,128)S(1)} %get-tuple-element.28), channel_id=1, source_target_pairs={{0,12},{4,8},{8,4},{12,0},{1,13},{5,9},{9,5},{13,1},{2,14},{6,10},... | collective-permute-start | bytes 196616 | tf_op jit(solution)/shard_map/ppermute | solution.py:31
  35.9 0.0 collective-permute-start.5
  35.9 1.5 %collective-permute-start.6 = (f32[4,32,128]{2,1,0:T(8,128)S(1)}, f32[4,32,128]{2,1,0:T(8,128)S(1)}, u32[]{:S(2)}, u32[]{:S(2)}) collective-permute-start(f32[4,32,128]{2,1,0:T(8,128)S(1)} %get-tuple-element.30), channel_id=1, source_target_pairs={{0,4},{4,0},{8,12},{12,8},{1,5},{5,1},{9,13},{13,9},{2,6},{6,2},{1... | collective-permute-start | bytes 196616 | tf_op jit(solution)/shard_map/ppermute | solution.py:31
  37.3 2.0 %collective-permute-done.4 = f32[4,32,128]{2,1,0:T(8,128)S(1)} collective-permute-done((f32[4,32,128]{2,1,0:T(8,128)S(1)}, f32[4,32,128]{2,1,0:T(8,128)S(1)}, u32[]{:S(2)}, u32[]{:S(2)}) %collective-permute-start.4) | collective-permute-done | bytes 65568 | tf_op jit(solution)/shard_map/ppermute | solution.py:31
  39.3 1.7 %collective-permute-done.5 = f32[4,32,128]{2,1,0:T(8,128)S(1)} collective-permute-done((f32[4,32,128]{2,1,0:T(8,128)S(1)}, f32[4,32,128]{2,1,0:T(8,128)S(1)}, u32[]{:S(2)}, u32[]{:S(2)}) %collective-permute-start.5) | collective-permute-done | bytes 65568 | tf_op jit(solution)/shard_map/ppermute | solution.py:31
  41.0 0.0 collective-permute-done.6
  41.1 1.5 %collective-permute-start.7 = (f32[32,128]{1,0:T(8,128)S(1)}, f32[32,128]{1,0:T(8,128)S(1)}, u32[]{:S(2)}, u32[]{:S(2)}) collective-permute-start(f32[32,128]{1,0:T(8,128)S(1)} %fusion), channel_id=1, source_target_pairs={{0,2},{2,0},{1,3},{3,1},{4,6},{6,4},{5,7},{7,5},{8,10},{10,8},{9,1... | collective-permute-start | bytes 49160 | tf_op jit(solution)/shard_map/ppermute | solution.py:31
  42.6 2.2 %collective-permute-done.7 = f32[32,128]{1,0:T(8,128)S(1)} collective-permute-done((f32[32,128]{1,0:T(8,128)S(1)}, f32[32,128]{1,0:T(8,128)S(1)}, u32[]{:S(2)}, u32[]{:S(2)}) %collective-permute-start.7) | collective-permute-done | bytes 16416 | tf_op jit(solution)/shard_map/ppermute | solution.py:31
  44.9 0.1 collective-permute-start.8
  45.0 2.4 %collective-permute-start.10 = (f32[4,32,128]{2,1,0:T(8,128)S(1)}, f32[4,32,128]{2,1,0:T(8,128)S(1)}, u32[]{:S(2)}, u32[]{:S(2)}) collective-permute-start(f32[4,32,128]{2,1,0:T(8,128)S(1)} %multiply_add_fusion.refs_0_), channel_id=1, source_target_pairs={{0,12},{4,8},{8,4},{12,0},{1,13},{5,9},{9,5},{13,1},{2,14},{6,10},... | collective-permute-start | bytes 196616 | tf_op jit(solution)/shard_map/ppermute | solution.py:31
  47.3 0.0 collective-permute-start.11
  47.3 2.1 %collective-permute-start.9 = (f32[4,32,128]{2,1,0:T(8,128)S(1)}, f32[4,32,128]{2,1,0:T(8,128)S(1)}, u32[]{:S(2)}, u32[]{:S(2)}) collective-permute-start(f32[4,32,128]{2,1,0:T(8,128)S(1)} %multiply_add_fusion.refs_0_), channel_id=1, source_target_pairs={{0,4},{4,0},{8,12},{12,8},{1,5},{5,1},{9,13},{13,9},{2,6},{6,2},{1... | collective-permute-start | bytes 196616 | tf_op jit(solution)/shard_map/ppermute | solution.py:31
  49.4 0.6 %add_multiply_fusion = f32[4,32]{1,0:T(4,128)} fusion(f32[4,32]{1,0:T(4,128)S(1)} %get-tuple-element.32, f32[4,32]{1,0:T(4,128)S(1)} %collective-permute-done.8), kind=kLoop, calls=%fused_computation.5 | loop fusion | flops 256 | bytes 1536 | tf_op jit(solution)/shard_map/div | solution.py:426
  50.0 1.8 %collective-permute-done.10.refs_2_ = f32[4,32,128]{2,1,0:T(8,128)S(1)} collective-permute-done((f32[4,32,128]{2,1,0:T(8,128)S(1)}, f32[4,32,128]{2,1,0:T(8,128)S(1)}, u32[]{:S(2)}, u32[]{:S(2)}) %collective-permute-start.10) | collective-permute-done | bytes 65568 | tf_op jit(solution)/shard_map/ppermute | solution.py:31
  51.8 2.3 %collective-permute-done.11.refs_3_ = f32[4,32,128]{2,1,0:T(8,128)S(1)} collective-permute-done((f32[4,32,128]{2,1,0:T(8,128)S(1)}, f32[4,32,128]{2,1,0:T(8,128)S(1)}, u32[]{:S(2)}, u32[]{:S(2)}) %collective-permute-start.11) | collective-permute-done | bytes 65568 | tf_op jit(solution)/shard_map/ppermute | solution.py:31
  54.1 0.7 %place.1 = f32[4,128,128]{2,1,0:T(8,128)} custom-call(s32[1]{0:T(128)} %bitcast.me_ref, f32[4,32,128]{2,1,0:T(8,128)S(1)} %multiply_add_fusion.refs_0_, f32[4,32,128]{2,1,0:T(8,128)S(1)} %collective-permute-done.9.refs_1_, f32[4,32,128]{2,1,0:T(8,128)S(1)} %collective-permute-done.10.refs_2_, f32[4,32,128]{2,1,0:T(8,128)S(1)} %collective-permute-done.11.refs_3_), custom_call_target="tpu_custom_call" | custom-call | tf_op jit(solution)/shard_map/place/pallas_call | solution.py:374
  (12 shorter events, 0.1 us)
Async XLA Ops:
  2.3 0.7 %copy-start.1 = (f32[4,128,128]{2,1,0:T(8,128)}, f32[4,128,128]{2,1,0:T(8,128)S(1)}, u32[]{:S(2)}) copy-start(f32[4,128,128]{2,1,0:T(8,128)S(1)} %get-tuple-element.18.x_hbm) | copy-start | bytes 786436
  3.9 5.2 %collective-permute-start = (f32[128,128]{1,0:T(8,128)S(1)}, f32[128,128]{1,0:T(8,128)S(1)}, u32[]{:S(2)}, u32[]{:S(2)}) collective-permute-start(f32[128,128]{1,0:T(8,128)S(1)} %get-tuple-element.21), channel_id=1, source_target_pairs={{0,2},{2,0},{1,3},{3,1},{4,6},{6,4},{5,7},{7,5},{8,10},{10,8},{9,1... | collective-permute-start | bytes 196616 | tf_op jit(solution)/shard_map/ppermute | solution.py:31
  15.4 8.8 %collective-permute-start.1 = (f32[264,128]{1,0:T(8,128)S(1)}, f32[264,128]{1,0:T(8,128)S(1)}, u32[]{:S(2)}, u32[]{:S(2)}) collective-permute-start(f32[264,128]{1,0:T(8,128)S(1)} %get-tuple-element.26.refs_0_), channel_id=1, source_target_pairs={{0,12},{4,8},{8,4},{12,0},{1,13},{5,9},{9,5},{13,1},{2,14},{6,10},... | collective-permute-start | bytes 405512 | tf_op jit(solution)/shard_map/ppermute | solution.py:31
  19.6 6.1 %collective-permute-start.2 = (f32[264,128]{1,0:T(8,128)S(1)}, f32[264,128]{1,0:T(8,128)S(1)}, u32[]{:S(2)}, u32[]{:S(2)}) collective-permute-start(f32[264,128]{1,0:T(8,128)S(1)} %get-tuple-element.26.refs_0_), channel_id=1, source_target_pairs={{0,4},{4,0},{8,12},{12,8},{1,5},{5,1},{9,13},{13,9},{2,6},{6,2},{1... | collective-permute-start | bytes 405512 | tf_op jit(solution)/shard_map/ppermute | solution.py:31
  19.6 10.3 %collective-permute-start.3 = (f32[264,128]{1,0:T(8,128)S(1)}, f32[264,128]{1,0:T(8,128)S(1)}, u32[]{:S(2)}, u32[]{:S(2)}) collective-permute-start(f32[264,128]{1,0:T(8,128)S(1)} %get-tuple-element.26.refs_0_), channel_id=1, source_target_pairs={{0,8},{4,12},{8,0},{12,4},{1,9},{5,13},{9,1},{13,5},{2,10},{6,14},... | collective-permute-start | bytes 405512 | tf_op jit(solution)/shard_map/ppermute | solution.py:31
  20.3 9.7 %copy-start = (bf16[128,8192]{1,0:T(8,128)(2,1)S(1)}, bf16[128,8192]{1,0:T(8,128)(2,1)}, u32[]{:S(2)}) copy-start(bf16[128,8192]{1,0:T(8,128)(2,1)} %d_ref.1) | copy-start | bytes 6291460
  29.9 7.4 %copy-start.2 = (f32[4,128]{1,0:T(4,128)S(1)}, f32[4,128]{1,0:T(4,128)}, u32[]{:S(2)}) copy-start(f32[4,128]{1,0:T(4,128)} %rho_hbm.3) | copy-start | bytes 6148
  32.9 6.4 %collective-permute-start.4 = (f32[4,32,128]{2,1,0:T(8,128)S(1)}, f32[4,32,128]{2,1,0:T(8,128)S(1)}, u32[]{:S(2)}, u32[]{:S(2)}) collective-permute-start(f32[4,32,128]{2,1,0:T(8,128)S(1)} %get-tuple-element.28), channel_id=1, source_target_pairs={{0,12},{4,8},{8,4},{12,0},{1,13},{5,9},{9,5},{13,1},{2,14},{6,10},... | collective-permute-start | bytes 196616 | tf_op jit(solution)/shard_map/ppermute | solution.py:31
  35.9 5.2 %collective-permute-start.5 = (f32[4,32,128]{2,1,0:T(8,128)S(1)}, f32[4,32,128]{2,1,0:T(8,128)S(1)}, u32[]{:S(2)}, u32[]{:S(2)}) collective-permute-start(f32[4,32,128]{2,1,0:T(8,128)S(1)} %get-tuple-element.29), channel_id=1, source_target_pairs={{0,8},{4,12},{8,0},{12,4},{1,9},{5,13},{9,1},{13,5},{2,10},{6,14},... | collective-permute-start | bytes 196616 | tf_op jit(solution)/shard_map/ppermute | solution.py:31
  35.9 5.2 %collective-permute-start.6 = (f32[4,32,128]{2,1,0:T(8,128)S(1)}, f32[4,32,128]{2,1,0:T(8,128)S(1)}, u32[]{:S(2)}, u32[]{:S(2)}) collective-permute-start(f32[4,32,128]{2,1,0:T(8,128)S(1)} %get-tuple-element.30), channel_id=1, source_target_pairs={{0,4},{4,0},{8,12},{12,8},{1,5},{5,1},{9,13},{13,9},{2,6},{6,2},{1... | collective-permute-start | bytes 196616 | tf_op jit(solution)/shard_map/ppermute | solution.py:31
  41.1 3.8 %collective-permute-start.7 = (f32[32,128]{1,0:T(8,128)S(1)}, f32[32,128]{1,0:T(8,128)S(1)}, u32[]{:S(2)}, u32[]{:S(2)}) collective-permute-start(f32[32,128]{1,0:T(8,128)S(1)} %fusion), channel_id=1, source_target_pairs={{0,2},{2,0},{1,3},{3,1},{4,6},{6,4},{5,7},{7,5},{8,10},{10,8},{9,1... | collective-permute-start | bytes 49160 | tf_op jit(solution)/shard_map/ppermute | solution.py:31
  44.9 4.5 %collective-permute-start.8 = (f32[4,32]{1,0:T(4,128)S(1)}, f32[4,32]{1,0:T(4,128)S(1)}, u32[]{:S(2)}, u32[]{:S(2)}) collective-permute-start(f32[4,32]{1,0:T(4,128)S(1)} %get-tuple-element.32), channel_id=1, source_target_pairs={{0,1},{1,0},{2,3},{3,2},{4,5},{5,4},{6,7},{7,6},{8,9},{9,8},{10,11... | collective-permute-start | bytes 1544 | tf_op jit(solution)/shard_map/ppermute | solution.py:31
  45.0 6.8 %collective-permute-start.10 = (f32[4,32,128]{2,1,0:T(8,128)S(1)}, f32[4,32,128]{2,1,0:T(8,128)S(1)}, u32[]{:S(2)}, u32[]{:S(2)}) collective-permute-start(f32[4,32,128]{2,1,0:T(8,128)S(1)} %multiply_add_fusion.refs_0_), channel_id=1, source_target_pairs={{0,12},{4,8},{8,4},{12,0},{1,13},{5,9},{9,5},{13,1},{2,14},{6,10},... | collective-permute-start | bytes 196616 | tf_op jit(solution)/shard_map/ppermute | solution.py:31
  47.3 6.7 %collective-permute-start.11 = (f32[4,32,128]{2,1,0:T(8,128)S(1)}, f32[4,32,128]{2,1,0:T(8,128)S(1)}, u32[]{:S(2)}, u32[]{:S(2)}) collective-permute-start(f32[4,32,128]{2,1,0:T(8,128)S(1)} %multiply_add_fusion.refs_0_), channel_id=1, source_target_pairs={{0,8},{4,12},{8,0},{12,4},{1,9},{5,13},{9,1},{13,5},{2,10},{6,14},... | collective-permute-start | bytes 196616 | tf_op jit(solution)/shard_map/ppermute | solution.py:31
  47.3 6.7 %collective-permute-start.9 = (f32[4,32,128]{2,1,0:T(8,128)S(1)}, f32[4,32,128]{2,1,0:T(8,128)S(1)}, u32[]{:S(2)}, u32[]{:S(2)}) collective-permute-start(f32[4,32,128]{2,1,0:T(8,128)S(1)} %multiply_add_fusion.refs_0_), channel_id=1, source_target_pairs={{0,4},{4,0},{8,12},{12,8},{1,5},{5,1},{9,13},{13,9},{2,6},{6,2},{1... | collective-permute-start | bytes 196616 | tf_op jit(solution)/shard_map/ppermute | solution.py:31

commit v6 on v5

--- a/solution.py
+++ b/solution.py
@@ -13,7 +13,7 @@
 bf16 = jnp.bfloat16
 VALUE_STEP = 2048
 SUMS_ORDER = (0, 3, 1, 2)
-PLACE_ORDER = (0, 1, 3, 2)
+PLACE_ORDER = (0, 2, 1, 3)
 
 
 def swap(value, axes, sizes, flips):
@@ -359,30 +359,30 @@
     )(slope, d, upstream)
 
 
-def place_kernel(shards, me_ref, *refs):
-    pieces, out_ref = [refs[PLACE_ORDER.index(k)] for k in range(shards)], refs[shards]
+def place_kernel(shards, share, me_ref, exposure_ref, other_ref, *refs):
+    pieces, (profile_ref, out_ref) = [refs[PLACE_ORDER.index(k)] for k in range(shards)], refs[shards:]
     size = pieces[0].shape[1]
+    profile_ref[...] = (exposure_ref[...] + other_ref[...]) * share
     for k in range(shards):
         at = pl.ds(pl.multiple_of((me_ref[0] ^ k) * size, size), size)
         out_ref[:, at, :] = pieces[k][...]
 
 
-def place(me, pieces):
+def place(me, share, exposure, other, pieces):
     shards = len(pieces)
     dates, size, factors = pieces[0].shape
-    whole = lambda *shape: pl.BlockSpec(shape, lambda i, s: (0,) * len(shape))
-    return pl.pallas_call(
-        functools.partial(place_kernel, shards),
-        grid_spec=pltpu.PrefetchScalarGridSpec(
-            num_scalar_prefetch=1,
-            grid=(1,),
-            in_specs=[whole(dates, size, factors)] * shards,
-            out_specs=whole(dates, shards * size, factors),
-        ),
-        out_shape=jax.ShapeDtypeStruct((dates, shards * size, factors), f32),
+    vmem = pl.BlockSpec(memory_space=pltpu.VMEM)
+    return pl.pallas_call(
+        functools.partial(place_kernel, shards, share),
+        in_specs=[pl.BlockSpec(memory_space=pltpu.SMEM)] + [vmem] * (2 + shards),
+        out_specs=[vmem] * 2,
+        out_shape=[
+            jax.ShapeDtypeStruct(exposure.shape, f32),
+            jax.ShapeDtypeStruct((dates, shards * size, factors), f32),
+        ],
         compiler_params=pltpu.CompilerParams(vmem_limit_bytes=4 << 20),
         name="place",
-    )(me, *[pieces[k] for k in PLACE_ORDER])
+    )(me, exposure, other, *[pieces[k] for k in PLACE_ORDER])
 
 
 def local_chain(x, rho):
@@ -403,7 +403,6 @@
     date = lax.axis_index("date").astype(jnp.int32)
     over = lambda value, k: swap(value, ("trade",), (shards,), (k,))
 
-    carried, x, rho_near = chain_pass(x, rho)
     def spread(value):
         return [value] + [over(value, k) for k in range(1, shards)]
 
@@ -421,10 +420,11 @@
     for t in reversed(range(1, dates)):
         weights.append(rho[t] * weights[-1])
     own = total + jnp.stack(weights[::-1])[:, None, :] * message[None]
-    own, exposure = lax.optimization_barrier((own, exposure))
     pieces = spread(own)
-    exposure_profile = (exposure + swap(exposure, ("path",), (2,), (1,))) / (paths * lax.axis_size("path"))
-    return exposure_profile, place(me, pieces)
+    pieces[3], exposure = lax.optimization_barrier((pieces[3], exposure))
+    other = swap(exposure, ("path",), (2,), (1,))
+    profile, gradient = place(me, 1.0 / (paths * lax.axis_size("path")), exposure, other, pieces)
+    return profile, gradient
 
 
 def far(x, rho, d, size, obligor, ceiling, mass):

time: 55 us -> 51.4 us (0.935)
  Pallas kernels: 17.8 us -> 16.2 us
  local copies, waits for them, and re-layouts: 0.71 us -> 0.01 us
  waiting for transfers between devices: 16.6 us -> 16 us
  other arithmetic: 0.63 us -> 0.05 us
    pallas_call x2 -> x1, Pallas kernels: 2.6 us -> 0.99 us  [chain_pass(): pl.pallas_call(chain_kernel, in_specs=[pl.BlockSpec(memory_space=pltpu.HB...]
    unnamed x6 -> x4, local copies, waits for them, and re-layouts: 0.7 us -> 0.01 us
    ppermute x12, waiting for transfers between devices: 16.6 us -> 16 us  [swap(): return lax.ppermute(value, axes, pairs)]
    div x1 -> x0, other arithmetic: 0.58 us -> none  [near(): (exposure + swap(exposure, ('path',), (2,), (1,))) / (paths * lax.axis_si...]
  transfers between devices with their start and end apart: 12 -> 12, of which waited for: 9 -> 9; matrix products, arithmetic and copies ran while one was open for 1% -> 0% of each run, Pallas kernels for 10% -> 10%
where the time goes in v6:
time: 51.4 us; the launch traced here: 51.2 us
  starting transfers between devices  18.3 us (36%)
  Pallas kernels  16.2 us (32%)
  waiting for transfers between devices  16 us (31%)
  between operations  0.7 us (1%)
    ppermute x12, starting transfers between devices, swap(): return lax.ppermute(value, axes, pairs)  18.3 us
    ppermute x12, waiting for transfers between devices, swap(): return lax.ppermute(value, axes, pairs)  16 us
    pallas_call x1, Pallas kernels, value_pass(): pl.pallas_call(functools.partial(value_kernel, min(VALUE_STEP, trades)),...  6.23 us
    pallas_call x1, Pallas kernels, slope_pass(): pl.pallas_call(functools.partial(slope_kernel, min(2048, trades)), in_spe...  3.42 us
    pallas_call x1, Pallas kernels, net_pull_pass(): pl.pallas_call(functools.partial(net_pull_kernel, min(2048, trades), cpty...  2.92 us
    pallas_call x1, Pallas kernels, prepare_pass(): pl.pallas_call(functools.partial(prepare_kernel, step), in_specs=[hbm] *...  1.89 us
  transfers between devices with their start and end apart: 12, of which 9 were waited for; matrix products, arithmetic and copies ran while one was open for 0% of the time, Pallas kernels for 10%

profile of v6, /device:TPU:0, one launch (start us, length us, event | category | flops | bytes accessed | tf_op | source)
XLA Modules:
  0.0 51.2 jit_solution(13045805382797051262)
XLA Ops:
  0.6 1.0 %chain_pass.1 = (f32[128,128]{1,0:T(8,128)S(1)}, f32[4,128,128]{2,1,0:T(8,128)S(1)}, f32[4,128]{1,0:T(4,128)S(1)}) custom-call(f32[4,128,128]{2,1,0:T(8,128)} %x_hbm.1, f32[4,128]{1,0:T(4,128)} %rho_hbm.1), custom_call_target="tpu_custom_call" | custom-call | tf_op jit(solution)/shard_map/chain_pass/pallas_call | solution.py:78
  1.6 3.0 %collective-permute-start = (f32[128,128]{1,0:T(8,128)S(1)}, f32[128,128]{1,0:T(8,128)S(1)}, u32[]{:S(2)}, u32[]{:S(2)}) collective-permute-start(f32[128,128]{1,0:T(8,128)S(1)} %get-tuple-element.19), channel_id=1, source_target_pairs={{0,2},{2,0},{1,3},{3,1},{4,6},{6,4},{5,7},{7,5},{8,10},{10,8},{9,1... | collective-permute-start | bytes 196616 | tf_op jit(solution)/shard_map/ppermute | solution.py:31
  4.6 1.9 %prepare_pass.1 = (bf16[8192,128]{1,0:T(8,128)(2,1)S(1)}, f32[64,128]{1,0:T(8,128)S(1)}, f32[8,128]{1,0:T(8,128)S(1)}) custom-call(bf16[128,8192]{1,0:T(8,128)(2,1)} %d_ref.1, f32[64,128]{1,0:T(8,128)} %bitcast.11, f32[4,32]{1,0:T(4,128)} %mass_hbm.1, f32[1,32]{1,0:T(1,128)} %bitcast.12, s32[1,64]{1,0:T(1,128)} %bitcast.13), custom_call_target="tpu_custom_call" | custom-call | bytes 4194304 | tf_op jit(solution)/shard_map/prepare_pass/pallas_call | solution.py:123
  6.5 0.4 collective-permute-done.arriving_ref
  6.9 6.2 %value_pass.1 = (f32[264,128]{1,0:T(8,128)S(1)}, bf16[128,512]{1,0:T(8,128)(2,1)S(1)}) custom-call(f32[4,128,128]{2,1,0:T(8,128)S(1)} %get-tuple-element.17.x_ref, f32[4,128]{1,0:T(4,128)S(1)} %get-tuple-element.18.rho_ref, f32[128,128]{1,0:T(8,128)S(1)} %collective-permute-done.arriving_ref, s32[1]{0:T(128)} %bitcast.1.keep_ref, ...), custom_call_target="tpu_custom_call" | custom-call | flops 1073741824 | bytes 2097152 | tf_op jit(solution)/shard_map/value_pass/pallas_call | solution.py:175
  13.1 4.1 %collective-permute-start.1 = (f32[264,128]{1,0:T(8,128)S(1)}, f32[264,128]{1,0:T(8,128)S(1)}, u32[]{:S(2)}, u32[]{:S(2)}) collective-permute-start(f32[264,128]{1,0:T(8,128)S(1)} %get-tuple-element.24.refs_0_), channel_id=1, source_target_pairs={{0,12},{4,8},{8,4},{12,0},{1,13},{5,9},{9,5},{13,1},{2,14},{6,10},... | collective-permute-start | bytes 405512 | tf_op jit(solution)/shard_map/ppermute | solution.py:31
  17.3 0.0 collective-permute-start.2
  17.3 0.6 %collective-permute-start.3 = (f32[264,128]{1,0:T(8,128)S(1)}, f32[264,128]{1,0:T(8,128)S(1)}, u32[]{:S(2)}, u32[]{:S(2)}) collective-permute-start(f32[264,128]{1,0:T(8,128)S(1)} %get-tuple-element.24.refs_0_), channel_id=1, source_target_pairs={{0,8},{4,12},{8,0},{12,4},{1,9},{5,13},{9,1},{13,5},{2,10},{6,14},... | collective-permute-start | bytes 405512 | tf_op jit(solution)/shard_map/ppermute | solution.py:31
  17.9 3.4 %slope_pass.1.slope_ref = f32[8192,512]{1,0:T(8,128)S(1)} custom-call(bf16[128,512]{1,0:T(8,128)(2,1)S(1)} %get-tuple-element.23.state_ref, bf16[8192,128]{1,0:T(8,128)(2,1)S(1)} %get-tuple-element.21.turned_ref, f32[64,128]{1,0:T(8,128)S(1)} %get-tuple-element.22.n_ref), custom_call_target="tpu_custom_call" | custom-call | flops 1073741824 | bytes 16777216 | tf_op jit(solution)/shard_map/slope_pass/pallas_call | solution.py:210
  21.3 0.5 %collective-permute-done.1.refs_1_ = f32[264,128]{1,0:T(8,128)S(1)} collective-permute-done((f32[264,128]{1,0:T(8,128)S(1)}, f32[264,128]{1,0:T(8,128)S(1)}, u32[]{:S(2)}, u32[]{:S(2)}) %collective-permute-start.1) | collective-permute-done | bytes 135200 | tf_op jit(solution)/shard_map/ppermute | solution.py:31
  21.9 1.5 %collective-permute-done.2.refs_2_ = f32[264,128]{1,0:T(8,128)S(1)} collective-permute-done((f32[264,128]{1,0:T(8,128)S(1)}, f32[264,128]{1,0:T(8,128)S(1)}, u32[]{:S(2)}, u32[]{:S(2)}) %collective-permute-start.2) | collective-permute-done | bytes 135200 | tf_op jit(solution)/shard_map/ppermute | solution.py:31
  23.3 4.2 %collective-permute-done.3.refs_3_ = f32[264,128]{1,0:T(8,128)S(1)} collective-permute-done((f32[264,128]{1,0:T(8,128)S(1)}, f32[264,128]{1,0:T(8,128)S(1)}, u32[]{:S(2)}, u32[]{:S(2)}) %collective-permute-start.3) | collective-permute-done | bytes 135200 | tf_op jit(solution)/shard_map/ppermute | solution.py:31
  27.6 0.0 copy-done
  27.6 2.9 %net_pull_pass.1 = (f32[4,32]{1,0:T(4,128)S(1)}, f32[4,32,128]{2,1,0:T(8,128)S(1)}, f32[4,32,128]{2,1,0:T(8,128)S(1)}, f32[4,32,128]{2,1,0:T(8,128)S(1)}, f32[4,32,128]{2,1,0:T(8,128)S(1)}) custom-call(s32[1]{0:T(128)} %bitcast.me_ref, f32[8192,512]{1,0:T(8,128)S(1)} %slope_pass.1.slope_ref, bf16[128,8192]{1,0:T(8,128)(2,1)S(1)} %copy-done, ...), custom_call_target="tpu_custom_call" | custom-call | flops 1073741824 | bytes 16777216 | tf_op jit(solution)/shard_map/net_pull_pass/pallas_call | solution.py:320
  30.5 3.0 %collective-permute-start.4 = (f32[4,32,128]{2,1,0:T(8,128)S(1)}, f32[4,32,128]{2,1,0:T(8,128)S(1)}, u32[]{:S(2)}, u32[]{:S(2)}) collective-permute-start(f32[4,32,128]{2,1,0:T(8,128)S(1)} %get-tuple-element.26), channel_id=1, source_target_pairs={{0,12},{4,8},{8,4},{12,0},{1,13},{5,9},{9,5},{13,1},{2,14},{6,10},... | collective-permute-start | bytes 196616 | tf_op jit(solution)/shard_map/ppermute | solution.py:31
  33.5 0.0 collective-permute-start.5
  33.5 1.5 %collective-permute-start.6 = (f32[4,32,128]{2,1,0:T(8,128)S(1)}, f32[4,32,128]{2,1,0:T(8,128)S(1)}, u32[]{:S(2)}, u32[]{:S(2)}) collective-permute-start(f32[4,32,128]{2,1,0:T(8,128)S(1)} %get-tuple-element.28), channel_id=1, source_target_pairs={{0,4},{4,0},{8,12},{12,8},{1,5},{5,1},{9,13},{13,9},{2,6},{6,2},{1... | collective-permute-start | bytes 196616 | tf_op jit(solution)/shard_map/ppermute | solution.py:31
  35.0 0.0 copy-done.1
  35.0 2.0 %collective-permute-done.4 = f32[4,32,128]{2,1,0:T(8,128)S(1)} collective-permute-done((f32[4,32,128]{2,1,0:T(8,128)S(1)}, f32[4,32,128]{2,1,0:T(8,128)S(1)}, u32[]{:S(2)}, u32[]{:S(2)}) %collective-permute-start.4) | collective-permute-done | bytes 65568 | tf_op jit(solution)/shard_map/ppermute | solution.py:31
  37.0 1.7 %collective-permute-done.5 = f32[4,32,128]{2,1,0:T(8,128)S(1)} collective-permute-done((f32[4,32,128]{2,1,0:T(8,128)S(1)}, f32[4,32,128]{2,1,0:T(8,128)S(1)}, u32[]{:S(2)}, u32[]{:S(2)}) %collective-permute-start.5) | collective-permute-done | bytes 65568 | tf_op jit(solution)/shard_map/ppermute | solution.py:31
  38.6 0.0 collective-permute-done.6
  38.7 1.6 %collective-permute-start.7 = (f32[32,128]{1,0:T(8,128)S(1)}, f32[32,128]{1,0:T(8,128)S(1)}, u32[]{:S(2)}, u32[]{:S(2)}) collective-permute-start(f32[32,128]{1,0:T(8,128)S(1)} %fusion), channel_id=1, source_target_pairs={{0,2},{2,0},{1,3},{3,1},{4,6},{6,4},{5,7},{7,5},{8,10},{10,8},{9,1... | collective-permute-start | bytes 49160 | tf_op jit(solution)/shard_map/ppermute | solution.py:31
  40.3 2.2 %collective-permute-done.7 = f32[32,128]{1,0:T(8,128)S(1)} collective-permute-done((f32[32,128]{1,0:T(8,128)S(1)}, f32[32,128]{1,0:T(8,128)S(1)}, u32[]{:S(2)}, u32[]{:S(2)}) %collective-permute-start.7) | collective-permute-done | bytes 16416 | tf_op jit(solution)/shard_map/ppermute | solution.py:31
  42.5 2.4 %collective-permute-start.8 = (f32[4,32,128]{2,1,0:T(8,128)S(1)}, f32[4,32,128]{2,1,0:T(8,128)S(1)}, u32[]{:S(2)}, u32[]{:S(2)}) collective-permute-start(f32[4,32,128]{2,1,0:T(8,128)S(1)} %multiply_add_fusion.refs_0_), channel_id=1, source_target_pairs={{0,12},{4,8},{8,4},{12,0},{1,13},{5,9},{9,5},{13,1},{2,14},{6,10},... | collective-permute-start | bytes 196616 | tf_op jit(solution)/shard_map/ppermute | solution.py:31
  44.9 0.0 collective-permute-start.10
  44.9 2.1 %collective-permute-start.11 = (f32[4,32,128]{2,1,0:T(8,128)S(1)}, f32[4,32,128]{2,1,0:T(8,128)S(1)}, u32[]{:S(2)}, u32[]{:S(2)}) collective-permute-start(f32[4,32,128]{2,1,0:T(8,128)S(1)} %multiply_add_fusion.refs_0_), channel_id=1, source_target_pairs={{0,4},{4,0},{8,12},{12,8},{1,5},{5,1},{9,13},{13,9},{2,6},{6,2},{1... | collective-permute-start | bytes 196616 | tf_op jit(solution)/shard_map/ppermute | solution.py:31
  47.0 1.7 %collective-permute-done.8.refs_3_ = f32[4,32,128]{2,1,0:T(8,128)S(1)} collective-permute-done((f32[4,32,128]{2,1,0:T(8,128)S(1)}, f32[4,32,128]{2,1,0:T(8,128)S(1)}, u32[]{:S(2)}, u32[]{:S(2)}) %collective-permute-start.8) | collective-permute-done | bytes 65568 | tf_op jit(solution)/shard_map/ppermute | solution.py:31
  48.6 0.0 collective-permute-start.9
  48.6 1.8 %collective-permute-done.10.refs_1_ = f32[4,32,128]{2,1,0:T(8,128)S(1)} collective-permute-done((f32[4,32,128]{2,1,0:T(8,128)S(1)}, f32[4,32,128]{2,1,0:T(8,128)S(1)}, u32[]{:S(2)}, u32[]{:S(2)}) %collective-permute-start.10) | collective-permute-done | bytes 65568 | tf_op jit(solution)/shard_map/ppermute | solution.py:31
  50.5 0.0 collective-permute-done.11.refs_2_
  50.5 0.0 collective-permute-done.9.other_ref
  50.5 0.7 %place.1 = (f32[4,32]{1,0:T(4,128)}, f32[4,128,128]{2,1,0:T(8,128)}) custom-call(s32[1]{0:T(128)} %bitcast.me_ref, f32[4,32]{1,0:T(4,128)S(1)} %get-tuple-element.30.exposure_ref, f32[4,32]{1,0:T(4,128)S(1)} %collective-permute-done.9.other_ref, f32[4,32,128]{2,1,0:T(8,128)S(1)} %multiply_add_fusion.refs_0_, ...), custom_call_target="tpu_custom_call" | custom-call | tf_op jit(solution)/shard_map/place/pallas_call | solution.py:375
  (8 shorter events, 0.1 us)
Async XLA Ops:
  1.6 5.2 %collective-permute-start = (f32[128,128]{1,0:T(8,128)S(1)}, f32[128,128]{1,0:T(8,128)S(1)}, u32[]{:S(2)}, u32[]{:S(2)}) collective-permute-start(f32[128,128]{1,0:T(8,128)S(1)} %get-tuple-element.19), channel_id=1, source_target_pairs={{0,2},{2,0},{1,3},{3,1},{4,6},{6,4},{5,7},{7,5},{8,10},{10,8},{9,1... | collective-permute-start | bytes 196616 | tf_op jit(solution)/shard_map/ppermute | solution.py:31
  13.1 8.7 %collective-permute-start.1 = (f32[264,128]{1,0:T(8,128)S(1)}, f32[264,128]{1,0:T(8,128)S(1)}, u32[]{:S(2)}, u32[]{:S(2)}) collective-permute-start(f32[264,128]{1,0:T(8,128)S(1)} %get-tuple-element.24.refs_0_), channel_id=1, source_target_pairs={{0,12},{4,8},{8,4},{12,0},{1,13},{5,9},{9,5},{13,1},{2,14},{6,10},... | collective-permute-start | bytes 405512 | tf_op jit(solution)/shard_map/ppermute | solution.py:31
  17.3 6.1 %collective-permute-start.2 = (f32[264,128]{1,0:T(8,128)S(1)}, f32[264,128]{1,0:T(8,128)S(1)}, u32[]{:S(2)}, u32[]{:S(2)}) collective-permute-start(f32[264,128]{1,0:T(8,128)S(1)} %get-tuple-element.24.refs_0_), channel_id=1, source_target_pairs={{0,4},{4,0},{8,12},{12,8},{1,5},{5,1},{9,13},{13,9},{2,6},{6,2},{1... | collective-permute-start | bytes 405512 | tf_op jit(solution)/shard_map/ppermute | solution.py:31
  17.3 10.3 %collective-permute-start.3 = (f32[264,128]{1,0:T(8,128)S(1)}, f32[264,128]{1,0:T(8,128)S(1)}, u32[]{:S(2)}, u32[]{:S(2)}) collective-permute-start(f32[264,128]{1,0:T(8,128)S(1)} %get-tuple-element.24.refs_0_), channel_id=1, source_target_pairs={{0,8},{4,12},{8,0},{12,4},{1,9},{5,13},{9,1},{13,5},{2,10},{6,14},... | collective-permute-start | bytes 405512 | tf_op jit(solution)/shard_map/ppermute | solution.py:31
  17.9 9.7 %copy-start = (bf16[128,8192]{1,0:T(8,128)(2,1)S(1)}, bf16[128,8192]{1,0:T(8,128)(2,1)}, u32[]{:S(2)}) copy-start(bf16[128,8192]{1,0:T(8,128)(2,1)} %d_ref.1) | copy-start | bytes 6291460
  27.6 7.4 %copy-start.1 = (f32[4,128]{1,0:T(4,128)S(1)}, f32[4,128]{1,0:T(4,128)}, u32[]{:S(2)}) copy-start(f32[4,128]{1,0:T(4,128)} %rho_hbm.1) | copy-start | bytes 6148
  30.5 6.5 %collective-permute-start.4 = (f32[4,32,128]{2,1,0:T(8,128)S(1)}, f32[4,32,128]{2,1,0:T(8,128)S(1)}, u32[]{:S(2)}, u32[]{:S(2)}) collective-permute-start(f32[4,32,128]{2,1,0:T(8,128)S(1)} %get-tuple-element.26), channel_id=1, source_target_pairs={{0,12},{4,8},{8,4},{12,0},{1,13},{5,9},{9,5},{13,1},{2,14},{6,10},... | collective-permute-start | bytes 196616 | tf_op jit(solution)/shard_map/ppermute | solution.py:31
  33.5 5.2 %collective-permute-start.5 = (f32[4,32,128]{2,1,0:T(8,128)S(1)}, f32[4,32,128]{2,1,0:T(8,128)S(1)}, u32[]{:S(2)}, u32[]{:S(2)}) collective-permute-start(f32[4,32,128]{2,1,0:T(8,128)S(1)} %get-tuple-element.27), channel_id=1, source_target_pairs={{0,8},{4,12},{8,0},{12,4},{1,9},{5,13},{9,1},{13,5},{2,10},{6,14},... | collective-permute-start | bytes 196616 | tf_op jit(solution)/shard_map/ppermute | solution.py:31
  33.5 5.2 %collective-permute-start.6 = (f32[4,32,128]{2,1,0:T(8,128)S(1)}, f32[4,32,128]{2,1,0:T(8,128)S(1)}, u32[]{:S(2)}, u32[]{:S(2)}) collective-permute-start(f32[4,32,128]{2,1,0:T(8,128)S(1)} %get-tuple-element.28), channel_id=1, source_target_pairs={{0,4},{4,0},{8,12},{12,8},{1,5},{5,1},{9,13},{13,9},{2,6},{6,2},{1... | collective-permute-start | bytes 196616 | tf_op jit(solution)/shard_map/ppermute | solution.py:31
  38.7 3.8 %collective-permute-start.7 = (f32[32,128]{1,0:T(8,128)S(1)}, f32[32,128]{1,0:T(8,128)S(1)}, u32[]{:S(2)}, u32[]{:S(2)}) collective-permute-start(f32[32,128]{1,0:T(8,128)S(1)} %fusion), channel_id=1, source_target_pairs={{0,2},{2,0},{1,3},{3,1},{4,6},{6,4},{5,7},{7,5},{8,10},{10,8},{9,1... | collective-permute-start | bytes 49160 | tf_op jit(solution)/shard_map/ppermute | solution.py:31
  42.5 6.1 %collective-permute-start.8 = (f32[4,32,128]{2,1,0:T(8,128)S(1)}, f32[4,32,128]{2,1,0:T(8,128)S(1)}, u32[]{:S(2)}, u32[]{:S(2)}) collective-permute-start(f32[4,32,128]{2,1,0:T(8,128)S(1)} %multiply_add_fusion.refs_0_), channel_id=1, source_target_pairs={{0,12},{4,8},{8,4},{12,0},{1,13},{5,9},{9,5},{13,1},{2,14},{6,10},... | collective-permute-start | bytes 196616 | tf_op jit(solution)/shard_map/ppermute | solution.py:31
  44.9 5.6 %collective-permute-start.10 = (f32[4,32,128]{2,1,0:T(8,128)S(1)}, f32[4,32,128]{2,1,0:T(8,128)S(1)}, u32[]{:S(2)}, u32[]{:S(2)}) collective-permute-start(f32[4,32,128]{2,1,0:T(8,128)S(1)} %multiply_add_fusion.refs_0_), channel_id=1, source_target_pairs={{0,8},{4,12},{8,0},{12,4},{1,9},{5,13},{9,1},{13,5},{2,10},{6,14},... | collective-permute-start | bytes 196616 | tf_op jit(solution)/shard_map/ppermute | solution.py:31
  44.9 5.6 %collective-permute-start.11 = (f32[4,32,128]{2,1,0:T(8,128)S(1)}, f32[4,32,128]{2,1,0:T(8,128)S(1)}, u32[]{:S(2)}, u32[]{:S(2)}) collective-permute-start(f32[4,32,128]{2,1,0:T(8,128)S(1)} %multiply_add_fusion.refs_0_), channel_id=1, source_target_pairs={{0,4},{4,0},{8,12},{12,8},{1,5},{5,1},{9,13},{13,9},{2,6},{6,2},{1... | collective-permute-start | bytes 196616 | tf_op jit(solution)/shard_map/ppermute | solution.py:31
  48.6 1.8 %collective-permute-start.9 = (f32[4,32]{1,0:T(4,128)S(1)}, f32[4,32]{1,0:T(4,128)S(1)}, u32[]{:S(2)}, u32[]{:S(2)}) collective-permute-start(f32[4,32]{1,0:T(4,128)S(1)} %get-tuple-element.30.exposure_ref), channel_id=1, source_target_pairs={{0,1},{1,0},{2,3},{3,2},{4,5},{5,4},{6,7},{7,6},{8,9},{9,8},{10,11... | collective-permute-start | bytes 1544 | tf_op jit(solution)/shard_map/ppermute | solution.py:31

commit v7 on v6

--- a/solution.py
+++ b/solution.py
@@ -11,8 +11,9 @@
 highest = lax.Precision.HIGHEST
 f32 = jnp.float32
 bf16 = jnp.bfloat16
-VALUE_STEP = 2048
-SUMS_ORDER = (0, 3, 1, 2)
+VALUE_STEP = 8192
+PULL_STEP = 8192
+SUMS_ORDER = (0, 3, 2, 1)
 PLACE_ORDER = (0, 2, 1, 3)
 
 
@@ -318,7 +319,7 @@
     piece = paths // shards
     vmem = pl.BlockSpec(memory_space=pltpu.VMEM)
     out = pl.pallas_call(
-        functools.partial(net_pull_kernel, min(2048, trades), cpty_dev, shards),
+        functools.partial(net_pull_kernel, min(PULL_STEP, trades), cpty_dev, shards),
         in_specs=[pl.BlockSpec(memory_space=pltpu.SMEM)] + [vmem] * (3 + shards),
         out_specs=[vmem] * (1 + shards),
         out_shape=[jax.ShapeDtypeStruct((dates, cpty_dev), f32)]

time: 51.4 us -> 49.7 us (0.967)
  Pallas kernels: 16.2 us -> 14.9 us
    pallas_call x1, Pallas kernels: 6.23 us -> 5.6 us  [value_pass(): pl.pallas_call(functools.partial(value_kernel, min(VALUE_STEP, trades)),...]
    pallas_call x1, Pallas kernels: 2.92 us -> 2.3 us  [net_pull_pass(): pl.pallas_call(functools.partial(net_pull_kernel, min(PULL_STEP, trades),...]
  transfers between devices with their start and end apart: 12 -> 12, of which waited for: 9 -> 8; matrix products, arithmetic and copies ran while one was open for 0% -> 0% of each run, Pallas kernels for 10% -> 11%
where the time goes in v7:
time: 49.7 us; the launch traced here: 49.5 us
  starting transfers between devices  18.3 us (37%)
  waiting for transfers between devices  15.6 us (31%)
  Pallas kernels  14.9 us (30%)
  between operations  0.7 us (1%)
    ppermute x12, starting transfers between devices, swap(): return lax.ppermute(value, axes, pairs)  18.3 us
    ppermute x12, waiting for transfers between devices, swap(): return lax.ppermute(value, axes, pairs)  15.6 us
    pallas_call x1, Pallas kernels, value_pass(): pl.pallas_call(functools.partial(value_kernel, min(VALUE_STEP, trades)),...  5.6 us
    pallas_call x1, Pallas kernels, slope_pass(): pl.pallas_call(functools.partial(slope_kernel, min(2048, trades)), in_spe...  3.39 us
    pallas_call x1, Pallas kernels, net_pull_pass(): pl.pallas_call(functools.partial(net_pull_kernel, min(PULL_STEP, trades),...  2.3 us
    pallas_call x1, Pallas kernels, prepare_pass(): pl.pallas_call(functools.partial(prepare_kernel, step), in_specs=[hbm] *...  1.89 us
  transfers between devices with their start and end apart: 12, of which 8 were waited for; matrix products, arithmetic and copies ran while one was open for 0% of the time, Pallas kernels for 11%

profile of v7, /device:TPU:0, one launch (start us, length us, event | category | flops | bytes accessed | tf_op | source)
XLA Modules:
  0.0 49.5 jit_solution(12230428488727624320)
XLA Ops:
  0.6 1.0 %chain_pass.1 = (f32[128,128]{1,0:T(8,128)S(1)}, f32[4,128,128]{2,1,0:T(8,128)S(1)}, f32[4,128]{1,0:T(4,128)S(1)}) custom-call(f32[4,128,128]{2,1,0:T(8,128)} %x_hbm.1, f32[4,128]{1,0:T(4,128)} %rho_hbm.1), custom_call_target="tpu_custom_call" | custom-call | tf_op jit(solution)/shard_map/chain_pass/pallas_call | solution.py:79
  1.6 3.0 %collective-permute-start = (f32[128,128]{1,0:T(8,128)S(1)}, f32[128,128]{1,0:T(8,128)S(1)}, u32[]{:S(2)}, u32[]{:S(2)}) collective-permute-start(f32[128,128]{1,0:T(8,128)S(1)} %get-tuple-element.19), channel_id=1, source_target_pairs={{0,2},{2,0},{1,3},{3,1},{4,6},{6,4},{5,7},{7,5},{8,10},{10,8},{9,1... | collective-permute-start | bytes 196616 | tf_op jit(solution)/shard_map/ppermute | solution.py:32
  4.6 1.9 %prepare_pass.1 = (bf16[8192,128]{1,0:T(8,128)(2,1)S(1)}, f32[64,128]{1,0:T(8,128)S(1)}, f32[8,128]{1,0:T(8,128)S(1)}) custom-call(bf16[128,8192]{1,0:T(8,128)(2,1)} %d_ref.1, f32[64,128]{1,0:T(8,128)} %bitcast.11, f32[4,32]{1,0:T(4,128)} %mass_hbm.1, f32[1,32]{1,0:T(1,128)} %bitcast.12, s32[1,64]{1,0:T(1,128)} %bitcast.13), custom_call_target="tpu_custom_call" | custom-call | bytes 4194304 | tf_op jit(solution)/shard_map/prepare_pass/pallas_call | solution.py:124
  6.5 0.4 collective-permute-done.arriving_ref
  6.9 5.6 %value_pass.1 = (f32[264,128]{1,0:T(8,128)S(1)}, bf16[128,512]{1,0:T(8,128)(2,1)S(1)}) custom-call(f32[4,128,128]{2,1,0:T(8,128)S(1)} %get-tuple-element.17.x_ref, f32[4,128]{1,0:T(4,128)S(1)} %get-tuple-element.18.rho_ref, f32[128,128]{1,0:T(8,128)S(1)} %collective-permute-done.arriving_ref, s32[1]{0:T(128)} %bitcast.1.keep_ref, ...), custom_call_target="tpu_custom_call" | custom-call | flops 1073741824 | bytes 2097152 | tf_op jit(solution)/shard_map/value_pass/pallas_call | solution.py:176
  12.5 4.2 %collective-permute-start.1 = (f32[264,128]{1,0:T(8,128)S(1)}, f32[264,128]{1,0:T(8,128)S(1)}, u32[]{:S(2)}, u32[]{:S(2)}) collective-permute-start(f32[264,128]{1,0:T(8,128)S(1)} %get-tuple-element.24.refs_0_), channel_id=1, source_target_pairs={{0,12},{4,8},{8,4},{12,0},{1,13},{5,9},{9,5},{13,1},{2,14},{6,10},... | collective-permute-start | bytes 405512 | tf_op jit(solution)/shard_map/ppermute | solution.py:32
  16.7 0.0 collective-permute-start.2
  16.7 0.6 %collective-permute-start.3 = (f32[264,128]{1,0:T(8,128)S(1)}, f32[264,128]{1,0:T(8,128)S(1)}, u32[]{:S(2)}, u32[]{:S(2)}) collective-permute-start(f32[264,128]{1,0:T(8,128)S(1)} %get-tuple-element.24.refs_0_), channel_id=1, source_target_pairs={{0,4},{4,0},{8,12},{12,8},{1,5},{5,1},{9,13},{13,9},{2,6},{6,2},{1... | collective-permute-start | bytes 405512 | tf_op jit(solution)/shard_map/ppermute | solution.py:32
  17.3 3.4 %slope_pass.1.slope_ref = f32[8192,512]{1,0:T(8,128)S(1)} custom-call(bf16[128,512]{1,0:T(8,128)(2,1)S(1)} %get-tuple-element.23.state_ref, bf16[8192,128]{1,0:T(8,128)(2,1)S(1)} %get-tuple-element.21.turned_ref, f32[64,128]{1,0:T(8,128)S(1)} %get-tuple-element.22.n_ref), custom_call_target="tpu_custom_call" | custom-call | flops 1073741824 | bytes 16777216 | tf_op jit(solution)/shard_map/slope_pass/pallas_call | solution.py:211
  20.7 0.5 collective-permute-done.1.refs_1_
  21.2 5.8 %collective-permute-done.2.refs_2_ = f32[264,128]{1,0:T(8,128)S(1)} collective-permute-done((f32[264,128]{1,0:T(8,128)S(1)}, f32[264,128]{1,0:T(8,128)S(1)}, u32[]{:S(2)}, u32[]{:S(2)}) %collective-permute-start.2) | collective-permute-done | bytes 135200 | tf_op jit(solution)/shard_map/ppermute | solution.py:32
  27.0 0.0 collective-permute-done.3.refs_3_
  27.0 0.0 copy-done
  27.0 2.3 %net_pull_pass.1 = (f32[4,32]{1,0:T(4,128)S(1)}, f32[4,32,128]{2,1,0:T(8,128)S(1)}, f32[4,32,128]{2,1,0:T(8,128)S(1)}, f32[4,32,128]{2,1,0:T(8,128)S(1)}, f32[4,32,128]{2,1,0:T(8,128)S(1)}) custom-call(s32[1]{0:T(128)} %bitcast.me_ref, f32[8192,512]{1,0:T(8,128)S(1)} %slope_pass.1.slope_ref, bf16[128,8192]{1,0:T(8,128)(2,1)S(1)} %copy-done, ...), custom_call_target="tpu_custom_call" | custom-call | flops 1073741824 | bytes 16777216 | tf_op jit(solution)/shard_map/net_pull_pass/pallas_call | solution.py:321
  29.3 2.5 %collective-permute-start.4 = (f32[4,32,128]{2,1,0:T(8,128)S(1)}, f32[4,32,128]{2,1,0:T(8,128)S(1)}, u32[]{:S(2)}, u32[]{:S(2)}) collective-permute-start(f32[4,32,128]{2,1,0:T(8,128)S(1)} %get-tuple-element.26), channel_id=1, source_target_pairs={{0,12},{4,8},{8,4},{12,0},{1,13},{5,9},{9,5},{13,1},{2,14},{6,10},... | collective-permute-start | bytes 196616 | tf_op jit(solution)/shard_map/ppermute | solution.py:32
  31.8 0.0 collective-permute-start.5
  31.8 1.9 %collective-permute-start.6 = (f32[4,32,128]{2,1,0:T(8,128)S(1)}, f32[4,32,128]{2,1,0:T(8,128)S(1)}, u32[]{:S(2)}, u32[]{:S(2)}) collective-permute-start(f32[4,32,128]{2,1,0:T(8,128)S(1)} %get-tuple-element.28), channel_id=1, source_target_pairs={{0,4},{4,0},{8,12},{12,8},{1,5},{5,1},{9,13},{13,9},{2,6},{6,2},{1... | collective-permute-start | bytes 196616 | tf_op jit(solution)/shard_map/ppermute | solution.py:32
  33.7 0.0 copy-done.1
  33.7 2.0 %collective-permute-done.4 = f32[4,32,128]{2,1,0:T(8,128)S(1)} collective-permute-done((f32[4,32,128]{2,1,0:T(8,128)S(1)}, f32[4,32,128]{2,1,0:T(8,128)S(1)}, u32[]{:S(2)}, u32[]{:S(2)}) %collective-permute-start.4) | collective-permute-done | bytes 65568 | tf_op jit(solution)/shard_map/ppermute | solution.py:32
  35.7 1.4 %collective-permute-done.5 = f32[4,32,128]{2,1,0:T(8,128)S(1)} collective-permute-done((f32[4,32,128]{2,1,0:T(8,128)S(1)}, f32[4,32,128]{2,1,0:T(8,128)S(1)}, u32[]{:S(2)}, u32[]{:S(2)}) %collective-permute-start.5) | collective-permute-done | bytes 65568 | tf_op jit(solution)/shard_map/ppermute | solution.py:32
  37.1 0.0 collective-permute-done.6
  37.1 1.6 %collective-permute-start.7 = (f32[32,128]{1,0:T(8,128)S(1)}, f32[32,128]{1,0:T(8,128)S(1)}, u32[]{:S(2)}, u32[]{:S(2)}) collective-permute-start(f32[32,128]{1,0:T(8,128)S(1)} %fusion), channel_id=1, source_target_pairs={{0,2},{2,0},{1,3},{3,1},{4,6},{6,4},{5,7},{7,5},{8,10},{10,8},{9,1... | collective-permute-start | bytes 49160 | tf_op jit(solution)/shard_map/ppermute | solution.py:32
  38.7 2.2 %collective-permute-done.7 = f32[32,128]{1,0:T(8,128)S(1)} collective-permute-done((f32[32,128]{1,0:T(8,128)S(1)}, f32[32,128]{1,0:T(8,128)S(1)}, u32[]{:S(2)}, u32[]{:S(2)}) %collective-permute-start.7) | collective-permute-done | bytes 16416 | tf_op jit(solution)/shard_map/ppermute | solution.py:32
  41.0 2.4 %collective-permute-start.8 = (f32[4,32,128]{2,1,0:T(8,128)S(1)}, f32[4,32,128]{2,1,0:T(8,128)S(1)}, u32[]{:S(2)}, u32[]{:S(2)}) collective-permute-start(f32[4,32,128]{2,1,0:T(8,128)S(1)} %multiply_add_fusion.refs_0_), channel_id=1, source_target_pairs={{0,12},{4,8},{8,4},{12,0},{1,13},{5,9},{9,5},{13,1},{2,14},{6,10},... | collective-permute-start | bytes 196616 | tf_op jit(solution)/shard_map/ppermute | solution.py:32
  43.4 0.0 collective-permute-start.10
  43.4 2.0 %collective-permute-start.11 = (f32[4,32,128]{2,1,0:T(8,128)S(1)}, f32[4,32,128]{2,1,0:T(8,128)S(1)}, u32[]{:S(2)}, u32[]{:S(2)}) collective-permute-start(f32[4,32,128]{2,1,0:T(8,128)S(1)} %multiply_add_fusion.refs_0_), channel_id=1, source_target_pairs={{0,4},{4,0},{8,12},{12,8},{1,5},{5,1},{9,13},{13,9},{2,6},{6,2},{1... | collective-permute-start | bytes 196616 | tf_op jit(solution)/shard_map/ppermute | solution.py:32
  45.4 1.7 %collective-permute-done.8.refs_3_ = f32[4,32,128]{2,1,0:T(8,128)S(1)} collective-permute-done((f32[4,32,128]{2,1,0:T(8,128)S(1)}, f32[4,32,128]{2,1,0:T(8,128)S(1)}, u32[]{:S(2)}, u32[]{:S(2)}) %collective-permute-start.8) | collective-permute-done | bytes 65568 | tf_op jit(solution)/shard_map/ppermute | solution.py:32
  47.1 0.0 collective-permute-start.9
  47.1 1.7 %collective-permute-done.10.refs_1_ = f32[4,32,128]{2,1,0:T(8,128)S(1)} collective-permute-done((f32[4,32,128]{2,1,0:T(8,128)S(1)}, f32[4,32,128]{2,1,0:T(8,128)S(1)}, u32[]{:S(2)}, u32[]{:S(2)}) %collective-permute-start.10) | collective-permute-done | bytes 65568 | tf_op jit(solution)/shard_map/ppermute | solution.py:32
  48.8 0.0 collective-permute-done.11.refs_2_
  48.8 0.0 collective-permute-done.9.other_ref
  48.8 0.7 %place.1 = (f32[4,32]{1,0:T(4,128)}, f32[4,128,128]{2,1,0:T(8,128)}) custom-call(s32[1]{0:T(128)} %bitcast.me_ref, f32[4,32]{1,0:T(4,128)S(1)} %get-tuple-element.30.exposure_ref, f32[4,32]{1,0:T(4,128)S(1)} %collective-permute-done.9.other_ref, f32[4,32,128]{2,1,0:T(8,128)S(1)} %multiply_add_fusion.refs_0_, ...), custom_call_target="tpu_custom_call" | custom-call | tf_op jit(solution)/shard_map/place/pallas_call | solution.py:376
  (8 shorter events, 0.1 us)
Async XLA Ops:
  1.6 5.2 %collective-permute-start = (f32[128,128]{1,0:T(8,128)S(1)}, f32[128,128]{1,0:T(8,128)S(1)}, u32[]{:S(2)}, u32[]{:S(2)}) collective-permute-start(f32[128,128]{1,0:T(8,128)S(1)} %get-tuple-element.19), channel_id=1, source_target_pairs={{0,2},{2,0},{1,3},{3,1},{4,6},{6,4},{5,7},{7,5},{8,10},{10,8},{9,1... | collective-permute-start | bytes 196616 | tf_op jit(solution)/shard_map/ppermute | solution.py:32
  12.5 8.7 %collective-permute-start.1 = (f32[264,128]{1,0:T(8,128)S(1)}, f32[264,128]{1,0:T(8,128)S(1)}, u32[]{:S(2)}, u32[]{:S(2)}) collective-permute-start(f32[264,128]{1,0:T(8,128)S(1)} %get-tuple-element.24.refs_0_), channel_id=1, source_target_pairs={{0,12},{4,8},{8,4},{12,0},{1,13},{5,9},{9,5},{13,1},{2,14},{6,10},... | collective-permute-start | bytes 405512 | tf_op jit(solution)/shard_map/ppermute | solution.py:32
  16.7 10.3 %collective-permute-start.2 = (f32[264,128]{1,0:T(8,128)S(1)}, f32[264,128]{1,0:T(8,128)S(1)}, u32[]{:S(2)}, u32[]{:S(2)}) collective-permute-start(f32[264,128]{1,0:T(8,128)S(1)} %get-tuple-element.24.refs_0_), channel_id=1, source_target_pairs={{0,8},{4,12},{8,0},{12,4},{1,9},{5,13},{9,1},{13,5},{2,10},{6,14},... | collective-permute-start | bytes 405512 | tf_op jit(solution)/shard_map/ppermute | solution.py:32
  16.7 10.3 %collective-permute-start.3 = (f32[264,128]{1,0:T(8,128)S(1)}, f32[264,128]{1,0:T(8,128)S(1)}, u32[]{:S(2)}, u32[]{:S(2)}) collective-permute-start(f32[264,128]{1,0:T(8,128)S(1)} %get-tuple-element.24.refs_0_), channel_id=1, source_target_pairs={{0,4},{4,0},{8,12},{12,8},{1,5},{5,1},{9,13},{13,9},{2,6},{6,2},{1... | collective-permute-start | bytes 405512 | tf_op jit(solution)/shard_map/ppermute | solution.py:32
  17.3 9.6 %copy-start = (bf16[128,8192]{1,0:T(8,128)(2,1)S(1)}, bf16[128,8192]{1,0:T(8,128)(2,1)}, u32[]{:S(2)}) copy-start(bf16[128,8192]{1,0:T(8,128)(2,1)} %d_ref.1) | copy-start | bytes 6291460
  27.0 6.8 %copy-start.1 = (f32[4,128]{1,0:T(4,128)S(1)}, f32[4,128]{1,0:T(4,128)}, u32[]{:S(2)}) copy-start(f32[4,128]{1,0:T(4,128)} %rho_hbm.1) | copy-start | bytes 6148
  29.3 6.4 %collective-permute-start.4 = (f32[4,32,128]{2,1,0:T(8,128)S(1)}, f32[4,32,128]{2,1,0:T(8,128)S(1)}, u32[]{:S(2)}, u32[]{:S(2)}) collective-permute-start(f32[4,32,128]{2,1,0:T(8,128)S(1)} %get-tuple-element.26), channel_id=1, source_target_pairs={{0,12},{4,8},{8,4},{12,0},{1,13},{5,9},{9,5},{13,1},{2,14},{6,10},... | collective-permute-start | bytes 196616 | tf_op jit(solution)/shard_map/ppermute | solution.py:32
  31.8 5.3 %collective-permute-start.5 = (f32[4,32,128]{2,1,0:T(8,128)S(1)}, f32[4,32,128]{2,1,0:T(8,128)S(1)}, u32[]{:S(2)}, u32[]{:S(2)}) collective-permute-start(f32[4,32,128]{2,1,0:T(8,128)S(1)} %get-tuple-element.27), channel_id=1, source_target_pairs={{0,8},{4,12},{8,0},{12,4},{1,9},{5,13},{9,1},{13,5},{2,10},{6,14},... | collective-permute-start | bytes 196616 | tf_op jit(solution)/shard_map/ppermute | solution.py:32
  31.8 5.3 %collective-permute-start.6 = (f32[4,32,128]{2,1,0:T(8,128)S(1)}, f32[4,32,128]{2,1,0:T(8,128)S(1)}, u32[]{:S(2)}, u32[]{:S(2)}) collective-permute-start(f32[4,32,128]{2,1,0:T(8,128)S(1)} %get-tuple-element.28), channel_id=1, source_target_pairs={{0,4},{4,0},{8,12},{12,8},{1,5},{5,1},{9,13},{13,9},{2,6},{6,2},{1... | collective-permute-start | bytes 196616 | tf_op jit(solution)/shard_map/ppermute | solution.py:32
  37.1 3.8 %collective-permute-start.7 = (f32[32,128]{1,0:T(8,128)S(1)}, f32[32,128]{1,0:T(8,128)S(1)}, u32[]{:S(2)}, u32[]{:S(2)}) collective-permute-start(f32[32,128]{1,0:T(8,128)S(1)} %fusion), channel_id=1, source_target_pairs={{0,2},{2,0},{1,3},{3,1},{4,6},{6,4},{5,7},{7,5},{8,10},{10,8},{9,1... | collective-permute-start | bytes 49160 | tf_op jit(solution)/shard_map/ppermute | solution.py:32
  41.0 6.1 %collective-permute-start.8 = (f32[4,32,128]{2,1,0:T(8,128)S(1)}, f32[4,32,128]{2,1,0:T(8,128)S(1)}, u32[]{:S(2)}, u32[]{:S(2)}) collective-permute-start(f32[4,32,128]{2,1,0:T(8,128)S(1)} %multiply_add_fusion.refs_0_), channel_id=1, source_target_pairs={{0,12},{4,8},{8,4},{12,0},{1,13},{5,9},{9,5},{13,1},{2,14},{6,10},... | collective-permute-start | bytes 196616 | tf_op jit(solution)/shard_map/ppermute | solution.py:32
  43.4 5.4 %collective-permute-start.10 = (f32[4,32,128]{2,1,0:T(8,128)S(1)}, f32[4,32,128]{2,1,0:T(8,128)S(1)}, u32[]{:S(2)}, u32[]{:S(2)}) collective-permute-start(f32[4,32,128]{2,1,0:T(8,128)S(1)} %multiply_add_fusion.refs_0_), channel_id=1, source_target_pairs={{0,8},{4,12},{8,0},{12,4},{1,9},{5,13},{9,1},{13,5},{2,10},{6,14},... | collective-permute-start | bytes 196616 | tf_op jit(solution)/shard_map/ppermute | solution.py:32
  43.4 5.4 %collective-permute-start.11 = (f32[4,32,128]{2,1,0:T(8,128)S(1)}, f32[4,32,128]{2,1,0:T(8,128)S(1)}, u32[]{:S(2)}, u32[]{:S(2)}) collective-permute-start(f32[4,32,128]{2,1,0:T(8,128)S(1)} %multiply_add_fusion.refs_0_), channel_id=1, source_target_pairs={{0,4},{4,0},{8,12},{12,8},{1,5},{5,1},{9,13},{13,9},{2,6},{6,2},{1... | collective-permute-start | bytes 196616 | tf_op jit(solution)/shard_map/ppermute | solution.py:32
  47.1 1.7 %collective-permute-start.9 = (f32[4,32]{1,0:T(4,128)S(1)}, f32[4,32]{1,0:T(4,128)S(1)}, u32[]{:S(2)}, u32[]{:S(2)}) collective-permute-start(f32[4,32]{1,0:T(4,128)S(1)} %get-tuple-element.30.exposure_ref), channel_id=1, source_target_pairs={{0,1},{1,0},{2,3},{3,2},{4,5},{5,4},{6,7},{7,6},{8,9},{9,8},{10,11... | collective-permute-start | bytes 1544 | tf_op jit(solution)/shard_map/ppermute | solution.py:32

commit v8 on v7

--- a/solution.py
+++ b/solution.py
@@ -14,7 +14,7 @@
 VALUE_STEP = 8192
 PULL_STEP = 8192
 SUMS_ORDER = (0, 3, 2, 1)
-PLACE_ORDER = (0, 2, 1, 3)
+PLACE_ORDER = (0, 1, 3, 2)
 
 
 def swap(value, axes, sizes, flips):
@@ -414,7 +414,7 @@
     sums = spread(sums)
     slope = slope_pass(state, turned, n)
     exposure, chain = net_pull_pass(dates, cpty_dev, me, slope, d, rho_near, sums)
-    total = chain[0] + over(chain[3], 3) + over(chain[2], 2) + over(chain[1], 1)
+    total = chain[0] + over(chain[2], 2) + over(chain[3], 3) + over(chain[1], 1)
 
     message = swap(rho[0][None, :] * total[0], ("date",), (2,), (1,))
     weights = [jnp.where(date > 0, 0.0, jnp.ones((factors,), f32))]

time: 49.7 us -> 49.2 us (0.990)
  starting transfers between devices: 18.3 us -> 17.4 us
    ppermute x12, starting transfers between devices: 18.3 us -> 17.4 us  [swap(): return lax.ppermute(value, axes, pairs)]
where the time goes in v8:
time: 49.2 us; the launch traced here: 49 us
  starting transfers between devices  17.4 us (35%)
  waiting for transfers between devices  15.9 us (32%)
  Pallas kernels  14.9 us (30%)
  between operations  0.7 us (1%)
    ppermute x12, starting transfers between devices, swap(): return lax.ppermute(value, axes, pairs)  17.4 us
    ppermute x12, waiting for transfers between devices, swap(): return lax.ppermute(value, axes, pairs)  15.9 us
    pallas_call x1, Pallas kernels, value_pass(): pl.pallas_call(functools.partial(value_kernel, min(VALUE_STEP, trades)),...  5.6 us
    pallas_call x1, Pallas kernels, slope_pass(): pl.pallas_call(functools.partial(slope_kernel, min(2048, trades)), in_spe...  3.39 us
    pallas_call x1, Pallas kernels, net_pull_pass(): pl.pallas_call(functools.partial(net_pull_kernel, min(PULL_STEP, trades),...  2.3 us
    pallas_call x1, Pallas kernels, prepare_pass(): pl.pallas_call(functools.partial(prepare_kernel, step), in_specs=[hbm] *...  1.89 us
    pallas_call x1, Pallas kernels, chain_pass(): pl.pallas_call(chain_kernel, in_specs=[pl.BlockSpec(memory_space=pltpu.HB...  0.99 us
  transfers between devices with their start and end apart: 12, of which 8 were waited for; matrix products, arithmetic and copies ran while one was open for 0% of the time, Pallas kernels for 11%

profile of v8, /device:TPU:0, one launch (start us, length us, event | category | flops | bytes accessed | tf_op | source)
XLA Modules:
  0.0 49.0 jit_solution(11849119035787104899)
XLA Ops:
  0.6 1.0 %chain_pass.1 = (f32[128,128]{1,0:T(8,128)S(1)}, f32[4,128,128]{2,1,0:T(8,128)S(1)}, f32[4,128]{1,0:T(4,128)S(1)}) custom-call(f32[4,128,128]{2,1,0:T(8,128)} %x_hbm.1, f32[4,128]{1,0:T(4,128)} %rho_hbm.1), custom_call_target="tpu_custom_call" | custom-call | tf_op jit(solution)/shard_map/chain_pass/pallas_call | solution.py:79
  1.6 3.0 %collective-permute-start = (f32[128,128]{1,0:T(8,128)S(1)}, f32[128,128]{1,0:T(8,128)S(1)}, u32[]{:S(2)}, u32[]{:S(2)}) collective-permute-start(f32[128,128]{1,0:T(8,128)S(1)} %get-tuple-element.19), channel_id=1, source_target_pairs={{0,2},{2,0},{1,3},{3,1},{4,6},{6,4},{5,7},{7,5},{8,10},{10,8},{9,1... | collective-permute-start | bytes 196616 | tf_op jit(solution)/shard_map/ppermute | solution.py:32
  4.6 1.9 %prepare_pass.1 = (bf16[8192,128]{1,0:T(8,128)(2,1)S(1)}, f32[64,128]{1,0:T(8,128)S(1)}, f32[8,128]{1,0:T(8,128)S(1)}) custom-call(bf16[128,8192]{1,0:T(8,128)(2,1)} %d_ref.1, f32[64,128]{1,0:T(8,128)} %bitcast.11, f32[4,32]{1,0:T(4,128)} %mass_hbm.1, f32[1,32]{1,0:T(1,128)} %bitcast.12, s32[1,64]{1,0:T(1,128)} %bitcast.13), custom_call_target="tpu_custom_call" | custom-call | bytes 4194304 | tf_op jit(solution)/shard_map/prepare_pass/pallas_call | solution.py:124
  6.5 0.4 collective-permute-done.arriving_ref
  6.9 5.6 %value_pass.1 = (f32[264,128]{1,0:T(8,128)S(1)}, bf16[128,512]{1,0:T(8,128)(2,1)S(1)}) custom-call(f32[4,128,128]{2,1,0:T(8,128)S(1)} %get-tuple-element.17.x_ref, f32[4,128]{1,0:T(4,128)S(1)} %get-tuple-element.18.rho_ref, f32[128,128]{1,0:T(8,128)S(1)} %collective-permute-done.arriving_ref, s32[1]{0:T(128)} %bitcast.1.keep_ref, ...), custom_call_target="tpu_custom_call" | custom-call | flops 1073741824 | bytes 2097152 | tf_op jit(solution)/shard_map/value_pass/pallas_call | solution.py:176
  12.5 4.2 %collective-permute-start.1 = (f32[264,128]{1,0:T(8,128)S(1)}, f32[264,128]{1,0:T(8,128)S(1)}, u32[]{:S(2)}, u32[]{:S(2)}) collective-permute-start(f32[264,128]{1,0:T(8,128)S(1)} %get-tuple-element.24.refs_0_), channel_id=1, source_target_pairs={{0,12},{4,8},{8,4},{12,0},{1,13},{5,9},{9,5},{13,1},{2,14},{6,10},... | collective-permute-start | bytes 405512 | tf_op jit(solution)/shard_map/ppermute | solution.py:32
  16.7 0.0 collective-permute-start.2
  16.7 0.6 %collective-permute-start.3 = (f32[264,128]{1,0:T(8,128)S(1)}, f32[264,128]{1,0:T(8,128)S(1)}, u32[]{:S(2)}, u32[]{:S(2)}) collective-permute-start(f32[264,128]{1,0:T(8,128)S(1)} %get-tuple-element.24.refs_0_), channel_id=1, source_target_pairs={{0,4},{4,0},{8,12},{12,8},{1,5},{5,1},{9,13},{13,9},{2,6},{6,2},{1... | collective-permute-start | bytes 405512 | tf_op jit(solution)/shard_map/ppermute | solution.py:32
  17.3 3.4 %slope_pass.1.slope_ref = f32[8192,512]{1,0:T(8,128)S(1)} custom-call(bf16[128,512]{1,0:T(8,128)(2,1)S(1)} %get-tuple-element.23.state_ref, bf16[8192,128]{1,0:T(8,128)(2,1)S(1)} %get-tuple-element.21.turned_ref, f32[64,128]{1,0:T(8,128)S(1)} %get-tuple-element.22.n_ref), custom_call_target="tpu_custom_call" | custom-call | flops 1073741824 | bytes 16777216 | tf_op jit(solution)/shard_map/slope_pass/pallas_call | solution.py:211
  20.7 0.5 collective-permute-done.1.refs_1_
  21.2 5.8 %collective-permute-done.2.refs_2_ = f32[264,128]{1,0:T(8,128)S(1)} collective-permute-done((f32[264,128]{1,0:T(8,128)S(1)}, f32[264,128]{1,0:T(8,128)S(1)}, u32[]{:S(2)}, u32[]{:S(2)}) %collective-permute-start.2) | collective-permute-done | bytes 135200 | tf_op jit(solution)/shard_map/ppermute | solution.py:32
  27.0 0.0 collective-permute-done.3.refs_3_
  27.0 0.0 copy-done
  27.0 2.3 %net_pull_pass.1 = (f32[4,32]{1,0:T(4,128)S(1)}, f32[4,32,128]{2,1,0:T(8,128)S(1)}, f32[4,32,128]{2,1,0:T(8,128)S(1)}, f32[4,32,128]{2,1,0:T(8,128)S(1)}, f32[4,32,128]{2,1,0:T(8,128)S(1)}) custom-call(s32[1]{0:T(128)} %bitcast.me_ref, f32[8192,512]{1,0:T(8,128)S(1)} %slope_pass.1.slope_ref, bf16[128,8192]{1,0:T(8,128)(2,1)S(1)} %copy-done, ...), custom_call_target="tpu_custom_call" | custom-call | flops 1073741824 | bytes 16777216 | tf_op jit(solution)/shard_map/net_pull_pass/pallas_call | solution.py:321
  29.3 0.2 collective-permute-start.4
  29.5 2.4 %collective-permute-start.5 = (f32[4,32,128]{2,1,0:T(8,128)S(1)}, f32[4,32,128]{2,1,0:T(8,128)S(1)}, u32[]{:S(2)}, u32[]{:S(2)}) collective-permute-start(f32[4,32,128]{2,1,0:T(8,128)S(1)} %get-tuple-element.27), channel_id=1, source_target_pairs={{0,12},{4,8},{8,4},{12,0},{1,13},{5,9},{9,5},{13,1},{2,14},{6,10},... | collective-permute-start | bytes 196616 | tf_op jit(solution)/shard_map/ppermute | solution.py:32
  31.9 0.9 %collective-permute-start.6 = (f32[4,32,128]{2,1,0:T(8,128)S(1)}, f32[4,32,128]{2,1,0:T(8,128)S(1)}, u32[]{:S(2)}, u32[]{:S(2)}) collective-permute-start(f32[4,32,128]{2,1,0:T(8,128)S(1)} %get-tuple-element.28), channel_id=1, source_target_pairs={{0,4},{4,0},{8,12},{12,8},{1,5},{5,1},{9,13},{13,9},{2,6},{6,2},{1... | collective-permute-start | bytes 196616 | tf_op jit(solution)/shard_map/ppermute | solution.py:32
  32.8 0.0 copy-done.1
  32.8 3.4 %collective-permute-done.4 = f32[4,32,128]{2,1,0:T(8,128)S(1)} collective-permute-done((f32[4,32,128]{2,1,0:T(8,128)S(1)}, f32[4,32,128]{2,1,0:T(8,128)S(1)}, u32[]{:S(2)}, u32[]{:S(2)}) %collective-permute-start.4) | collective-permute-done | bytes 65568 | tf_op jit(solution)/shard_map/ppermute | solution.py:32
  36.2 0.0 collective-permute-done.5
  36.2 0.6 %collective-permute-done.6 = f32[4,32,128]{2,1,0:T(8,128)S(1)} collective-permute-done((f32[4,32,128]{2,1,0:T(8,128)S(1)}, f32[4,32,128]{2,1,0:T(8,128)S(1)}, u32[]{:S(2)}, u32[]{:S(2)}) %collective-permute-start.6) | collective-permute-done | bytes 65568 | tf_op jit(solution)/shard_map/ppermute | solution.py:32
  36.9 1.6 %collective-permute-start.7 = (f32[32,128]{1,0:T(8,128)S(1)}, f32[32,128]{1,0:T(8,128)S(1)}, u32[]{:S(2)}, u32[]{:S(2)}) collective-permute-start(f32[32,128]{1,0:T(8,128)S(1)} %fusion), channel_id=1, source_target_pairs={{0,2},{2,0},{1,3},{3,1},{4,6},{6,4},{5,7},{7,5},{8,10},{10,8},{9,1... | collective-permute-start | bytes 49160 | tf_op jit(solution)/shard_map/ppermute | solution.py:32
  38.5 2.2 %collective-permute-done.7 = f32[32,128]{1,0:T(8,128)S(1)} collective-permute-done((f32[32,128]{1,0:T(8,128)S(1)}, f32[32,128]{1,0:T(8,128)S(1)}, u32[]{:S(2)}, u32[]{:S(2)}) %collective-permute-start.7) | collective-permute-done | bytes 16416 | tf_op jit(solution)/shard_map/ppermute | solution.py:32
  40.7 1.9 %collective-permute-start.8 = (f32[4,32,128]{2,1,0:T(8,128)S(1)}, f32[4,32,128]{2,1,0:T(8,128)S(1)}, u32[]{:S(2)}, u32[]{:S(2)}) collective-permute-start(f32[4,32,128]{2,1,0:T(8,128)S(1)} %multiply_add_fusion.refs_0_), channel_id=1, source_target_pairs={{0,12},{4,8},{8,4},{12,0},{1,13},{5,9},{9,5},{13,1},{2,14},{6,10},... | collective-permute-start | bytes 196616 | tf_op jit(solution)/shard_map/ppermute | solution.py:32
  42.6 0.0 collective-permute-start.10
  42.6 2.6 %collective-permute-start.11 = (f32[4,32,128]{2,1,0:T(8,128)S(1)}, f32[4,32,128]{2,1,0:T(8,128)S(1)}, u32[]{:S(2)}, u32[]{:S(2)}) collective-permute-start(f32[4,32,128]{2,1,0:T(8,128)S(1)} %multiply_add_fusion.refs_0_), channel_id=1, source_target_pairs={{0,8},{4,12},{8,0},{12,4},{1,9},{5,13},{9,1},{13,5},{2,10},{6,14},... | collective-permute-start | bytes 196616 | tf_op jit(solution)/shard_map/ppermute | solution.py:32
  45.2 1.7 %collective-permute-done.8.refs_2_ = f32[4,32,128]{2,1,0:T(8,128)S(1)} collective-permute-done((f32[4,32,128]{2,1,0:T(8,128)S(1)}, f32[4,32,128]{2,1,0:T(8,128)S(1)}, u32[]{:S(2)}, u32[]{:S(2)}) %collective-permute-start.8) | collective-permute-done | bytes 65568 | tf_op jit(solution)/shard_map/ppermute | solution.py:32
  46.9 0.0 collective-permute-start.9
  46.9 1.3 %collective-permute-done.10.refs_1_ = f32[4,32,128]{2,1,0:T(8,128)S(1)} collective-permute-done((f32[4,32,128]{2,1,0:T(8,128)S(1)}, f32[4,32,128]{2,1,0:T(8,128)S(1)}, u32[]{:S(2)}, u32[]{:S(2)}) %collective-permute-start.10) | collective-permute-done | bytes 65568 | tf_op jit(solution)/shard_map/ppermute | solution.py:32
  48.2 0.0 collective-permute-done.11.refs_3_
  48.2 0.0 collective-permute-done.9.other_ref
  48.2 0.7 %place.1 = (f32[4,32]{1,0:T(4,128)}, f32[4,128,128]{2,1,0:T(8,128)}) custom-call(s32[1]{0:T(128)} %bitcast.me_ref, f32[4,32]{1,0:T(4,128)S(1)} %get-tuple-element.30.exposure_ref, f32[4,32]{1,0:T(4,128)S(1)} %collective-permute-done.9.other_ref, f32[4,32,128]{2,1,0:T(8,128)S(1)} %multiply_add_fusion.refs_0_, ...), custom_call_target="tpu_custom_call" | custom-call | tf_op jit(solution)/shard_map/place/pallas_call | solution.py:376
  (8 shorter events, 0.1 us)
Async XLA Ops:
  1.6 5.2 %collective-permute-start = (f32[128,128]{1,0:T(8,128)S(1)}, f32[128,128]{1,0:T(8,128)S(1)}, u32[]{:S(2)}, u32[]{:S(2)}) collective-permute-start(f32[128,128]{1,0:T(8,128)S(1)} %get-tuple-element.19), channel_id=1, source_target_pairs={{0,2},{2,0},{1,3},{3,1},{4,6},{6,4},{5,7},{7,5},{8,10},{10,8},{9,1... | collective-permute-start | bytes 196616 | tf_op jit(solution)/shard_map/ppermute | solution.py:32
  12.5 8.7 %collective-permute-start.1 = (f32[264,128]{1,0:T(8,128)S(1)}, f32[264,128]{1,0:T(8,128)S(1)}, u32[]{:S(2)}, u32[]{:S(2)}) collective-permute-start(f32[264,128]{1,0:T(8,128)S(1)} %get-tuple-element.24.refs_0_), channel_id=1, source_target_pairs={{0,12},{4,8},{8,4},{12,0},{1,13},{5,9},{9,5},{13,1},{2,14},{6,10},... | collective-permute-start | bytes 405512 | tf_op jit(solution)/shard_map/ppermute | solution.py:32
  16.7 10.3 %collective-permute-start.2 = (f32[264,128]{1,0:T(8,128)S(1)}, f32[264,128]{1,0:T(8,128)S(1)}, u32[]{:S(2)}, u32[]{:S(2)}) collective-permute-start(f32[264,128]{1,0:T(8,128)S(1)} %get-tuple-element.24.refs_0_), channel_id=1, source_target_pairs={{0,8},{4,12},{8,0},{12,4},{1,9},{5,13},{9,1},{13,5},{2,10},{6,14},... | collective-permute-start | bytes 405512 | tf_op jit(solution)/shard_map/ppermute | solution.py:32
  16.7 10.3 %collective-permute-start.3 = (f32[264,128]{1,0:T(8,128)S(1)}, f32[264,128]{1,0:T(8,128)S(1)}, u32[]{:S(2)}, u32[]{:S(2)}) collective-permute-start(f32[264,128]{1,0:T(8,128)S(1)} %get-tuple-element.24.refs_0_), channel_id=1, source_target_pairs={{0,4},{4,0},{8,12},{12,8},{1,5},{5,1},{9,13},{13,9},{2,6},{6,2},{1... | collective-permute-start | bytes 405512 | tf_op jit(solution)/shard_map/ppermute | solution.py:32
  17.3 9.6 %copy-start = (bf16[128,8192]{1,0:T(8,128)(2,1)S(1)}, bf16[128,8192]{1,0:T(8,128)(2,1)}, u32[]{:S(2)}) copy-start(bf16[128,8192]{1,0:T(8,128)(2,1)} %d_ref.1) | copy-start | bytes 6291460
  27.0 5.9 %copy-start.1 = (f32[4,128]{1,0:T(4,128)S(1)}, f32[4,128]{1,0:T(4,128)}, u32[]{:S(2)}) copy-start(f32[4,128]{1,0:T(4,128)} %rho_hbm.1) | copy-start | bytes 6148
  29.3 6.9 %collective-permute-start.4 = (f32[4,32,128]{2,1,0:T(8,128)S(1)}, f32[4,32,128]{2,1,0:T(8,128)S(1)}, u32[]{:S(2)}, u32[]{:S(2)}) collective-permute-start(f32[4,32,128]{2,1,0:T(8,128)S(1)} %get-tuple-element.26), channel_id=1, source_target_pairs={{0,8},{4,12},{8,0},{12,4},{1,9},{5,13},{9,1},{13,5},{2,10},{6,14},... | collective-permute-start | bytes 196616 | tf_op jit(solution)/shard_map/ppermute | solution.py:32
  29.5 6.7 %collective-permute-start.5 = (f32[4,32,128]{2,1,0:T(8,128)S(1)}, f32[4,32,128]{2,1,0:T(8,128)S(1)}, u32[]{:S(2)}, u32[]{:S(2)}) collective-permute-start(f32[4,32,128]{2,1,0:T(8,128)S(1)} %get-tuple-element.27), channel_id=1, source_target_pairs={{0,12},{4,8},{8,4},{12,0},{1,13},{5,9},{9,5},{13,1},{2,14},{6,10},... | collective-permute-start | bytes 196616 | tf_op jit(solution)/shard_map/ppermute | solution.py:32
  31.9 5.0 %collective-permute-start.6 = (f32[4,32,128]{2,1,0:T(8,128)S(1)}, f32[4,32,128]{2,1,0:T(8,128)S(1)}, u32[]{:S(2)}, u32[]{:S(2)}) collective-permute-start(f32[4,32,128]{2,1,0:T(8,128)S(1)} %get-tuple-element.28), channel_id=1, source_target_pairs={{0,4},{4,0},{8,12},{12,8},{1,5},{5,1},{9,13},{13,9},{2,6},{6,2},{1... | collective-permute-start | bytes 196616 | tf_op jit(solution)/shard_map/ppermute | solution.py:32
  36.9 3.8 %collective-permute-start.7 = (f32[32,128]{1,0:T(8,128)S(1)}, f32[32,128]{1,0:T(8,128)S(1)}, u32[]{:S(2)}, u32[]{:S(2)}) collective-permute-start(f32[32,128]{1,0:T(8,128)S(1)} %fusion), channel_id=1, source_target_pairs={{0,2},{2,0},{1,3},{3,1},{4,6},{6,4},{5,7},{7,5},{8,10},{10,8},{9,1... | collective-permute-start | bytes 49160 | tf_op jit(solution)/shard_map/ppermute | solution.py:32
  40.7 6.2 %collective-permute-start.8 = (f32[4,32,128]{2,1,0:T(8,128)S(1)}, f32[4,32,128]{2,1,0:T(8,128)S(1)}, u32[]{:S(2)}, u32[]{:S(2)}) collective-permute-start(f32[4,32,128]{2,1,0:T(8,128)S(1)} %multiply_add_fusion.refs_0_), channel_id=1, source_target_pairs={{0,12},{4,8},{8,4},{12,0},{1,13},{5,9},{9,5},{13,1},{2,14},{6,10},... | collective-permute-start | bytes 196616 | tf_op jit(solution)/shard_map/ppermute | solution.py:32
  42.6 5.6 %collective-permute-start.10 = (f32[4,32,128]{2,1,0:T(8,128)S(1)}, f32[4,32,128]{2,1,0:T(8,128)S(1)}, u32[]{:S(2)}, u32[]{:S(2)}) collective-permute-start(f32[4,32,128]{2,1,0:T(8,128)S(1)} %multiply_add_fusion.refs_0_), channel_id=1, source_target_pairs={{0,4},{4,0},{8,12},{12,8},{1,5},{5,1},{9,13},{13,9},{2,6},{6,2},{1... | collective-permute-start | bytes 196616 | tf_op jit(solution)/shard_map/ppermute | solution.py:32
  42.6 5.6 %collective-permute-start.11 = (f32[4,32,128]{2,1,0:T(8,128)S(1)}, f32[4,32,128]{2,1,0:T(8,128)S(1)}, u32[]{:S(2)}, u32[]{:S(2)}) collective-permute-start(f32[4,32,128]{2,1,0:T(8,128)S(1)} %multiply_add_fusion.refs_0_), channel_id=1, source_target_pairs={{0,8},{4,12},{8,0},{12,4},{1,9},{5,13},{9,1},{13,5},{2,10},{6,14},... | collective-permute-start | bytes 196616 | tf_op jit(solution)/shard_map/ppermute | solution.py:32
  46.9 1.3 %collective-permute-start.9 = (f32[4,32]{1,0:T(4,128)S(1)}, f32[4,32]{1,0:T(4,128)S(1)}, u32[]{:S(2)}, u32[]{:S(2)}) collective-permute-start(f32[4,32]{1,0:T(4,128)S(1)} %get-tuple-element.30.exposure_ref), channel_id=1, source_target_pairs={{0,1},{1,0},{2,3},{3,2},{4,5},{5,4},{6,7},{7,6},{8,9},{9,8},{10,11... | collective-permute-start | bytes 1544 | tf_op jit(solution)/shard_map/ppermute | solution.py:32

commit v9 on v8

--- a/solution.py
+++ b/solution.py
@@ -189,18 +189,20 @@
     )(x, rho, arriving, keep, facts, turned, n)
 
 
-def slope_kernel(step, state_ref, turned_ref, n_ref, slope_ref, half_ref):
+def sigmoid(v):
+    return 1.0 / (1.0 + jnp.exp(-v))
+
+
+def slope_kernel(step, state_ref, turned_ref, n_ref, slope_ref):
     blocks = step // block_width
-    half_ref[...] = state_ref[...] * 0.5
 
     @pl.loop(0, turned_ref.shape[0] // step)
     def _(c):
-        size_t = 0.5 * n_ref[pl.ds(pl.multiple_of(c * blocks, blocks), blocks), :].T
+        size_t = n_ref[pl.ds(pl.multiple_of(c * blocks, blocks), blocks), :].T
         turned = turned_ref[pl.ds(pl.multiple_of(c * step, step), step), :]
-        linear = jnp.dot(turned, half_ref[...], preferred_element_type=f32)
+        linear = jnp.dot(turned, state_ref[...], preferred_element_type=f32)
         for b in range(blocks):
-            size = size_t[:, b : b + 1]
-            slope = jnp.tanh(linear[b * block_width : (b + 1) * block_width]) * size + size
+            slope = sigmoid(linear[b * block_width : (b + 1) * block_width]) * size_t[:, b : b + 1]
             slope_ref[pl.ds(pl.multiple_of(c * step + b * block_width, block_width), block_width), :] = slope
 
 
@@ -213,10 +215,9 @@
         in_specs=[vmem] * 3,
         out_specs=vmem,
         out_shape=jax.ShapeDtypeStruct((trades, rows), f32),
-        scratch_shapes=[pltpu.VMEM((factors, rows), bf16)],
         compiler_params=pltpu.CompilerParams(vmem_limit_bytes=16 << 20),
         cost_estimate=pl.CostEstimate(
-            flops=2 * rows * trades * factors, bytes_accessed=4 * trades * rows, transcendentals=rows * trades
+            flops=2 * rows * trades * factors, bytes_accessed=4 * trades * rows, transcendentals=2 * rows * trades
         ),
         name="slope_pass",
     )(state, turned, n)
@@ -258,13 +259,13 @@
     adjoint, totals = [], []
     for k in range(shards):
         shifted = netted[k * cpty_dev : (k + 1) * cpty_dev] - columns[k][:cpty_dev, dates : dates + 1]
-        slope = 0.5 * jnp.tanh(0.5 * shifted) + 0.5
+        slope = sigmoid(shifted)
         parts = []
         for t in range(dates):
             parts.append(slope[:, t * paths : (t + 1) * paths] * columns[k][:cpty_dev, t : t + 1])
         adjoint.append(jnp.concatenate(parts, axis=1))
         if k == 0:
-            exposed = softplus(shifted)
+            exposed = jnp.maximum(shifted, 0.0) + jnp.log1p(jnp.exp(-jnp.abs(shifted)))
             for t in range(dates):
                 totals.append(jnp.sum(exposed[:, t * paths : (t + 1) * paths], axis=1, keepdims=True))
     upstream_ref[...] = split_dot(own, jnp.concatenate(adjoint, axis=0))

time: 49.2 us -> 49.2 us (level)
  Pallas kernels: 14.9 us -> 16.8 us
  waiting for transfers between devices: 15.9 us -> 14 us
    ppermute x12, waiting for transfers between devices: 15.9 us -> 14 us  [swap(): return lax.ppermute(value, axes, pairs)]
    pallas_call x1, Pallas kernels: 3.39 us -> 5.25 us  [slope_pass(): pl.pallas_call(functools.partial(slope_kernel, min(2048, trades)), in_spe...]
  transfers between devices with their start and end apart: 12 -> 12, of which waited for: 8 -> 7; matrix products, arithmetic and copies ran while one was open for 0% -> 0% of each run, Pallas kernels for 11% -> 15%
where the time goes in v9:
time: 49.2 us; the launch traced here: 49 us
  starting transfers between devices  17.4 us (35%)
  Pallas kernels  16.8 us (34%)
  waiting for transfers between devices  14 us (28%)
  between operations  0.7 us (1%)
    ppermute x12, starting transfers between devices, swap(): return lax.ppermute(value, axes, pairs)  17.4 us
    ppermute x12, waiting for transfers between devices, swap(): return lax.ppermute(value, axes, pairs)  14 us
    pallas_call x1, Pallas kernels, value_pass(): pl.pallas_call(functools.partial(value_kernel, min(VALUE_STEP, trades)),...  5.6 us
    pallas_call x1, Pallas kernels, slope_pass(): pl.pallas_call(functools.partial(slope_kernel, min(2048, trades)), in_spe...  5.25 us
    pallas_call x1, Pallas kernels, net_pull_pass(): pl.pallas_call(functools.partial(net_pull_kernel, min(PULL_STEP, trades),...  2.33 us
    pallas_call x1, Pallas kernels, prepare_pass(): pl.pallas_call(functools.partial(prepare_kernel, step), in_specs=[hbm] *...  1.89 us
    pallas_call x1, Pallas kernels, chain_pass(): pl.pallas_call(chain_kernel, in_specs=[pl.BlockSpec(memory_space=pltpu.HB...  0.99 us
  transfers between devices with their start and end apart: 12, of which 7 were waited for; matrix products, arithmetic and copies ran while one was open for 0% of the time, Pallas kernels for 15%

profile of v9, /device:TPU:0, one launch (start us, length us, event | category | flops | bytes accessed | tf_op | source)
XLA Modules:
  0.0 49.0 jit_solution(16860076478541681111)
XLA Ops:
  0.6 1.0 %chain_pass.1 = (f32[128,128]{1,0:T(8,128)S(1)}, f32[4,128,128]{2,1,0:T(8,128)S(1)}, f32[4,128]{1,0:T(4,128)S(1)}) custom-call(f32[4,128,128]{2,1,0:T(8,128)} %x_hbm.1, f32[4,128]{1,0:T(4,128)} %rho_hbm.1), custom_call_target="tpu_custom_call" | custom-call | tf_op jit(solution)/shard_map/chain_pass/pallas_call | solution.py:79
  1.6 3.0 %collective-permute-start = (f32[128,128]{1,0:T(8,128)S(1)}, f32[128,128]{1,0:T(8,128)S(1)}, u32[]{:S(2)}, u32[]{:S(2)}) collective-permute-start(f32[128,128]{1,0:T(8,128)S(1)} %get-tuple-element.19), channel_id=1, source_target_pairs={{0,2},{2,0},{1,3},{3,1},{4,6},{6,4},{5,7},{7,5},{8,10},{10,8},{9,1... | collective-permute-start | bytes 196616 | tf_op jit(solution)/shard_map/ppermute | solution.py:32
  4.6 1.9 %prepare_pass.1 = (bf16[8192,128]{1,0:T(8,128)(2,1)S(1)}, f32[64,128]{1,0:T(8,128)S(1)}, f32[8,128]{1,0:T(8,128)S(1)}) custom-call(bf16[128,8192]{1,0:T(8,128)(2,1)} %d_ref.1, f32[64,128]{1,0:T(8,128)} %bitcast.11, f32[4,32]{1,0:T(4,128)} %mass_hbm.1, f32[1,32]{1,0:T(1,128)} %bitcast.12, s32[1,64]{1,0:T(1,128)} %bitcast.13), custom_call_target="tpu_custom_call" | custom-call | bytes 4194304 | tf_op jit(solution)/shard_map/prepare_pass/pallas_call | solution.py:124
  6.5 0.4 collective-permute-done.arriving_ref
  6.9 5.6 %value_pass.1 = (f32[264,128]{1,0:T(8,128)S(1)}, bf16[128,512]{1,0:T(8,128)(2,1)S(1)}) custom-call(f32[4,128,128]{2,1,0:T(8,128)S(1)} %get-tuple-element.17.x_ref, f32[4,128]{1,0:T(4,128)S(1)} %get-tuple-element.18.rho_ref, f32[128,128]{1,0:T(8,128)S(1)} %collective-permute-done.arriving_ref, s32[1]{0:T(128)} %bitcast.1.keep_ref, ...), custom_call_target="tpu_custom_call" | custom-call | flops 1073741824 | bytes 2097152 | tf_op jit(solution)/shard_map/value_pass/pallas_call | solution.py:176
  12.5 4.2 %collective-permute-start.1 = (f32[264,128]{1,0:T(8,128)S(1)}, f32[264,128]{1,0:T(8,128)S(1)}, u32[]{:S(2)}, u32[]{:S(2)}) collective-permute-start(f32[264,128]{1,0:T(8,128)S(1)} %get-tuple-element.24.refs_0_), channel_id=1, source_target_pairs={{0,12},{4,8},{8,4},{12,0},{1,13},{5,9},{9,5},{13,1},{2,14},{6,10},... | collective-permute-start | bytes 405512 | tf_op jit(solution)/shard_map/ppermute | solution.py:32
  16.7 0.0 collective-permute-start.2
  16.7 0.6 %collective-permute-start.3 = (f32[264,128]{1,0:T(8,128)S(1)}, f32[264,128]{1,0:T(8,128)S(1)}, u32[]{:S(2)}, u32[]{:S(2)}) collective-permute-start(f32[264,128]{1,0:T(8,128)S(1)} %get-tuple-element.24.refs_0_), channel_id=1, source_target_pairs={{0,4},{4,0},{8,12},{12,8},{1,5},{5,1},{9,13},{13,9},{2,6},{6,2},{1... | collective-permute-start | bytes 405512 | tf_op jit(solution)/shard_map/ppermute | solution.py:32
  17.3 5.2 %slope_pass.1.slope_ref = f32[8192,512]{1,0:T(8,128)S(1)} custom-call(bf16[128,512]{1,0:T(8,128)(2,1)S(1)} %get-tuple-element.23.state_ref, bf16[8192,128]{1,0:T(8,128)(2,1)S(1)} %get-tuple-element.21.turned_ref, f32[64,128]{1,0:T(8,128)S(1)} %get-tuple-element.22.n_ref), custom_call_target="tpu_custom_call" | custom-call | flops 1073741824 | bytes 16777216 | tf_op jit(solution)/shard_map/slope_pass/pallas_call | solution.py:213
  22.6 0.0 collective-permute-done.1.refs_1_
  22.6 4.4 %collective-permute-done.2.refs_2_ = f32[264,128]{1,0:T(8,128)S(1)} collective-permute-done((f32[264,128]{1,0:T(8,128)S(1)}, f32[264,128]{1,0:T(8,128)S(1)}, u32[]{:S(2)}, u32[]{:S(2)}) %collective-permute-start.2) | collective-permute-done | bytes 135200 | tf_op jit(solution)/shard_map/ppermute | solution.py:32
  27.0 0.0 collective-permute-done.3.refs_3_
  27.0 0.0 copy-done
  27.0 2.3 %net_pull_pass.1 = (f32[4,32]{1,0:T(4,128)S(1)}, f32[4,32,128]{2,1,0:T(8,128)S(1)}, f32[4,32,128]{2,1,0:T(8,128)S(1)}, f32[4,32,128]{2,1,0:T(8,128)S(1)}, f32[4,32,128]{2,1,0:T(8,128)S(1)}) custom-call(s32[1]{0:T(128)} %bitcast.me_ref, f32[8192,512]{1,0:T(8,128)S(1)} %slope_pass.1.slope_ref, bf16[128,8192]{1,0:T(8,128)(2,1)S(1)} %copy-done, ...), custom_call_target="tpu_custom_call" | custom-call | flops 1073741824 | bytes 16777216 | tf_op jit(solution)/shard_map/net_pull_pass/pallas_call | solution.py:322
  29.3 0.2 collective-permute-start.4
  29.5 2.4 %collective-permute-start.5 = (f32[4,32,128]{2,1,0:T(8,128)S(1)}, f32[4,32,128]{2,1,0:T(8,128)S(1)}, u32[]{:S(2)}, u32[]{:S(2)}) collective-permute-start(f32[4,32,128]{2,1,0:T(8,128)S(1)} %get-tuple-element.27), channel_id=1, source_target_pairs={{0,12},{4,8},{8,4},{12,0},{1,13},{5,9},{9,5},{13,1},{2,14},{6,10},... | collective-permute-start | bytes 196616 | tf_op jit(solution)/shard_map/ppermute | solution.py:32
  31.9 0.9 %collective-permute-start.6 = (f32[4,32,128]{2,1,0:T(8,128)S(1)}, f32[4,32,128]{2,1,0:T(8,128)S(1)}, u32[]{:S(2)}, u32[]{:S(2)}) collective-permute-start(f32[4,32,128]{2,1,0:T(8,128)S(1)} %get-tuple-element.28), channel_id=1, source_target_pairs={{0,4},{4,0},{8,12},{12,8},{1,5},{5,1},{9,13},{13,9},{2,6},{6,2},{1... | collective-permute-start | bytes 196616 | tf_op jit(solution)/shard_map/ppermute | solution.py:32
  32.9 0.0 copy-done.1
  32.9 3.4 %collective-permute-done.4 = f32[4,32,128]{2,1,0:T(8,128)S(1)} collective-permute-done((f32[4,32,128]{2,1,0:T(8,128)S(1)}, f32[4,32,128]{2,1,0:T(8,128)S(1)}, u32[]{:S(2)}, u32[]{:S(2)}) %collective-permute-start.4) | collective-permute-done | bytes 65568 | tf_op jit(solution)/shard_map/ppermute | solution.py:32
  36.2 0.0 collective-permute-done.5
  36.2 0.6 %collective-permute-done.6 = f32[4,32,128]{2,1,0:T(8,128)S(1)} collective-permute-done((f32[4,32,128]{2,1,0:T(8,128)S(1)}, f32[4,32,128]{2,1,0:T(8,128)S(1)}, u32[]{:S(2)}, u32[]{:S(2)}) %collective-permute-start.6) | collective-permute-done | bytes 65568 | tf_op jit(solution)/shard_map/ppermute | solution.py:32
  36.9 1.6 %collective-permute-start.7 = (f32[32,128]{1,0:T(8,128)S(1)}, f32[32,128]{1,0:T(8,128)S(1)}, u32[]{:S(2)}, u32[]{:S(2)}) collective-permute-start(f32[32,128]{1,0:T(8,128)S(1)} %fusion), channel_id=1, source_target_pairs={{0,2},{2,0},{1,3},{3,1},{4,6},{6,4},{5,7},{7,5},{8,10},{10,8},{9,1... | collective-permute-start | bytes 49160 | tf_op jit(solution)/shard_map/ppermute | solution.py:32
  38.5 2.2 %collective-permute-done.7 = f32[32,128]{1,0:T(8,128)S(1)} collective-permute-done((f32[32,128]{1,0:T(8,128)S(1)}, f32[32,128]{1,0:T(8,128)S(1)}, u32[]{:S(2)}, u32[]{:S(2)}) %collective-permute-start.7) | collective-permute-done | bytes 16416 | tf_op jit(solution)/shard_map/ppermute | solution.py:32
  40.7 1.9 %collective-permute-start.8 = (f32[4,32,128]{2,1,0:T(8,128)S(1)}, f32[4,32,128]{2,1,0:T(8,128)S(1)}, u32[]{:S(2)}, u32[]{:S(2)}) collective-permute-start(f32[4,32,128]{2,1,0:T(8,128)S(1)} %multiply_add_fusion.refs_0_), channel_id=1, source_target_pairs={{0,12},{4,8},{8,4},{12,0},{1,13},{5,9},{9,5},{13,1},{2,14},{6,10},... | collective-permute-start | bytes 196616 | tf_op jit(solution)/shard_map/ppermute | solution.py:32
  42.6 0.0 collective-permute-start.10
  42.6 2.6 %collective-permute-start.11 = (f32[4,32,128]{2,1,0:T(8,128)S(1)}, f32[4,32,128]{2,1,0:T(8,128)S(1)}, u32[]{:S(2)}, u32[]{:S(2)}) collective-permute-start(f32[4,32,128]{2,1,0:T(8,128)S(1)} %multiply_add_fusion.refs_0_), channel_id=1, source_target_pairs={{0,8},{4,12},{8,0},{12,4},{1,9},{5,13},{9,1},{13,5},{2,10},{6,14},... | collective-permute-start | bytes 196616 | tf_op jit(solution)/shard_map/ppermute | solution.py:32
  45.2 1.7 %collective-permute-done.8.refs_2_ = f32[4,32,128]{2,1,0:T(8,128)S(1)} collective-permute-done((f32[4,32,128]{2,1,0:T(8,128)S(1)}, f32[4,32,128]{2,1,0:T(8,128)S(1)}, u32[]{:S(2)}, u32[]{:S(2)}) %collective-permute-start.8) | collective-permute-done | bytes 65568 | tf_op jit(solution)/shard_map/ppermute | solution.py:32
  46.9 0.0 collective-permute-start.9
  46.9 1.3 %collective-permute-done.10.refs_1_ = f32[4,32,128]{2,1,0:T(8,128)S(1)} collective-permute-done((f32[4,32,128]{2,1,0:T(8,128)S(1)}, f32[4,32,128]{2,1,0:T(8,128)S(1)}, u32[]{:S(2)}, u32[]{:S(2)}) %collective-permute-start.10) | collective-permute-done | bytes 65568 | tf_op jit(solution)/shard_map/ppermute | solution.py:32
  48.3 0.0 collective-permute-done.11.refs_3_
  48.3 0.0 collective-permute-done.9.other_ref
  48.3 0.7 %place.1 = (f32[4,32]{1,0:T(4,128)}, f32[4,128,128]{2,1,0:T(8,128)}) custom-call(s32[1]{0:T(128)} %bitcast.me_ref, f32[4,32]{1,0:T(4,128)S(1)} %get-tuple-element.30.exposure_ref, f32[4,32]{1,0:T(4,128)S(1)} %collective-permute-done.9.other_ref, f32[4,32,128]{2,1,0:T(8,128)S(1)} %multiply_add_fusion.refs_0_, ...), custom_call_target="tpu_custom_call" | custom-call | tf_op jit(solution)/shard_map/place/pallas_call | solution.py:377
  (8 shorter events, 0.1 us)
Async XLA Ops:
  1.6 5.2 %collective-permute-start = (f32[128,128]{1,0:T(8,128)S(1)}, f32[128,128]{1,0:T(8,128)S(1)}, u32[]{:S(2)}, u32[]{:S(2)}) collective-permute-start(f32[128,128]{1,0:T(8,128)S(1)} %get-tuple-element.19), channel_id=1, source_target_pairs={{0,2},{2,0},{1,3},{3,1},{4,6},{6,4},{5,7},{7,5},{8,10},{10,8},{9,1... | collective-permute-start | bytes 196616 | tf_op jit(solution)/shard_map/ppermute | solution.py:32
  12.5 10.1 %collective-permute-start.1 = (f32[264,128]{1,0:T(8,128)S(1)}, f32[264,128]{1,0:T(8,128)S(1)}, u32[]{:S(2)}, u32[]{:S(2)}) collective-permute-start(f32[264,128]{1,0:T(8,128)S(1)} %get-tuple-element.24.refs_0_), channel_id=1, source_target_pairs={{0,12},{4,8},{8,4},{12,0},{1,13},{5,9},{9,5},{13,1},{2,14},{6,10},... | collective-permute-start | bytes 405512 | tf_op jit(solution)/shard_map/ppermute | solution.py:32
  16.7 10.3 %collective-permute-start.2 = (f32[264,128]{1,0:T(8,128)S(1)}, f32[264,128]{1,0:T(8,128)S(1)}, u32[]{:S(2)}, u32[]{:S(2)}) collective-permute-start(f32[264,128]{1,0:T(8,128)S(1)} %get-tuple-element.24.refs_0_), channel_id=1, source_target_pairs={{0,8},{4,12},{8,0},{12,4},{1,9},{5,13},{9,1},{13,5},{2,10},{6,14},... | collective-permute-start | bytes 405512 | tf_op jit(solution)/shard_map/ppermute | solution.py:32
  16.7 10.3 %collective-permute-start.3 = (f32[264,128]{1,0:T(8,128)S(1)}, f32[264,128]{1,0:T(8,128)S(1)}, u32[]{:S(2)}, u32[]{:S(2)}) collective-permute-start(f32[264,128]{1,0:T(8,128)S(1)} %get-tuple-element.24.refs_0_), channel_id=1, source_target_pairs={{0,4},{4,0},{8,12},{12,8},{1,5},{5,1},{9,13},{13,9},{2,6},{6,2},{1... | collective-permute-start | bytes 405512 | tf_op jit(solution)/shard_map/ppermute | solution.py:32
  17.3 9.6 %copy-start = (bf16[128,8192]{1,0:T(8,128)(2,1)S(1)}, bf16[128,8192]{1,0:T(8,128)(2,1)}, u32[]{:S(2)}) copy-start(bf16[128,8192]{1,0:T(8,128)(2,1)} %d_ref.1) | copy-start | bytes 6291460
  27.0 5.9 %copy-start.1 = (f32[4,128]{1,0:T(4,128)S(1)}, f32[4,128]{1,0:T(4,128)}, u32[]{:S(2)}) copy-start(f32[4,128]{1,0:T(4,128)} %rho_hbm.1) | copy-start | bytes 6148
  29.3 6.9 %collective-permute-start.4 = (f32[4,32,128]{2,1,0:T(8,128)S(1)}, f32[4,32,128]{2,1,0:T(8,128)S(1)}, u32[]{:S(2)}, u32[]{:S(2)}) collective-permute-start(f32[4,32,128]{2,1,0:T(8,128)S(1)} %get-tuple-element.26), channel_id=1, source_target_pairs={{0,8},{4,12},{8,0},{12,4},{1,9},{5,13},{9,1},{13,5},{2,10},{6,14},... | collective-permute-start | bytes 196616 | tf_op jit(solution)/shard_map/ppermute | solution.py:32
  29.5 6.7 %collective-permute-start.5 = (f32[4,32,128]{2,1,0:T(8,128)S(1)}, f32[4,32,128]{2,1,0:T(8,128)S(1)}, u32[]{:S(2)}, u32[]{:S(2)}) collective-permute-start(f32[4,32,128]{2,1,0:T(8,128)S(1)} %get-tuple-element.27), channel_id=1, source_target_pairs={{0,12},{4,8},{8,4},{12,0},{1,13},{5,9},{9,5},{13,1},{2,14},{6,10},... | collective-permute-start | bytes 196616 | tf_op jit(solution)/shard_map/ppermute | solution.py:32
  31.9 5.0 %collective-permute-start.6 = (f32[4,32,128]{2,1,0:T(8,128)S(1)}, f32[4,32,128]{2,1,0:T(8,128)S(1)}, u32[]{:S(2)}, u32[]{:S(2)}) collective-permute-start(f32[4,32,128]{2,1,0:T(8,128)S(1)} %get-tuple-element.28), channel_id=1, source_target_pairs={{0,4},{4,0},{8,12},{12,8},{1,5},{5,1},{9,13},{13,9},{2,6},{6,2},{1... | collective-permute-start | bytes 196616 | tf_op jit(solution)/shard_map/ppermute | solution.py:32
  36.9 3.8 %collective-permute-start.7 = (f32[32,128]{1,0:T(8,128)S(1)}, f32[32,128]{1,0:T(8,128)S(1)}, u32[]{:S(2)}, u32[]{:S(2)}) collective-permute-start(f32[32,128]{1,0:T(8,128)S(1)} %fusion), channel_id=1, source_target_pairs={{0,2},{2,0},{1,3},{3,1},{4,6},{6,4},{5,7},{7,5},{8,10},{10,8},{9,1... | collective-permute-start | bytes 49160 | tf_op jit(solution)/shard_map/ppermute | solution.py:32
  40.7 6.2 %collective-permute-start.8 = (f32[4,32,128]{2,1,0:T(8,128)S(1)}, f32[4,32,128]{2,1,0:T(8,128)S(1)}, u32[]{:S(2)}, u32[]{:S(2)}) collective-permute-start(f32[4,32,128]{2,1,0:T(8,128)S(1)} %multiply_add_fusion.refs_0_), channel_id=1, source_target_pairs={{0,12},{4,8},{8,4},{12,0},{1,13},{5,9},{9,5},{13,1},{2,14},{6,10},... | collective-permute-start | bytes 196616 | tf_op jit(solution)/shard_map/ppermute | solution.py:32
  42.6 5.6 %collective-permute-start.10 = (f32[4,32,128]{2,1,0:T(8,128)S(1)}, f32[4,32,128]{2,1,0:T(8,128)S(1)}, u32[]{:S(2)}, u32[]{:S(2)}) collective-permute-start(f32[4,32,128]{2,1,0:T(8,128)S(1)} %multiply_add_fusion.refs_0_), channel_id=1, source_target_pairs={{0,4},{4,0},{8,12},{12,8},{1,5},{5,1},{9,13},{13,9},{2,6},{6,2},{1... | collective-permute-start | bytes 196616 | tf_op jit(solution)/shard_map/ppermute | solution.py:32
  42.6 5.6 %collective-permute-start.11 = (f32[4,32,128]{2,1,0:T(8,128)S(1)}, f32[4,32,128]{2,1,0:T(8,128)S(1)}, u32[]{:S(2)}, u32[]{:S(2)}) collective-permute-start(f32[4,32,128]{2,1,0:T(8,128)S(1)} %multiply_add_fusion.refs_0_), channel_id=1, source_target_pairs={{0,8},{4,12},{8,0},{12,4},{1,9},{5,13},{9,1},{13,5},{2,10},{6,14},... | collective-permute-start | bytes 196616 | tf_op jit(solution)/shard_map/ppermute | solution.py:32
  46.9 1.3 %collective-permute-start.9 = (f32[4,32]{1,0:T(4,128)S(1)}, f32[4,32]{1,0:T(4,128)S(1)}, u32[]{:S(2)}, u32[]{:S(2)}) collective-permute-start(f32[4,32]{1,0:T(4,128)S(1)} %get-tuple-element.30.exposure_ref), channel_id=1, source_target_pairs={{0,1},{1,0},{2,3},{3,2},{4,5},{5,4},{6,7},{7,6},{8,9},{9,8},{10,11... | collective-permute-start | bytes 1544 | tf_op jit(solution)/shard_map/ppermute | solution.py:32

commit v10 on v9

--- a/solution.py
+++ b/solution.py
@@ -211,7 +211,7 @@
     trades = turned.shape[0]
     vmem = pl.BlockSpec(memory_space=pltpu.VMEM)
     return pl.pallas_call(
-        functools.partial(slope_kernel, min(2048, trades)),
+        functools.partial(slope_kernel, min(8192, trades)),
         in_specs=[vmem] * 3,
         out_specs=vmem,
         out_shape=jax.ShapeDtypeStruct((trades, rows), f32),
@@ -229,8 +229,8 @@
     rest = value - high.astype(f32)
     middle = rest.astype(bf16)
     low = (rest - middle.astype(f32)).astype(bf16)
-    dot = functools.partial(jnp.dot, selector, preferred_element_type=f32)
-    return dot(low) + dot(middle) + dot(high)
+    parts = jnp.concatenate([low, middle, high], axis=0)
+    return jnp.dot(jnp.concatenate([selector] * 3, axis=1), parts, preferred_element_type=f32)
 
 
 def net_stage(cpty_dev, dates, me, sums, upstream_ref):
@@ -247,13 +247,10 @@
     tiles = rows // 128
     last = tiles * blocks
     columns = [part[last:, :].T for part in sums]
-    netted = None
-    for k in range(shards):
-        row = label(sums[k][last + dates + 1 : last + dates + 2, :blocks])
-        pick = lax.broadcasted_iota(jnp.int32, (cpties, blocks), 0) == row
-        slabs = [sums[k][q * blocks : (q + 1) * blocks] for q in range(tiles)]
-        part = split_dot(jnp.where(pick, 1.0, 0.0), jnp.concatenate(slabs, axis=1))
-        netted = part if netted is None else netted + part
+    rows_of = [label(part[last + dates + 1 : last + dates + 2, :blocks]) for part in sums]
+    pick = lax.broadcasted_iota(jnp.int32, (cpties, shards * blocks), 0) == jnp.concatenate(rows_of, axis=1)
+    slabs = [jnp.concatenate([part[q * blocks : (q + 1) * blocks] for q in range(tiles)], axis=1) for part in sums]
+    netted = split_dot(jnp.where(pick, 1.0, 0.0), jnp.concatenate(slabs, axis=0))
     column = label(columns[0][:blocks, dates + 1 : dates + 2])
     own = jnp.where(lax.broadcasted_iota(jnp.int32, (blocks, cpties), 1) == column, 1.0, 0.0)
     adjoint, totals = [], []

time: 49.2 us -> 49 us (level)
  Pallas kernels: 16.8 us -> 16 us
  waiting for transfers between devices: 14 us -> 14.7 us
    ppermute x12, waiting for transfers between devices: 14 us -> 14.7 us  [swap(): return lax.ppermute(value, axes, pairs)]
    pallas_call x1, Pallas kernels: 5.25 us -> 4.62 us  [slope_pass(): pl.pallas_call(functools.partial(slope_kernel, min(8192, trades)), in_spe...]
  transfers between devices with their start and end apart: 12 -> 12, of which waited for: 7 -> 7; matrix products, arithmetic and copies ran while one was open for 0% -> 0% of each run, Pallas kernels for 15% -> 13%
where the time goes in v10:
time: 49 us; the launch traced here: 48.8 us
  starting transfers between devices  17.4 us (36%)
  Pallas kernels  16 us (33%)
  waiting for transfers between devices  14.7 us (30%)
  between operations  0.7 us (1%)
    ppermute x12, starting transfers between devices, swap(): return lax.ppermute(value, axes, pairs)  17.4 us
    ppermute x12, waiting for transfers between devices, swap(): return lax.ppermute(value, axes, pairs)  14.7 us
    pallas_call x1, Pallas kernels, value_pass(): pl.pallas_call(functools.partial(value_kernel, min(VALUE_STEP, trades)),...  5.6 us
    pallas_call x1, Pallas kernels, slope_pass(): pl.pallas_call(functools.partial(slope_kernel, min(8192, trades)), in_spe...  4.62 us
    pallas_call x1, Pallas kernels, net_pull_pass(): pl.pallas_call(functools.partial(net_pull_kernel, min(PULL_STEP, trades),...  2.13 us
    pallas_call x1, Pallas kernels, prepare_pass(): pl.pallas_call(functools.partial(prepare_kernel, step), in_specs=[hbm] *...  1.89 us
    pallas_call x1, Pallas kernels, chain_pass(): pl.pallas_call(chain_kernel, in_specs=[pl.BlockSpec(memory_space=pltpu.HB...  0.99 us
  transfers between devices with their start and end apart: 12, of which 7 were waited for; matrix products, arithmetic and copies ran while one was open for 0% of the time, Pallas kernels for 13%

profile of v10, /device:TPU:0, one launch (start us, length us, event | category | flops | bytes accessed | tf_op | source)
XLA Modules:
  0.0 48.8 jit_solution(1178283842071439206)
XLA Ops:
  0.6 1.0 %chain_pass.1 = (f32[128,128]{1,0:T(8,128)S(1)}, f32[4,128,128]{2,1,0:T(8,128)S(1)}, f32[4,128]{1,0:T(4,128)S(1)}) custom-call(f32[4,128,128]{2,1,0:T(8,128)} %x_hbm.1, f32[4,128]{1,0:T(4,128)} %rho_hbm.1), custom_call_target="tpu_custom_call" | custom-call | tf_op jit(solution)/shard_map/chain_pass/pallas_call | solution.py:79
  1.6 3.0 %collective-permute-start = (f32[128,128]{1,0:T(8,128)S(1)}, f32[128,128]{1,0:T(8,128)S(1)}, u32[]{:S(2)}, u32[]{:S(2)}) collective-permute-start(f32[128,128]{1,0:T(8,128)S(1)} %get-tuple-element.19), channel_id=1, source_target_pairs={{0,2},{2,0},{1,3},{3,1},{4,6},{6,4},{5,7},{7,5},{8,10},{10,8},{9,1... | collective-permute-start | bytes 196616 | tf_op jit(solution)/shard_map/ppermute | solution.py:32
  4.6 1.9 %prepare_pass.1 = (bf16[8192,128]{1,0:T(8,128)(2,1)S(1)}, f32[64,128]{1,0:T(8,128)S(1)}, f32[8,128]{1,0:T(8,128)S(1)}) custom-call(bf16[128,8192]{1,0:T(8,128)(2,1)} %d_ref.1, f32[64,128]{1,0:T(8,128)} %bitcast.11, f32[4,32]{1,0:T(4,128)} %mass_hbm.1, f32[1,32]{1,0:T(1,128)} %bitcast.12, s32[1,64]{1,0:T(1,128)} %bitcast.13), custom_call_target="tpu_custom_call" | custom-call | bytes 4194304 | tf_op jit(solution)/shard_map/prepare_pass/pallas_call | solution.py:124
  6.5 0.4 collective-permute-done.arriving_ref
  6.9 5.6 %value_pass.1 = (f32[264,128]{1,0:T(8,128)S(1)}, bf16[128,512]{1,0:T(8,128)(2,1)S(1)}) custom-call(f32[4,128,128]{2,1,0:T(8,128)S(1)} %get-tuple-element.17.x_ref, f32[4,128]{1,0:T(4,128)S(1)} %get-tuple-element.18.rho_ref, f32[128,128]{1,0:T(8,128)S(1)} %collective-permute-done.arriving_ref, s32[1]{0:T(128)} %bitcast.1.keep_ref, ...), custom_call_target="tpu_custom_call" | custom-call | flops 1073741824 | bytes 2097152 | tf_op jit(solution)/shard_map/value_pass/pallas_call | solution.py:176
  12.5 4.2 %collective-permute-start.1 = (f32[264,128]{1,0:T(8,128)S(1)}, f32[264,128]{1,0:T(8,128)S(1)}, u32[]{:S(2)}, u32[]{:S(2)}) collective-permute-start(f32[264,128]{1,0:T(8,128)S(1)} %get-tuple-element.24.refs_0_), channel_id=1, source_target_pairs={{0,12},{4,8},{8,4},{12,0},{1,13},{5,9},{9,5},{13,1},{2,14},{6,10},... | collective-permute-start | bytes 405512 | tf_op jit(solution)/shard_map/ppermute | solution.py:32
  16.7 0.0 collective-permute-start.2
  16.7 0.6 %collective-permute-start.3 = (f32[264,128]{1,0:T(8,128)S(1)}, f32[264,128]{1,0:T(8,128)S(1)}, u32[]{:S(2)}, u32[]{:S(2)}) collective-permute-start(f32[264,128]{1,0:T(8,128)S(1)} %get-tuple-element.24.refs_0_), channel_id=1, source_target_pairs={{0,4},{4,0},{8,12},{12,8},{1,5},{5,1},{9,13},{13,9},{2,6},{6,2},{1... | collective-permute-start | bytes 405512 | tf_op jit(solution)/shard_map/ppermute | solution.py:32
  17.3 4.6 %slope_pass.1.slope_ref = f32[8192,512]{1,0:T(8,128)S(1)} custom-call(bf16[128,512]{1,0:T(8,128)(2,1)S(1)} %get-tuple-element.23.state_ref, bf16[8192,128]{1,0:T(8,128)(2,1)S(1)} %get-tuple-element.21.turned_ref, f32[64,128]{1,0:T(8,128)S(1)} %get-tuple-element.22.n_ref), custom_call_target="tpu_custom_call" | custom-call | flops 1073741824 | bytes 16777216 | tf_op jit(solution)/shard_map/slope_pass/pallas_call | solution.py:213
  22.0 0.0 collective-permute-done.1.refs_1_
  22.0 5.0 %collective-permute-done.2.refs_2_ = f32[264,128]{1,0:T(8,128)S(1)} collective-permute-done((f32[264,128]{1,0:T(8,128)S(1)}, f32[264,128]{1,0:T(8,128)S(1)}, u32[]{:S(2)}, u32[]{:S(2)}) %collective-permute-start.2) | collective-permute-done | bytes 135200 | tf_op jit(solution)/shard_map/ppermute | solution.py:32
  27.0 0.0 collective-permute-done.3.refs_3_
  27.0 0.0 copy-done
  27.0 2.1 %net_pull_pass.1 = (f32[4,32]{1,0:T(4,128)S(1)}, f32[4,32,128]{2,1,0:T(8,128)S(1)}, f32[4,32,128]{2,1,0:T(8,128)S(1)}, f32[4,32,128]{2,1,0:T(8,128)S(1)}, f32[4,32,128]{2,1,0:T(8,128)S(1)}) custom-call(s32[1]{0:T(128)} %bitcast.me_ref, f32[8192,512]{1,0:T(8,128)S(1)} %slope_pass.1.slope_ref, bf16[128,8192]{1,0:T(8,128)(2,1)S(1)} %copy-done, ...), custom_call_target="tpu_custom_call" | custom-call | flops 1073741824 | bytes 16777216 | tf_op jit(solution)/shard_map/net_pull_pass/pallas_call | solution.py:319
  29.1 0.2 collective-permute-start.4
  29.3 2.4 %collective-permute-start.5 = (f32[4,32,128]{2,1,0:T(8,128)S(1)}, f32[4,32,128]{2,1,0:T(8,128)S(1)}, u32[]{:S(2)}, u32[]{:S(2)}) collective-permute-start(f32[4,32,128]{2,1,0:T(8,128)S(1)} %get-tuple-element.27), channel_id=1, source_target_pairs={{0,12},{4,8},{8,4},{12,0},{1,13},{5,9},{9,5},{13,1},{2,14},{6,10},... | collective-permute-start | bytes 196616 | tf_op jit(solution)/shard_map/ppermute | solution.py:32
  31.7 0.9 %collective-permute-start.6 = (f32[4,32,128]{2,1,0:T(8,128)S(1)}, f32[4,32,128]{2,1,0:T(8,128)S(1)}, u32[]{:S(2)}, u32[]{:S(2)}) collective-permute-start(f32[4,32,128]{2,1,0:T(8,128)S(1)} %get-tuple-element.28), channel_id=1, source_target_pairs={{0,4},{4,0},{8,12},{12,8},{1,5},{5,1},{9,13},{13,9},{2,6},{6,2},{1... | collective-permute-start | bytes 196616 | tf_op jit(solution)/shard_map/ppermute | solution.py:32
  32.7 0.0 copy-done.1
  32.7 3.4 %collective-permute-done.4 = f32[4,32,128]{2,1,0:T(8,128)S(1)} collective-permute-done((f32[4,32,128]{2,1,0:T(8,128)S(1)}, f32[4,32,128]{2,1,0:T(8,128)S(1)}, u32[]{:S(2)}, u32[]{:S(2)}) %collective-permute-start.4) | collective-permute-done | bytes 65568 | tf_op jit(solution)/shard_map/ppermute | solution.py:32
  36.0 0.0 collective-permute-done.5
  36.0 0.6 %collective-permute-done.6 = f32[4,32,128]{2,1,0:T(8,128)S(1)} collective-permute-done((f32[4,32,128]{2,1,0:T(8,128)S(1)}, f32[4,32,128]{2,1,0:T(8,128)S(1)}, u32[]{:S(2)}, u32[]{:S(2)}) %collective-permute-start.6) | collective-permute-done | bytes 65568 | tf_op jit(solution)/shard_map/ppermute | solution.py:32
  36.7 1.6 %collective-permute-start.7 = (f32[32,128]{1,0:T(8,128)S(1)}, f32[32,128]{1,0:T(8,128)S(1)}, u32[]{:S(2)}, u32[]{:S(2)}) collective-permute-start(f32[32,128]{1,0:T(8,128)S(1)} %fusion), channel_id=1, source_target_pairs={{0,2},{2,0},{1,3},{3,1},{4,6},{6,4},{5,7},{7,5},{8,10},{10,8},{9,1... | collective-permute-start | bytes 49160 | tf_op jit(solution)/shard_map/ppermute | solution.py:32
  38.3 2.2 %collective-permute-done.7 = f32[32,128]{1,0:T(8,128)S(1)} collective-permute-done((f32[32,128]{1,0:T(8,128)S(1)}, f32[32,128]{1,0:T(8,128)S(1)}, u32[]{:S(2)}, u32[]{:S(2)}) %collective-permute-start.7) | collective-permute-done | bytes 16416 | tf_op jit(solution)/shard_map/ppermute | solution.py:32
  40.5 1.9 %collective-permute-start.8 = (f32[4,32,128]{2,1,0:T(8,128)S(1)}, f32[4,32,128]{2,1,0:T(8,128)S(1)}, u32[]{:S(2)}, u32[]{:S(2)}) collective-permute-start(f32[4,32,128]{2,1,0:T(8,128)S(1)} %multiply_add_fusion.refs_0_), channel_id=1, source_target_pairs={{0,12},{4,8},{8,4},{12,0},{1,13},{5,9},{9,5},{13,1},{2,14},{6,10},... | collective-permute-start | bytes 196616 | tf_op jit(solution)/shard_map/ppermute | solution.py:32
  42.4 0.0 collective-permute-start.10
  42.4 2.6 %collective-permute-start.11 = (f32[4,32,128]{2,1,0:T(8,128)S(1)}, f32[4,32,128]{2,1,0:T(8,128)S(1)}, u32[]{:S(2)}, u32[]{:S(2)}) collective-permute-start(f32[4,32,128]{2,1,0:T(8,128)S(1)} %multiply_add_fusion.refs_0_), channel_id=1, source_target_pairs={{0,8},{4,12},{8,0},{12,4},{1,9},{5,13},{9,1},{13,5},{2,10},{6,14},... | collective-permute-start | bytes 196616 | tf_op jit(solution)/shard_map/ppermute | solution.py:32
  45.0 1.7 %collective-permute-done.8.refs_2_ = f32[4,32,128]{2,1,0:T(8,128)S(1)} collective-permute-done((f32[4,32,128]{2,1,0:T(8,128)S(1)}, f32[4,32,128]{2,1,0:T(8,128)S(1)}, u32[]{:S(2)}, u32[]{:S(2)}) %collective-permute-start.8) | collective-permute-done | bytes 65568 | tf_op jit(solution)/shard_map/ppermute | solution.py:32
  46.7 0.0 collective-permute-start.9
  46.7 1.3 %collective-permute-done.10.refs_1_ = f32[4,32,128]{2,1,0:T(8,128)S(1)} collective-permute-done((f32[4,32,128]{2,1,0:T(8,128)S(1)}, f32[4,32,128]{2,1,0:T(8,128)S(1)}, u32[]{:S(2)}, u32[]{:S(2)}) %collective-permute-start.10) | collective-permute-done | bytes 65568 | tf_op jit(solution)/shard_map/ppermute | solution.py:32
  48.1 0.0 collective-permute-done.11.refs_3_
  48.1 0.0 collective-permute-done.9.other_ref
  48.1 0.7 %place.1 = (f32[4,32]{1,0:T(4,128)}, f32[4,128,128]{2,1,0:T(8,128)}) custom-call(s32[1]{0:T(128)} %bitcast.me_ref, f32[4,32]{1,0:T(4,128)S(1)} %get-tuple-element.30.exposure_ref, f32[4,32]{1,0:T(4,128)S(1)} %collective-permute-done.9.other_ref, f32[4,32,128]{2,1,0:T(8,128)S(1)} %multiply_add_fusion.refs_0_, ...), custom_call_target="tpu_custom_call" | custom-call | tf_op jit(solution)/shard_map/place/pallas_call | solution.py:374
  (8 shorter events, 0.1 us)
Async XLA Ops:
  1.6 5.2 %collective-permute-start = (f32[128,128]{1,0:T(8,128)S(1)}, f32[128,128]{1,0:T(8,128)S(1)}, u32[]{:S(2)}, u32[]{:S(2)}) collective-permute-start(f32[128,128]{1,0:T(8,128)S(1)} %get-tuple-element.19), channel_id=1, source_target_pairs={{0,2},{2,0},{1,3},{3,1},{4,6},{6,4},{5,7},{7,5},{8,10},{10,8},{9,1... | collective-permute-start | bytes 196616 | tf_op jit(solution)/shard_map/ppermute | solution.py:32
  12.5 9.5 %collective-permute-start.1 = (f32[264,128]{1,0:T(8,128)S(1)}, f32[264,128]{1,0:T(8,128)S(1)}, u32[]{:S(2)}, u32[]{:S(2)}) collective-permute-start(f32[264,128]{1,0:T(8,128)S(1)} %get-tuple-element.24.refs_0_), channel_id=1, source_target_pairs={{0,12},{4,8},{8,4},{12,0},{1,13},{5,9},{9,5},{13,1},{2,14},{6,10},... | collective-permute-start | bytes 405512 | tf_op jit(solution)/shard_map/ppermute | solution.py:32
  16.7 10.3 %collective-permute-start.2 = (f32[264,128]{1,0:T(8,128)S(1)}, f32[264,128]{1,0:T(8,128)S(1)}, u32[]{:S(2)}, u32[]{:S(2)}) collective-permute-start(f32[264,128]{1,0:T(8,128)S(1)} %get-tuple-element.24.refs_0_), channel_id=1, source_target_pairs={{0,8},{4,12},{8,0},{12,4},{1,9},{5,13},{9,1},{13,5},{2,10},{6,14},... | collective-permute-start | bytes 405512 | tf_op jit(solution)/shard_map/ppermute | solution.py:32
  16.7 10.3 %collective-permute-start.3 = (f32[264,128]{1,0:T(8,128)S(1)}, f32[264,128]{1,0:T(8,128)S(1)}, u32[]{:S(2)}, u32[]{:S(2)}) collective-permute-start(f32[264,128]{1,0:T(8,128)S(1)} %get-tuple-element.24.refs_0_), channel_id=1, source_target_pairs={{0,4},{4,0},{8,12},{12,8},{1,5},{5,1},{9,13},{13,9},{2,6},{6,2},{1... | collective-permute-start | bytes 405512 | tf_op jit(solution)/shard_map/ppermute | solution.py:32
  17.3 9.6 %copy-start = (bf16[128,8192]{1,0:T(8,128)(2,1)S(1)}, bf16[128,8192]{1,0:T(8,128)(2,1)}, u32[]{:S(2)}) copy-start(bf16[128,8192]{1,0:T(8,128)(2,1)} %d_ref.1) | copy-start | bytes 6291460
  27.0 5.7 %copy-start.1 = (f32[4,128]{1,0:T(4,128)S(1)}, f32[4,128]{1,0:T(4,128)}, u32[]{:S(2)}) copy-start(f32[4,128]{1,0:T(4,128)} %rho_hbm.1) | copy-start | bytes 6148
  29.1 6.9 %collective-permute-start.4 = (f32[4,32,128]{2,1,0:T(8,128)S(1)}, f32[4,32,128]{2,1,0:T(8,128)S(1)}, u32[]{:S(2)}, u32[]{:S(2)}) collective-permute-start(f32[4,32,128]{2,1,0:T(8,128)S(1)} %get-tuple-element.26), channel_id=1, source_target_pairs={{0,8},{4,12},{8,0},{12,4},{1,9},{5,13},{9,1},{13,5},{2,10},{6,14},... | collective-permute-start | bytes 196616 | tf_op jit(solution)/shard_map/ppermute | solution.py:32
  29.3 6.7 %collective-permute-start.5 = (f32[4,32,128]{2,1,0:T(8,128)S(1)}, f32[4,32,128]{2,1,0:T(8,128)S(1)}, u32[]{:S(2)}, u32[]{:S(2)}) collective-permute-start(f32[4,32,128]{2,1,0:T(8,128)S(1)} %get-tuple-element.27), channel_id=1, source_target_pairs={{0,12},{4,8},{8,4},{12,0},{1,13},{5,9},{9,5},{13,1},{2,14},{6,10},... | collective-permute-start | bytes 196616 | tf_op jit(solution)/shard_map/ppermute | solution.py:32
  31.7 5.0 %collective-permute-start.6 = (f32[4,32,128]{2,1,0:T(8,128)S(1)}, f32[4,32,128]{2,1,0:T(8,128)S(1)}, u32[]{:S(2)}, u32[]{:S(2)}) collective-permute-start(f32[4,32,128]{2,1,0:T(8,128)S(1)} %get-tuple-element.28), channel_id=1, source_target_pairs={{0,4},{4,0},{8,12},{12,8},{1,5},{5,1},{9,13},{13,9},{2,6},{6,2},{1... | collective-permute-start | bytes 196616 | tf_op jit(solution)/shard_map/ppermute | solution.py:32
  36.7 3.8 %collective-permute-start.7 = (f32[32,128]{1,0:T(8,128)S(1)}, f32[32,128]{1,0:T(8,128)S(1)}, u32[]{:S(2)}, u32[]{:S(2)}) collective-permute-start(f32[32,128]{1,0:T(8,128)S(1)} %fusion), channel_id=1, source_target_pairs={{0,2},{2,0},{1,3},{3,1},{4,6},{6,4},{5,7},{7,5},{8,10},{10,8},{9,1... | collective-permute-start | bytes 49160 | tf_op jit(solution)/shard_map/ppermute | solution.py:32
  40.5 6.2 %collective-permute-start.8 = (f32[4,32,128]{2,1,0:T(8,128)S(1)}, f32[4,32,128]{2,1,0:T(8,128)S(1)}, u32[]{:S(2)}, u32[]{:S(2)}) collective-permute-start(f32[4,32,128]{2,1,0:T(8,128)S(1)} %multiply_add_fusion.refs_0_), channel_id=1, source_target_pairs={{0,12},{4,8},{8,4},{12,0},{1,13},{5,9},{9,5},{13,1},{2,14},{6,10},... | collective-permute-start | bytes 196616 | tf_op jit(solution)/shard_map/ppermute | solution.py:32
  42.4 5.6 %collective-permute-start.10 = (f32[4,32,128]{2,1,0:T(8,128)S(1)}, f32[4,32,128]{2,1,0:T(8,128)S(1)}, u32[]{:S(2)}, u32[]{:S(2)}) collective-permute-start(f32[4,32,128]{2,1,0:T(8,128)S(1)} %multiply_add_fusion.refs_0_), channel_id=1, source_target_pairs={{0,4},{4,0},{8,12},{12,8},{1,5},{5,1},{9,13},{13,9},{2,6},{6,2},{1... | collective-permute-start | bytes 196616 | tf_op jit(solution)/shard_map/ppermute | solution.py:32
  42.4 5.6 %collective-permute-start.11 = (f32[4,32,128]{2,1,0:T(8,128)S(1)}, f32[4,32,128]{2,1,0:T(8,128)S(1)}, u32[]{:S(2)}, u32[]{:S(2)}) collective-permute-start(f32[4,32,128]{2,1,0:T(8,128)S(1)} %multiply_add_fusion.refs_0_), channel_id=1, source_target_pairs={{0,8},{4,12},{8,0},{12,4},{1,9},{5,13},{9,1},{13,5},{2,10},{6,14},... | collective-permute-start | bytes 196616 | tf_op jit(solution)/shard_map/ppermute | solution.py:32
  46.7 1.3 %collective-permute-start.9 = (f32[4,32]{1,0:T(4,128)S(1)}, f32[4,32]{1,0:T(4,128)S(1)}, u32[]{:S(2)}, u32[]{:S(2)}) collective-permute-start(f32[4,32]{1,0:T(4,128)S(1)} %get-tuple-element.30.exposure_ref), channel_id=1, source_target_pairs={{0,1},{1,0},{2,3},{3,2},{4,5},{5,4},{6,7},{7,6},{8,9},{9,8},{10,11... | collective-permute-start | bytes 1544 | tf_op jit(solution)/shard_map/ppermute | solution.py:32
